TPU v7x, 128 devices: a whole 4x4x4 slice. The times are simulated.
128 devices in a mesh: cells: 32 (over z, x, core), rcpt: 4 (over y).
Axes of the slice: x: 4, y: 4, z: 4, core: 2. Of those that a mesh axis runs over, the one named last changes fastest.
Arguments:
- control: float32 [24, 256], replicated, may hold values from -3 to 3
- background: float32 [24, 524288], P(None, 'cells'), may hold values from 0.3 to 3
- ensemble: bfloat16 [256, 524288], P(None, 'cells'), may hold values from -0.3125 to 0.3125
- footprint: bfloat16 [4, 8192, 128, 128], P('rcpt', 'cells'), may hold values from 0.00023365021 to 0.0234375
- tile_block: int32 [4, 8192], P('rcpt', 'cells'), may hold values from 0 to 127
- tile_row: int32 [4, 8192], P('rcpt', 'cells'), may hold values from 0 to 2047, as said below
- tile_count: int32 [4, 32], P('rcpt', 'cells'), may hold values from 32 to 256, as said below
- hour: int32 [4, 262144], P('rcpt'), may hold values from 0 to 23
- observed: float32 [4, 262144], P('rcpt'), may hold values from -6 to 6
- inv_var: float32 [4, 262144], P('rcpt'), may hold values from 0.5 to 4
Outputs:
- gradients: float32 [2, 24, 256], replicated
- modelled_final: float32 [4, 262144], P('rcpt', 'cells')
Inputs may be any that keep to these rules, and one draw needn't show every extreme that they name: `tile_count`: in every group one device holds exactly 256 live slots. Slots at or past a device's count hold no tile and are ignored. `tile_row`: receptor tiles fall into 32 shares of 64 consecutive tiles. Of the 256 slots of one device (slots c * 256 to (c + 1) * 256 - 1 of a group), exactly 8 name tiles of each share.
All inputs are finite; a program needn't handle non-finite values.
Results may differ from a plain program's by a relative error of at most 0.0059.
Values may be sent and summed in bfloat16 or wider, within the bound.
No kernel may reach another device: no remote copies, remote signals or barrier semaphores. Data moves between devices by JAX's collectives and lax.ppermute only.
A program may use at most 128 MiB of HBM per device.

v0:
```python
import math

import jax
import jax.numpy as jnp
from jax import lax
from jax.sharding import Mesh
from jax.sharding import PartitionSpec as P

CELLS = ("cells_0", "cells_1", "cells_2")
CELLS_RCPT = ("cells_0", "cells_1", "cells_2", "rcpt")


step_size = 0.5
turn_tiles = 64


def split_up(value, dim, count):
    lengths = value.shape
    pieces = value.reshape(*lengths[:dim], count, lengths[dim] // count, *lengths[dim + 1 :])
    return jnp.moveaxis(pieces, dim, 0)


def sent_and_summed(value, axis, dim):
    count = lax.axis_size(axis)
    pieces = lax.all_to_all(split_up(value, dim, count), axis, 0, 0, tiled=True)
    return jnp.sum(pieces, axis=0)


def laid_out(pieces, dim):
    lengths = list(pieces.shape[1:])
    lengths[dim] *= pieces.shape[0]
    return jnp.moveaxis(pieces, 0, dim).reshape(lengths)


def from_everyone(value, axis):
    copies = jnp.broadcast_to(value, (lax.axis_size(axis), *value.shape))
    return lax.all_to_all(copies, axis, split_axis=0, concat_axis=0, tiled=True)


def gather_directly(value, axis, dim):
    return laid_out(from_everyone(value, axis), dim)


def by_axis(value, axes):
    for axis in axes:
        value = lax.psum(value, axis)
    return value


def forward_tiles(tile_data, live_limit, row_index, emission_rows, per_turn):
    capacity = tile_data.shape[0]
    tile_height = tile_data.shape[1]

    def forward_one_turn(turn_idx, contrib_all):
        begin_at = turn_idx * per_turn
        tile_part = lax.dynamic_slice_in_dim(tile_data, begin_at, per_turn, 0)
        picked = jnp.take(emission_rows, row_index(begin_at), axis=0)
        is_live = begin_at + jnp.arange(per_turn, dtype=jnp.int32) < live_limit
        contrib = jnp.einsum("gib,gib->gi", tile_part, picked, preferred_element_type=jnp.float32)
        contrib = contrib * is_live[:, None].astype(jnp.float32)
        return lax.dynamic_update_slice_in_dim(contrib_all, contrib, begin_at, 0)

    turn_count = (live_limit + per_turn - 1) // per_turn
    return lax.fori_loop(
        0, turn_count, forward_one_turn, jnp.zeros((capacity, tile_height), jnp.float32)
    )


def adjoint_tiles(
    tile_data, hour_slots, dep_slots, live_limit, store_adj, initial, hour_count, per_turn
):

    def adjoint_one_turn(turn_idx, total_adj):
        begin_at = turn_idx * per_turn
        tile_part = lax.dynamic_slice_in_dim(tile_data, begin_at, per_turn, 0)
        hour_part = lax.dynamic_slice_in_dim(hour_slots, begin_at, per_turn, 0)
        dep_part = lax.dynamic_slice_in_dim(dep_slots, begin_at, per_turn, 0)
        is_live = begin_at + jnp.arange(per_turn, dtype=jnp.int32) < live_limit
        matches = hour_part[:, None, :] == jnp.arange(hour_count, dtype=jnp.int32)[None, :, None]
        weighted = jnp.where(matches, dep_part[:, None, :], jnp.zeros((), jnp.bfloat16))
        adj_part = jnp.einsum(
            "ghi,gib->hgb", weighted, tile_part, preferred_element_type=jnp.float32
        )
        adj_part = adj_part * is_live[None, :, None].astype(jnp.float32)
        return store_adj(total_adj, begin_at, adj_part)

    turn_count = (live_limit + per_turn - 1) // per_turn
    return lax.fori_loop(0, turn_count, adjoint_one_turn, initial)


def per_device(
    control,
    background,
    ensemble,
    footprint,
    tile_block,
    tile_row,
    tile_count,
    hour,
    observed,
    inv_var,
):
    hour_count = control.shape[0]
    cells_dev = background.shape[1]
    capacity = footprint.shape[1]
    tile_height = footprint.shape[2]
    block_width = footprint.shape[3]
    blocks_dev = cells_dev // block_width
    receptors = hour.shape[1]
    row_tiles = receptors // tile_height
    hour_tab = hour[0].reshape(row_tiles, tile_height)
    own_tiles = footprint[0]
    own_blocks = tile_block[0]
    own_rows = tile_row[0]
    live_count = tile_count[0, 0]
    cell_devices = lax.axis_size(CELLS)
    position = lax.axis_index(CELLS)
    share_size = receptors // cell_devices
    per_turn = math.gcd(capacity, turn_tiles)
    hour_slots = hour_tab[own_rows]

    def share_departure(own_modelled):
        own_observed = lax.dynamic_slice_in_dim(observed[0], position * share_size, share_size)
        own_weight = lax.dynamic_slice_in_dim(inv_var[0], position * share_size, share_size)
        return (own_weight * (own_modelled - own_observed)).astype(jnp.bfloat16)

    def evaluate(control_now):
        ensemble_part = jnp.dot(
            control_now.astype(jnp.bfloat16), ensemble, preferred_element_type=jnp.float32
        )
        emission = (
            (background + ensemble_part)
            .astype(jnp.bfloat16)
            .reshape(hour_count, blocks_dev, block_width)
        )
        emission_rows = emission.reshape(hour_count * blocks_dev, block_width)

        def row_index(begin_at):
            hour_part = lax.dynamic_slice_in_dim(hour_slots, begin_at, per_turn, 0)
            block_part = lax.dynamic_slice_in_dim(own_blocks, begin_at, per_turn, 0)
            return hour_part * blocks_dev + block_part[:, None]

        def store_adj(total_adj, begin_at, adj_part):
            block_part = lax.dynamic_slice_in_dim(own_blocks, begin_at, per_turn, 0)
            return total_adj.at[:, block_part].add(adj_part)

        initial = jnp.zeros((hour_count, blocks_dev, block_width), jnp.float32)
        slot_part = forward_tiles(own_tiles, live_count, row_index, emission_rows, per_turn)
        modelled = (
            jnp.zeros((row_tiles, tile_height), jnp.float32)
            .at[own_rows]
            .add(slot_part)
            .reshape(receptors)
        )
        own_modelled = sent_and_summed(modelled, CELLS, 0)
        departure = gather_directly(share_departure(own_modelled), CELLS, 0)
        work_dep = departure.reshape(row_tiles, tile_height)[own_rows]
        adjoint = adjoint_tiles(
            own_tiles, hour_slots, work_dep, live_count, store_adj, initial, hour_count, per_turn
        )
        rounded = adjoint.reshape(hour_count, cells_dev).astype(jnp.bfloat16)
        local_grad = lax.dot_general(
            rounded, ensemble, (((1,), (1,)), ((), ())), preferred_element_type=jnp.float32
        )
        gradient = control_now + by_axis(local_grad, CELLS_RCPT)
        return (gradient, own_modelled)

    first_grad, unused = evaluate(control)
    second_grad, own_final = evaluate(control - step_size * first_grad)
    return (jnp.stack([first_grad, second_grad]), own_final[None, :])


def solution(mesh):
    torus = Mesh(
        mesh.devices.reshape(4, 4, 2, mesh.shape["rcpt"]), ("cells_0", "cells_1", "cells_2", "rcpt")
    )
    return jax.shard_map(
        per_device,
        mesh=torus,
        in_specs=(
            P(),
            P(None, CELLS),
            P(None, CELLS),
            P("rcpt", CELLS, None, None),
            P("rcpt", CELLS),
            P("rcpt", CELLS),
            P("rcpt", CELLS),
            P("rcpt", None),
            P("rcpt", None),
            P("rcpt", None),
        ),
        out_specs=(P(), P("rcpt", CELLS)),
        check_vma=False,
    )
```

profile of v0, /device:TPU:0, one launch (start us, length us, event | category | flops | bytes accessed | tf_op | source)
XLA Modules:
  0.0 558.4 jit_solution(16430458801044514826)
XLA Ops:
  2.1 5.0 fusion.32
  8.3 34.7 %while.40 = (s32[]{:T(128)}, f32[256,128]{1,0:T(8,128)S(1)}, s32[]{:T(128)}, bf16[256,128,128]{2,1,0:T(8,128)(2,1)}, s32[256,128]{1,0:T(8,128)S(1)}, /*index=5*/...) while((s32[]{:T(128)}, f32[256,128]{1,0:T(8,128)S(1)}, ...), condition=%wide.region_1.3_spmd, body=%wide.region_0.2_spmd.sunk | while | flops 5357766 | bytes 8636351 | solution.py:64
  8.5 29.2 %gather_fusion = bf16[8192,128]{1,0:T(8,128)(2,1)} fusion(bf16[3072,128]{1,0:T(8,128)(2,1)S(1)} %get-tuple-element.477, s32[8192]{0:T(1024)S(1)} %bitcast_clamp_fusion.4), kind=kCustom, calls=%fused_computation.clone.clone.1 | custom fusion | bytes 4227072 | tf_op jit(solution)/shard_map/while/body/jit(_take)/gather | solution.py:57
  37.8 4.4 fusion.59
  45.4 109.7 %all-to-all-start = ((f32[32,1,8192]{2,1,0:T(1,128)}), f32[32,1,8192]{2,1,0:T(1,128)S(1)}, u32[]{:S(2)}, u32[]{:S(2)}) async-start(f32[32,1,8192]{2,1,0:T(1,128)} %bitcast.13), calls=%async_computation | async-start | bytes 2097152 | tf_op jit(solution)/shard_map/all_to_all | solution.py:25
  155.9 16.4 %all-to-all-done = f32[32,1,8192]{2,1,0:T(1,128)S(1)} async-done(((f32[32,1,8192]{2,1,0:T(1,128)}), f32[32,1,8192]{2,1,0:T(1,128)S(1)}, u32[]{:S(2)}, u32[]{:S(2)}) %all-to-all-start) | async-done | bytes 1048608 | tf_op jit(solution)/shard_map/all_to_all | solution.py:25
  174.5 3.7 reduce.8
  179.4 4.1 all-to-all-start.1
  183.5 11.4 %all-to-all-done.1 = bf16[32,2,4096]{2,1,0:T(2,128)(2,1)S(1)} async-done(((bf16[32,2,4096]{2,1,0:T(2,128)(2,1)}), bf16[32,2,4096]{2,1,0:T(2,128)(2,1)S(1)}, u32[]{:S(2)}, u32[]{:S(2)}) %all-to-all-start.1) | async-done | bytes 524320 | tf_op jit(solution)/shard_map/all_to_all | solution.py:37
  195.4 3.2 reduce.4
  200.4 6.8 %while.41 = (s32[]{:T(128)}, f32[24,128,128]{2,0,1:T(8,128)S(1)}, s32[]{:T(128)}, s32[256]{0:T(256)S(1)}, bf16[256,128,128]{2,1,0:T(8,128)(2,1)}, /*index=5*/s32...) while((s32[]{:T(128)}, f32[24,128,128]{2,0,1:T(8,128)S(1)}, ...), condition=%wide.region_6.8_spmd, body=%wide.region_4.7_spmd.sunk | while | flops 51118468 | bytes 5391803 | solution.py:88
  204.1 3.1 scatter_fusion
  207.2 5.7 %fusion.37 = f32[24,256]{1,0:T(8,128)S(1)} fusion(bf16[256,16384]{1,0:T(8,128)(2,1)} %param.22, f32[24,128,128]{2,0,1:T(8,128)S(1)} %get-tuple-element.176), kind=kOutput, calls=%fused_computation.60 | convolution fusion | flops 201719808 | bytes 9986048 | tf_op jit(solution)/shard_map/dot_general | solution.py:162
  212.9 35.6 %psum.56 = f32[24,256]{1,0:T(8,128)S(1)} all-reduce(f32[24,256]{1,0:T(8,128)S(1)} %fusion.37), channel_id=1, replica_groups=mesh['cells_0'=4,'cells_1'=4,'cells_2'=2,'rcpt'=4] {'cells_0'}, use_global_device_ids=true, to_apply=%region_7.9 | all-reduce | flops 6144 | bytes 49152 | tf_op jit(solution)/shard_map/psum | solution.py:46
  248.5 14.4 %psum.57 = f32[24,256]{1,0:T(8,128)S(1)} all-reduce(f32[24,256]{1,0:T(8,128)S(1)} %psum.56), channel_id=1, replica_groups=mesh['cells_0'=4,'cells_1'=4,'cells_2'=2,'rcpt'=4] {'cells_1'}, use_global_device_ids=true, to_apply=%region_8.10 | all-reduce | flops 6144 | bytes 49152 | tf_op jit(solution)/shard_map/psum | solution.py:46
  262.9 3.4 psum.58
  266.3 19.0 %psum.59 = f32[24,256]{1,0:T(8,128)S(1)} all-reduce(f32[24,256]{1,0:T(8,128)S(1)} %psum.58), channel_id=1, replica_groups=mesh['cells_0'=4,'cells_1'=4,'cells_2'=2,'rcpt'=4] {'rcpt'}, use_global_device_ids=true, to_apply=%region_10.12 | all-reduce | flops 6144 | bytes 49152 | tf_op jit(solution)/shard_map/psum | solution.py:46
  285.3 5.0 fusion.33
  290.7 34.7 %while.42 = (s32[]{:T(128)}, f32[256,128]{1,0:T(8,128)S(1)}, s32[]{:T(128)}, bf16[256,128,128]{2,1,0:T(8,128)(2,1)}, s32[256,128]{1,0:T(8,128)S(1)}, /*index=5*/...) while((s32[]{:T(128)}, f32[256,128]{1,0:T(8,128)S(1)}, ...), condition=%wide.region_12.14_spmd, body=%wide.region_11.13_spmd.sunk | while | flops 5357766 | bytes 8636351 | solution.py:64
  290.9 29.2 %gather_fusion.1 = bf16[8192,128]{1,0:T(8,128)(2,1)} fusion(bf16[3072,128]{1,0:T(8,128)(2,1)S(1)} %get-tuple-element.549, s32[8192]{0:T(1024)S(1)} %bitcast_clamp_fusion.5), kind=kCustom, calls=%fused_computation.1.clone.clone.1 | custom fusion | bytes 4227072 | tf_op jit(solution)/shard_map/while/body/jit(_take)/gather | solution.py:57
  320.3 4.4 fusion.63
  327.1 122.4 %all_to_all.30 = f32[32,1,8192]{2,1,0:T(1,128)S(1)} all-to-all(f32[32,1,8192]{2,1,0:T(1,128)S(1)} %bitcast.61), channel_id=1, replica_groups=mesh['cells_0'=4,'cells_1'=4,'cells_2'=2,'rcpt'=4] {'cells_0','cells_1',..., dimensions={0} | all-to-all | bytes 2097152 | tf_op jit(solution)/shard_map/all_to_all | solution.py:25
  451.2 3.7 reduce.9
  456.1 3.9 all-to-all-start.3
  460.0 11.6 %all-to-all-done.3 = bf16[32,2,4096]{2,1,0:T(2,128)(2,1)S(1)} async-done(((bf16[32,2,4096]{2,1,0:T(2,128)(2,1)}), bf16[32,2,4096]{2,1,0:T(2,128)(2,1)S(1)}, u32[]{:S(2)}, u32[]{:S(2)}) %all-to-all-start.3) | async-done | bytes 524320 | tf_op jit(solution)/shard_map/all_to_all | solution.py:37
  472.1 3.2 reduce.5
  477.1 7.1 %while.43 = (s32[]{:T(128)}, f32[24,128,128]{2,0,1:T(8,128)S(1)}, s32[]{:T(128)}, s32[256]{0:T(256)S(1)}, bf16[256,128,128]{2,1,0:T(8,128)(2,1)}, /*index=5*/s32...) while((s32[]{:T(128)}, f32[24,128,128]{2,0,1:T(8,128)S(1)}, ...), condition=%wide.region_17.19_spmd, body=%wide.region_15.18_spmd.sunk | while | flops 51118468 | bytes 5391803 | solution.py:88
  484.2 5.7 %fusion.34 = f32[24,256]{1,0:T(8,128)S(1)} fusion(bf16[256,16384]{1,0:T(8,128)(2,1)} %param.22, f32[24,128,128]{2,0,1:T(8,128)S(1)} %get-tuple-element.178), kind=kOutput, calls=%fused_computation.57 | convolution fusion | flops 201719808 | bytes 9986048 | tf_op jit(solution)/shard_map/dot_general | solution.py:162
  489.9 35.6 %psum.60 = f32[24,256]{1,0:T(8,128)S(1)} all-reduce(f32[24,256]{1,0:T(8,128)S(1)} %fusion.34), channel_id=1, replica_groups=mesh['cells_0'=4,'cells_1'=4,'cells_2'=2,'rcpt'=4] {'cells_0'}, use_global_device_ids=true, to_apply=%region_18.20 | all-reduce | flops 6144 | bytes 49152 | tf_op jit(solution)/shard_map/psum | solution.py:46
  525.5 14.4 %psum.61 = f32[24,256]{1,0:T(8,128)S(1)} all-reduce(f32[24,256]{1,0:T(8,128)S(1)} %psum.60), channel_id=1, replica_groups=mesh['cells_0'=4,'cells_1'=4,'cells_2'=2,'rcpt'=4] {'cells_1'}, use_global_device_ids=true, to_apply=%region_19.21 | all-reduce | flops 6144 | bytes 49152 | tf_op jit(solution)/shard_map/psum | solution.py:46
  539.9 3.4 psum.62
  543.3 14.4 %psum.63 = f32[24,256]{1,0:T(8,128)S(1)} all-reduce(f32[24,256]{1,0:T(8,128)S(1)} %psum.62), channel_id=1, replica_groups=mesh['cells_0'=4,'cells_1'=4,'cells_2'=2,'rcpt'=4] {'rcpt'}, use_global_device_ids=true, to_apply=%region_21.23 | all-reduce | flops 6144 | bytes 49152 | tf_op jit(solution)/shard_map/psum | solution.py:46
  (72 shorter events, 30.9 us)
Async XLA Ops:
  0.6 6.9 %copy-start = (s32[1,262144]{1,0:T(1,128)S(1)}, s32[1,262144]{1,0:T(1,128)}, u32[]{:S(2)}) copy-start(s32[1,262144]{1,0:T(1,128)} %param.27) | copy-start | bytes 3145732
  7.1 1.2 copy-start.10
  45.4 127.0 %all-to-all-start = ((f32[32,1,8192]{2,1,0:T(1,128)}), f32[32,1,8192]{2,1,0:T(1,128)S(1)}, u32[]{:S(2)}, u32[]{:S(2)}) async-start(f32[32,1,8192]{2,1,0:T(1,128)} %bitcast.13), calls=%async_computation | async-start | bytes 2097152 | tf_op jit(solution)/shard_map/all_to_all | solution.py:25
  155.9 18.1 %copy-start.1 = (f32[1,8192]{1,0:T(1,128)}, f32[1,8192]{1,0:T(1,128)S(1)}, u32[]{:S(2)}) copy-start(f32[1,8192]{1,0:T(1,128)S(1)} %get-tuple-element.245) | copy-start | bytes 98308
  155.9 18.1 %copy-start.3 = (f32[1,8192]{1,0:T(1,128)}, f32[1,8192]{1,0:T(1,128)S(1)}, u32[]{:S(2)}) copy-start(f32[1,8192]{1,0:T(1,128)S(1)} %get-tuple-element.246) | copy-start | bytes 98308
  179.4 15.5 %all-to-all-start.1 = ((bf16[32,2,4096]{2,1,0:T(2,128)(2,1)}), bf16[32,2,4096]{2,1,0:T(2,128)(2,1)S(1)}, u32[]{:S(2)}, u32[]{:S(2)}) async-start(bf16[32,2,4096]{2,1,0:T(2,128)(2,1)} %reshape.191), calls=%async_computation.1 | async-start | bytes 1048576 | tf_op jit(solution)/shard_map/all_to_all | solution.py:37
  207.2 78.1 %copy-start.5 = (f32[24,256]{1,0:T(8,128)S(1)}, f32[24,256]{1,0:T(8,128)}, u32[]{:S(2)}) copy-start(f32[24,256]{1,0:T(8,128)} %param.20) | copy-start | bytes 73732
  285.3 5.0 copy-start.7
  325.4 124.8 %copy-start.2 = (f32[1,8192]{1,0:T(1,128)S(1)}, f32[1,8192]{1,0:T(1,128)}, u32[]{:S(2)}) copy-start(f32[1,8192]{1,0:T(1,128)} %copy-done.1) | copy-start | bytes 98308
  325.4 124.8 %copy-start.4 = (f32[1,8192]{1,0:T(1,128)S(1)}, f32[1,8192]{1,0:T(1,128)}, u32[]{:S(2)}) copy-start(f32[1,8192]{1,0:T(1,128)} %copy-done.3) | copy-start | bytes 98308
  450.2 5.9 %copy-start.9 = (f32[8192]{0:T(1024)}, f32[8192]{0:T(1024)S(1)}, u32[]{:S(2)}) copy-start(f32[8192]{0:T(1024)S(1)} %reduce_sum.19) | copy-start | bytes 98308
  456.1 15.5 %all-to-all-start.3 = ((bf16[32,2,4096]{2,1,0:T(2,128)(2,1)}), bf16[32,2,4096]{2,1,0:T(2,128)(2,1)S(1)}, u32[]{:S(2)}, u32[]{:S(2)}) async-start(bf16[32,2,4096]{2,1,0:T(2,128)(2,1)} %reshape.193), calls=%async_computation.3 | async-start | bytes 1048576 | tf_op jit(solution)/shard_map/all_to_all | solution.py:37
  484.2 73.5 %copy-start.6 = (f32[24,256]{1,0:T(8,128)S(1)}, f32[24,256]{1,0:T(8,128)}, u32[]{:S(2)}) copy-start(f32[24,256]{1,0:T(8,128)} %param.20) | copy-start | bytes 73732
  484.2 73.5 %copy-start.8 = (f32[24,256]{1,0:T(8,128)S(1)}, f32[24,256]{1,0:T(8,128)}, u32[]{:S(2)}) copy-start(f32[24,256]{1,0:T(8,128)} %copy-done.7) | copy-start | bytes 73732
where the time goes:
time: 560 us; the launch traced here: 558 us
  blocking collectives  263 us (47%)
  starting transfers between devices  118 us (21%)
  local copies, waits for them, and re-layouts  71.8 us (13%)
  waiting for transfers between devices  39.4 us (7%)
  other arithmetic  38.8 us (7%)
  matrix products  25.9 us (5%)
    psum x8, blocking collectives, by_axis(): value = lax.psum(value, axis)  140 us
    all_to_all x1, blocking collectives, sent_and_summed(): pieces = lax.all_to_all(split_up(value, dim, count), axis, 0, 0, tiled=True)  122 us
    all_to_all x1, starting transfers between devices, sent_and_summed(): pieces = lax.all_to_all(split_up(value, dim, count), axis, 0, 0, tiled=True)  110 us
    gather x2, local copies, waits for them, and re-layouts, forward_one_turn(): picked = jnp.take(emission_rows, row_index(begin_at), axis=0)  58.5 us
    all_to_all x2, waiting for transfers between devices, from_everyone(): return lax.all_to_all(copies, axis, split_axis=0, concat_axis=0, tiled=True)  23 us
    all_to_all x1, waiting for transfers between devices, sent_and_summed(): pieces = lax.all_to_all(split_up(value, dim, count), axis, 0, 0, tiled=True)  16.4 us
    dot_general x2, matrix products, evaluate(): lax.dot_general(rounded, ensemble, (((1,), (1,)), ((), ())), preferred_el...  11.4 us
  transfers between devices with their start and end apart: 3, of which 3 were waited for; matrix products, arithmetic and copies ran while one was open for 0% of the time, Pallas kernels for 0%

commit v1 on v0

v1 whole, which is shorter than its diff:
```python
import jax
import jax.numpy as jnp
from jax import lax
from jax.experimental import pallas as pl
from jax.experimental.pallas import tpu as pltpu
from jax.sharding import Mesh
from jax.sharding import PartitionSpec as P

CELLS = ("cells_0", "cells_1", "cells_2")
PLANE = ("cells_0", "cells_1")
REST = ("cells_2", "rcpt")

step_size = 0.5

ENS_CHUNKS = 8
TILE_CHUNK = 32
UNROLL = 8
F32 = jnp.float32
BF16 = jnp.bfloat16


def from_everyone(value, axis):
    copies = jnp.broadcast_to(value, (lax.axis_size(axis), *value.shape))
    return lax.all_to_all(copies, axis, split_axis=0, concat_axis=0, tiled=True)


def copy_into(source, target, sem):
    return pltpu.make_async_copy(source, target, sem)


def forward_kernel(
    meta, weights, background, ensemble, footprint, hour,
    out, ens_buf, bg_buf, tile_buf, hour_buf, emis, partial, row_ids,
    ens_sem, bg_sem, tile_sem, hour_sem,
):
    slots = tile_buf.shape[0]
    hours = weights.shape[0]
    width = ens_buf.shape[2]
    blocks = width // 128
    live = meta[3 * slots]
    chunks = slots // TILE_CHUNK

    def ens_copy(c):
        return copy_into(ensemble.at[:, pl.ds(c * width, width)], ens_buf.at[c], ens_sem.at[c])

    def bg_copy(c):
        return copy_into(background.at[:, pl.ds(c * width, width)], bg_buf.at[c], bg_sem.at[c])

    def tile_copy(c):
        part = pl.ds(c * TILE_CHUNK, TILE_CHUNK)
        return copy_into(footprint.at[part], tile_buf.at[part], tile_sem.at[c])

    for c in range(ENS_CHUNKS):
        ens_copy(c).start()
        bg_copy(c).start()
    hour_copy = copy_into(hour, hour_buf, hour_sem)
    hour_copy.start()
    for c in range(chunks):
        @pl.when(c * TILE_CHUNK < live)
        def _():
            tile_copy(c).start()

    partial[...] = jnp.zeros_like(partial)
    row_ids[...] = jnp.zeros_like(row_ids)
    scaled = weights[...].astype(BF16)
    for c in range(ENS_CHUNKS):
        ens_copy(c).wait()
        bg_copy(c).wait()
        values = bg_buf[c] + jnp.dot(scaled, ens_buf[c], preferred_element_type=F32)
        values = values.astype(BF16)
        for b in range(blocks):
            emis[c * blocks + b] = values[:, b * 128 : (b + 1) * 128]
    hour_copy.wait()
    hour_line = lax.broadcasted_iota(jnp.int32, (hours, 128), 0)

    for c in range(chunks):
        @pl.when(c * TILE_CHUNK < live)
        def _():
            tile_copy(c).wait()

            def some_slots(g, carry):
                for u in range(UNROLL):
                    s = c * TILE_CHUNK + g * UNROLL + u
                    row = meta[slots + s]
                    place = meta[2 * slots + s]
                    every = lax.dot_general(
                        emis[meta[s]], tile_buf[s], (((1,), (1,)), ((), ())),
                        preferred_element_type=F32,
                    )
                    chosen = (hour_line == hour_buf[pl.ds(row, 1), :]) & (s < live)
                    line = jnp.sum(jnp.where(chosen, every, 0.0), axis=0, keepdims=True)
                    partial[pl.ds(place, 1), :] = line
                    row_ids[pl.ds(place, 1), :] = jnp.full((1, 128), (row % 64).astype(F32))
                return carry

            here = jnp.minimum(live - c * TILE_CHUNK, TILE_CHUNK)
            lax.fori_loop(0, (here + UNROLL - 1) // UNROLL, some_slots, 0)

    both = jnp.concatenate(
        [partial[...].reshape(slots // 8, 8, 128), row_ids[...].reshape(slots // 8, 8, 128)], axis=1
    )
    out[...] = both.astype(BF16)


def departure_kernel(position, received, observed, inv_var, modelled, send):
    tiles = modelled.shape[0]
    senders = received.shape[0]
    both = received[...].astype(F32)
    data = both[:, 0:8, :].reshape(senders * 8, 128).astype(BF16)
    ids = both[:, 8:16, 0:tiles].reshape(senders * 8, tiles)
    lane = lax.broadcasted_iota(jnp.int32, ids.shape, 1).astype(F32)
    pick = jnp.where(ids == lane, 1.0, 0.0).astype(BF16)
    own = lax.dot_general(pick, data, (((0,), (0,)), ((), ())), preferred_element_type=F32)
    modelled[...] = own
    departure = (inv_var[...] * (own - observed[...])).astype(BF16)
    send[...] = jnp.dot(pick, departure, preferred_element_type=F32).astype(BF16)


def adjoint_kernel(
    meta, departures, ensemble, footprint, hour,
    out, ens_buf, tile_buf, hour_buf, dep_buf, adjoint,
    ens_sem, tile_sem, hour_sem,
):
    slots = tile_buf.shape[0]
    hours = out.shape[0]
    width = ens_buf.shape[2]
    blocks = width // 128
    live = meta[3 * slots]
    chunks = slots // TILE_CHUNK

    def ens_copy(c):
        return copy_into(ensemble.at[:, pl.ds(c * width, width)], ens_buf.at[c], ens_sem.at[c])

    def tile_copy(c):
        part = pl.ds(c * TILE_CHUNK, TILE_CHUNK)
        return copy_into(footprint.at[part], tile_buf.at[part], tile_sem.at[c])

    hour_copy = copy_into(hour, hour_buf, hour_sem)
    hour_copy.start()
    for c in range(chunks):
        @pl.when(c * TILE_CHUNK < live)
        def _():
            tile_copy(c).start()
    for c in range(ENS_CHUNKS):
        ens_copy(c).start()

    dep_buf[...] = departures[...].astype(F32)
    adjoint[...] = jnp.zeros_like(adjoint)
    hour_copy.wait()
    hour_line = lax.broadcasted_iota(jnp.int32, (hours, 128), 0)

    for c in range(chunks):
        @pl.when(c * TILE_CHUNK < live)
        def _():
            tile_copy(c).wait()

            def some_slots(g, carry):
                for u in range(UNROLL):
                    s = c * TILE_CHUNK + g * UNROLL + u
                    block = meta[s]
                    chosen = (hour_line == hour_buf[pl.ds(meta[slots + s], 1), :]) & (s < live)
                    weighted = jnp.where(chosen, dep_buf[pl.ds(meta[2 * slots + s], 1), :], 0.0)
                    adjoint[block] += jnp.dot(
                        weighted.astype(BF16), tile_buf[s], preferred_element_type=F32
                    )
                return carry

            here = jnp.minimum(live - c * TILE_CHUNK, TILE_CHUNK)
            lax.fori_loop(0, (here + UNROLL - 1) // UNROLL, some_slots, 0)

    total = jnp.zeros(out.shape, F32)
    for c in range(ENS_CHUNKS):
        ens_copy(c).wait()
        rounded = jnp.concatenate([adjoint[c * blocks + b] for b in range(blocks)], axis=1)
        total = total + lax.dot_general(
            rounded.astype(BF16), ens_buf[c], (((1,), (1,)), ((), ())), preferred_element_type=F32
        )
    out[...] = total


def per_device(
    control, background, ensemble, footprint, tile_block, tile_row, tile_count, hour, observed, inv_var,
):
    hours, members = control.shape
    cells_dev = background.shape[1]
    slots = footprint.shape[1]
    receptors = hour.shape[1]
    row_tiles = receptors // 128
    devices = lax.axis_size(CELLS)
    share_tiles = row_tiles // devices
    width = cells_dev // ENS_CHUNKS
    chunks = slots // TILE_CHUNK

    hour_tab = hour.reshape(row_tiles, 128)
    obs_tab = observed.reshape(row_tiles, 128)
    var_tab = inv_var.reshape(row_tiles, 128)
    tiles = footprint[0]
    rows = tile_row[0]
    owner = rows // share_tiles
    order = jnp.arange(slots, dtype=jnp.int32)
    earlier = (owner[None, :] == owner[:, None]) & (order[None, :] < order[:, None])
    place = owner * (slots // devices) + jnp.sum(earlier.astype(jnp.int32), axis=1)
    meta = jnp.concatenate([tile_block[0], rows, place, tile_count[0]])
    position = lax.axis_index(CELLS).astype(jnp.int32).reshape(1)

    smem = pl.BlockSpec(memory_space=pltpu.SMEM)
    vmem = pl.BlockSpec(memory_space=pltpu.VMEM)
    hbm = pl.BlockSpec(memory_space=pl.ANY)

    forward = pl.pallas_call(
        forward_kernel,
        out_shape=jax.ShapeDtypeStruct((devices, 16, 128), BF16),
        in_specs=[smem, vmem, hbm, hbm, hbm, hbm],
        out_specs=vmem,
        scratch_shapes=[
            pltpu.VMEM((ENS_CHUNKS, members, width), BF16),
            pltpu.VMEM((ENS_CHUNKS, hours, width), F32),
            pltpu.VMEM((slots, 128, 128), BF16),
            pltpu.VMEM((row_tiles, 128), jnp.int32),
            pltpu.VMEM((cells_dev // 128, hours, 128), BF16),
            pltpu.VMEM((slots, 128), F32),
            pltpu.VMEM((slots, 128), F32),
            pltpu.SemaphoreType.DMA((ENS_CHUNKS,)),
            pltpu.SemaphoreType.DMA((ENS_CHUNKS,)),
            pltpu.SemaphoreType.DMA((chunks,)),
            pltpu.SemaphoreType.DMA,
        ],
        name="forward",
    )

    share = pl.BlockSpec((share_tiles, 128), lambda i, p: (p[0], 0))
    depart = pl.pallas_call(
        departure_kernel,
        out_shape=(
            jax.ShapeDtypeStruct((share_tiles, 128), F32),
            jax.ShapeDtypeStruct((slots, 128), BF16),
        ),
        grid_spec=pltpu.PrefetchScalarGridSpec(
            num_scalar_prefetch=1,
            grid=(1,),
            in_specs=[pl.BlockSpec((devices, 16, 128), lambda i, p: (0, 0, 0)), share, share],
            out_specs=[
                pl.BlockSpec((share_tiles, 128), lambda i, p: (0, 0)),
                pl.BlockSpec((slots, 128), lambda i, p: (0, 0)),
            ],
        ),
        name="depart",
    )

    adjoint = pl.pallas_call(
        adjoint_kernel,
        out_shape=jax.ShapeDtypeStruct((hours, members), F32),
        in_specs=[smem, vmem, hbm, hbm, hbm],
        out_specs=vmem,
        scratch_shapes=[
            pltpu.VMEM((ENS_CHUNKS, members, width), BF16),
            pltpu.VMEM((slots, 128, 128), BF16),
            pltpu.VMEM((row_tiles, 128), jnp.int32),
            pltpu.VMEM((slots, 128), F32),
            pltpu.VMEM((cells_dev // 128, hours, 128), F32),
            pltpu.SemaphoreType.DMA((ENS_CHUNKS,)),
            pltpu.SemaphoreType.DMA((chunks,)),
            pltpu.SemaphoreType.DMA,
        ],
        name="adjoint",
    )

    def evaluate(control_now):
        partials = forward(meta, control_now, background, ensemble, tiles, hour_tab)
        received = lax.all_to_all(partials, CELLS, 0, 0, tiled=True)
        modelled, send = depart(position, received, obs_tab, var_tab)
        send = send.reshape(devices, slots // devices, 128)
        back = lax.all_to_all(send, CELLS, 0, 0, tiled=True).reshape(slots, 128)
        local = adjoint(meta, back, ensemble, tiles, hour_tab)
        plane = from_everyone(local.astype(BF16), PLANE)
        partly = jnp.sum(plane.astype(F32), axis=0).astype(BF16)
        rest = from_everyone(partly, REST)
        gradient = control_now + jnp.sum(rest.astype(F32), axis=0)
        return gradient, modelled

    first_grad, unused = evaluate(control)
    second_grad, final = evaluate(control - step_size * first_grad)
    return jnp.stack([first_grad, second_grad]), final.reshape(1, receptors // devices)


def solution(mesh):
    torus = Mesh(
        mesh.devices.reshape(4, 4, 2, mesh.shape["rcpt"]), ("cells_0", "cells_1", "cells_2", "rcpt")
    )
    return jax.shard_map(
        per_device,
        mesh=torus,
        in_specs=(
            P(),
            P(None, CELLS),
            P(None, CELLS),
            P("rcpt", CELLS, None, None),
            P("rcpt", CELLS),
            P("rcpt", CELLS),
            P("rcpt", CELLS),
            P("rcpt", None),
            P("rcpt", None),
            P("rcpt", None),
        ),
        out_specs=(P(), P("rcpt", CELLS)),
        check_vma=False,
    )
```

time: 560 us -> 173 us (0.31)
  blocking collectives: 263 us -> 90.6 us
  starting transfers between devices: 118 us -> 10.4 us
  local copies, waits for them, and re-layouts: 71.8 us -> 0.7 us
  Pallas kernels: 0 us -> 54.1 us
  other arithmetic: 38.8 us -> 6.38 us
  waiting for transfers between devices: 39.4 us -> 7.76 us
  matrix products: 25.9 us -> 0 us
    psum x8 -> x0, blocking collectives: 140 us -> none  [by_axis(): value = lax.psum(value, axis)]
    all_to_all x3 -> x1, starting transfers between devices: 118 us -> 10.4 us  [evaluate(): received = lax.all_to_all(partials, CELLS, 0, 0, tiled=True)]
    gather x5 -> x0, local copies, waits for them, and re-layouts: 62.1 us -> none  [the longest x2 58.5 us: forward_one_turn(): picked = jnp.take(emission_rows, row_index(begin_at), axis=0)]
    pallas_call x0 -> x6, Pallas kernels: none -> 54.1 us  [the longest x2 27.8 us: evaluate(): local = adjoint(meta, back, ensemble, tiles, hour_tab)]
    all_to_all x1 -> x7, blocking collectives: 122 us -> 90.6 us  [the longest x4 51.3 us: from_everyone(): return lax.all_to_all(copies, axis, split_axis=0, concat_axis=0, tiled=True)]
    all_to_all x3 -> x1, waiting for transfers between devices: 39.4 us -> 7.76 us  [evaluate(): received = lax.all_to_all(partials, CELLS, 0, 0, tiled=True)]
    dot_general x6 -> x0, matrix products: 25.9 us -> none  [the longest x2 11.4 us: evaluate(): lax.dot_general(rounded, ensemble, (((1,), (1,)), ((), ())), preferred_el...]
    scatter-add x4 -> x0, other arithmetic: 10.2 us -> none  [the longest x2 6.12 us: store_adj(): return total_adj.at[:, block_part].add(adj_part)]
  transfers between devices with their start and end apart: 3 -> 1, of which waited for: 3 -> 1; matrix products, arithmetic and copies ran while one was open for 0% -> 0% of each run, Pallas kernels for 0% -> 0%
where the time goes in v1:
time: 173 us; the launch traced here: 171 us
  blocking collectives  90.6 us (52%)
  Pallas kernels  54.1 us (31%)
  starting transfers between devices  10.4 us (6%)
  waiting for transfers between devices  7.76 us (4%)
  other arithmetic  6.38 us (4%)
    all_to_all x4, blocking collectives, from_everyone(): return lax.all_to_all(copies, axis, split_axis=0, concat_axis=0, tiled=True)  51.3 us
    pallas_call x2, Pallas kernels, evaluate(): local = adjoint(meta, back, ensemble, tiles, hour_tab)  27.8 us
    all_to_all x2, blocking collectives, evaluate(): back = lax.all_to_all(send, CELLS, 0, 0, tiled=True).reshape(slots, 128)  24 us
    pallas_call x2, Pallas kernels, evaluate(): partials = forward(meta, control_now, background, ensemble, tiles, hour_tab)  22.5 us
    all_to_all x1, blocking collectives, evaluate(): received = lax.all_to_all(partials, CELLS, 0, 0, tiled=True)  15.3 us
    all_to_all x1, starting transfers between devices, evaluate(): received = lax.all_to_all(partials, CELLS, 0, 0, tiled=True)  10.4 us
    all_to_all x1, waiting for transfers between devices, evaluate(): received = lax.all_to_all(partials, CELLS, 0, 0, tiled=True)  7.76 us
    pallas_call x2, Pallas kernels, evaluate(): modelled, send = depart(position, received, obs_tab, var_tab)  3.77 us
  transfers between devices with their start and end apart: 1, of which 1 were waited for; matrix products, arithmetic and copies ran while one was open for 0% of the time, Pallas kernels for 0%

profile of v1, /device:TPU:0, one launch (start us, length us, event | category | flops | bytes accessed | tf_op | source)
XLA Modules:
  0.0 171.4 jit_solution(13014522798433456139)
XLA Ops:
  1.3 0.7 and_select_fusion
  2.0 0.7 and_select_fusion.1
  2.7 0.2 convert_reduce_fusion
  2.8 0.7 multiply_add_fusion
  3.5 1.3 pad_add_fusion.meta
  4.8 11.2 %forward.2 = bf16[32,16,128]{2,1,0:T(8,128)(2,1)} custom-call(s32[769]{0:T(1024)} %pad_add_fusion.meta, f32[24,256]{1,0:T(8,128)} %weights.1, f32[24,16384]{1,0:T(8,128)} %background.3, bf16[256,16384]{1,0:T(8,128)(2,1)} %ensemble.7, bf16[256,128,128]{2,1,0:T(8,128)(2,1)} %bitcast.19, s32[2048,128]{1,0:T(8,128)} %bitcast.23), custom_call_target="tpu_custom_call" | custom-call | tf_op jit(solution)/shard_map/forward/pallas_call | solution.py:269
  16.1 10.4 %all-to-all-start = ((bf16[32,16,128]{2,1,0:T(8,128)(2,1)}), bf16[32,16,128]{2,1,0:T(8,128)(2,1)S(1)}, u32[]{:S(2)}, u32[]{:S(2)}) async-start(bf16[32,16,128]{2,1,0:T(8,128)(2,1)} %forward.2), calls=%async_computation | async-start | bytes 262144 | tf_op jit(solution)/shard_map/all_to_all | solution.py:270
  26.5 7.8 %all-to-all-done.received = bf16[32,16,128]{2,1,0:T(8,128)(2,1)S(1)} async-done(((bf16[32,16,128]{2,1,0:T(8,128)(2,1)}), bf16[32,16,128]{2,1,0:T(8,128)(2,1)S(1)}, u32[]{:S(2)}, u32[]{:S(2)}) %all-to-all-start) | async-done | bytes 131104 | tf_op jit(solution)/shard_map/all_to_all | solution.py:270
  34.2 0.0 copy-start
  34.2 0.6 copy-done
  34.9 1.9 %depart.2 = (f32[64,128]{1,0:T(8,128)}, bf16[256,128]{1,0:T(8,128)(2,1)}) custom-call(s32[1]{0:T(128)} %bitcast.4.position, bf16[32,16,128]{2,1,0:T(8,128)(2,1)} %copy-done, f32[2048,128]{1,0:T(8,128)} %bitcast.27, f32[2048,128]{1,0:T(8,128)} %bitcast.29), custom_call_target="tpu_custom_call" | custom-call | tf_op jit(solution)/shard_map/depart/pallas_call | solution.py:271
  36.8 12.0 %all_to_all.40 = bf16[32,8,128]{2,1,0:T(8,128)(2,1)} all-to-all(bf16[32,8,128]{2,1,0:T(8,128)(2,1)} %bitcast.34), channel_id=1, replica_groups=mesh['cells_0'=4,'cells_1'=4,'cells_2'=2,'rcpt'=4] {'cells_0','cells_1',..., dimensions={0} | all-to-all | bytes 131072 | tf_op jit(solution)/shard_map/all_to_all | solution.py:273
  48.8 0.0 copy-start.2
  48.8 13.9 %adjoint.2 = f32[24,256]{1,0:T(8,128)} custom-call(s32[769]{0:T(1024)} %pad_add_fusion.meta, bf16[256,128]{1,0:T(8,128)(2,1)} %bitcast.32, bf16[256,16384]{1,0:T(8,128)(2,1)} %ensemble.7, bf16[256,128,128]{2,1,0:T(8,128)(2,1)} %bitcast.20, s32[2048,128]{1,0:T(8,128)} %bitcast.24), custom_call_target="tpu_custom_call" | custom-call | tf_op jit(solution)/shard_map/adjoint/pallas_call | solution.py:274
  62.7 0.7 convert_element_type.20
  63.5 10.9 %all_to_all.41 = bf16[16,24,256]{2,1,0:T(8,128)(2,1)S(1)} all-to-all(bf16[16,24,256]{2,1,0:T(8,128)(2,1)S(1)} %broadcast_in_dim.16), channel_id=1, replica_groups=mesh['cells_0'=4,'cells_1'=4,'cells_2'=2,'rcpt'=4] {'cells_0','cells_1'}, dimensions={0} | all-to-all | bytes 393216 | tf_op jit(solution)/shard_map/all_to_all | solution.py:24
  74.5 16.7 %all_to_all.42 = bf16[8,24,256]{2,1,0:T(8,128)(2,1)S(1)} all-to-all(bf16[8,24,256]{2,1,0:T(8,128)(2,1)S(1)} %broadcast_in_dim.17), channel_id=1, replica_groups=mesh['cells_0'=4,'cells_1'=4,'cells_2'=2,'rcpt'=4] {'cells_2','rcpt'}, dimensions={0} | all-to-all | bytes 196608 | tf_op jit(solution)/shard_map/all_to_all | solution.py:24
  91.2 0.0 copy-done.2
  91.2 0.6 add_bitcast_fusion.1
  91.8 11.2 %forward.3 = bf16[32,16,128]{2,1,0:T(8,128)(2,1)} custom-call(s32[769]{0:T(1024)} %pad_add_fusion.meta, f32[24,256]{1,0:T(8,128)} %get-tuple-element.9.weights, f32[24,16384]{1,0:T(8,128)} %background.3, bf16[256,16384]{1,0:T(8,128)(2,1)} %ensemble.7, bf16[256,128,128]{2,1,0:T(8,128)(2,1)} %bitcast.21, s32[2048,128]{1,0:T(8,128)} %bitcast.25), custom_call_target="tpu_custom_call" | custom-call | tf_op jit(solution)/shard_map/forward/pallas_call | solution.py:269
  103.1 15.3 %all_to_all.43.received = bf16[32,16,128]{2,1,0:T(8,128)(2,1)} all-to-all(bf16[32,16,128]{2,1,0:T(8,128)(2,1)} %forward.3), channel_id=1, replica_groups=mesh['cells_0'=4,'cells_1'=4,'cells_2'=2,'rcpt'=4] {'cells_0','cells_1',..., dimensions={0} | all-to-all | bytes 262144 | tf_op jit(solution)/shard_map/all_to_all | solution.py:270
  118.4 1.9 %depart.3 = (f32[64,128]{1,0:T(8,128)}, bf16[256,128]{1,0:T(8,128)(2,1)}) custom-call(s32[1]{0:T(128)} %bitcast.4.position, bf16[32,16,128]{2,1,0:T(8,128)(2,1)} %all_to_all.43.received, f32[2048,128]{1,0:T(8,128)} %bitcast.28, f32[2048,128]{1,0:T(8,128)} %bitcast.30), custom_call_target="tpu_custom_call" | custom-call | tf_op jit(solution)/shard_map/depart/pallas_call | solution.py:271
  120.2 12.0 %all_to_all.44 = bf16[32,8,128]{2,1,0:T(8,128)(2,1)} all-to-all(bf16[32,8,128]{2,1,0:T(8,128)(2,1)} %bitcast.33), channel_id=1, replica_groups=mesh['cells_0'=4,'cells_1'=4,'cells_2'=2,'rcpt'=4] {'cells_0','cells_1',..., dimensions={0} | all-to-all | bytes 131072 | tf_op jit(solution)/shard_map/all_to_all | solution.py:273
  132.2 0.0 copy-start.1
  132.3 13.9 %adjoint.3 = f32[24,256]{1,0:T(8,128)} custom-call(s32[769]{0:T(1024)} %pad_add_fusion.meta, bf16[256,128]{1,0:T(8,128)(2,1)} %bitcast.31, bf16[256,16384]{1,0:T(8,128)(2,1)} %ensemble.7, bf16[256,128,128]{2,1,0:T(8,128)(2,1)} %bitcast.22, s32[2048,128]{1,0:T(8,128)} %bitcast.26), custom_call_target="tpu_custom_call" | custom-call | tf_op jit(solution)/shard_map/adjoint/pallas_call | solution.py:274
  146.2 0.7 convert_element_type.22
  146.9 10.9 %all_to_all.45 = bf16[16,24,256]{2,1,0:T(8,128)(2,1)S(1)} all-to-all(bf16[16,24,256]{2,1,0:T(8,128)(2,1)S(1)} %broadcast_in_dim.18), channel_id=1, replica_groups=mesh['cells_0'=4,'cells_1'=4,'cells_2'=2,'rcpt'=4] {'cells_0','cells_1'}, dimensions={0} | all-to-all | bytes 393216 | tf_op jit(solution)/shard_map/all_to_all | solution.py:24
  157.9 12.8 %all_to_all.46 = bf16[8,24,256]{2,1,0:T(8,128)(2,1)S(1)} all-to-all(bf16[8,24,256]{2,1,0:T(8,128)(2,1)S(1)} %broadcast_in_dim.19), channel_id=1, replica_groups=mesh['cells_0'=4,'cells_1'=4,'cells_2'=2,'rcpt'=4] {'cells_2','rcpt'}, dimensions={0} | all-to-all | bytes 196608 | tf_op jit(solution)/shard_map/all_to_all | solution.py:24
  170.7 0.0 copy-done.1
  170.7 0.6 pad_maximum_fusion
  (9 shorter events, 0.2 us)
Async XLA Ops:
  16.1 18.2 %all-to-all-start = ((bf16[32,16,128]{2,1,0:T(8,128)(2,1)}), bf16[32,16,128]{2,1,0:T(8,128)(2,1)S(1)}, u32[]{:S(2)}, u32[]{:S(2)}) async-start(bf16[32,16,128]{2,1,0:T(8,128)(2,1)} %forward.2), calls=%async_computation | async-start | bytes 262144 | tf_op jit(solution)/shard_map/all_to_all | solution.py:270
  34.2 0.6 copy-start
  48.8 42.4 %copy-start.2 = (f32[24,256]{1,0:T(8,128)S(1)}, f32[24,256]{1,0:T(8,128)}, u32[]{:S(2)}) copy-start(f32[24,256]{1,0:T(8,128)} %weights.1) | copy-start | bytes 73732
  132.2 38.5 %copy-start.1 = (f32[24,256]{1,0:T(8,128)S(1)}, f32[24,256]{1,0:T(8,128)}, u32[]{:S(2)}) copy-start(f32[24,256]{1,0:T(8,128)} %get-tuple-element.9.weights) | copy-start | bytes 73732

commit v2 on v1

v2 whole, which is shorter than its diff:
```python
import jax
import jax.numpy as jnp
from jax import lax
from jax.experimental import pallas as pl
from jax.experimental.pallas import tpu as pltpu
from jax.sharding import Mesh
from jax.sharding import PartitionSpec as P

CELLS = ("cells_0", "cells_1", "cells_2")
PLANE = ("cells_0", "cells_1")
REST = ("cells_2", "rcpt")

step_size = 0.5

ENS_CHUNKS = 8
TILE_CHUNK = 32
UNROLL = 8
F32 = jnp.float32
BF16 = jnp.bfloat16
I32 = jnp.int32


def slot_places(rows, share_tiles, per_share):
    slots = rows.shape[1]
    owner = jnp.broadcast_to(rows // share_tiles, (slots, slots))
    down = lax.broadcasted_iota(I32, (slots, slots), 0)
    across = lax.broadcasted_iota(I32, (slots, slots), 1)
    column = jnp.sum(jnp.where(down == across, owner, 0), axis=1, keepdims=True)
    earlier = (owner == column) & (down < across)
    rank = jnp.sum(earlier.astype(I32), axis=0, keepdims=True)
    return (rows // share_tiles) * per_share + rank


def emissions(scaled, background, ensemble, emis, c):
    blocks = ensemble.shape[2] // 128
    values = background[c] + jnp.dot(scaled, ensemble[c], preferred_element_type=F32)
    values = values.astype(BF16).astype(F32)
    for b in range(blocks):
        emis[c * blocks + b] = values[:, b * 128 : (b + 1) * 128]


def live_groups(live, work):
    lax.fori_loop(0, (live + UNROLL - 1) // UNROLL, lambda g, carry: (work(g), carry)[1], 0)


def forward_group(g, live, block, place, tiles, hour_rows, emis, partial):
    hours = emis.shape[1]
    hour_line = lax.broadcasted_iota(I32, (hours, 128), 0)
    none = jnp.zeros((hours, 128), F32)
    base = pl.multiple_of(g * UNROLL, UNROLL)
    these = hour_rows[pl.ds(base, UNROLL), :]
    for u in range(0, UNROLL, 2):
        s = base + u
        left = jnp.concatenate([emis[block[0, s]], none], axis=1)
        right = jnp.concatenate([none, emis[block[0, s + 1]]], axis=1)
        pair = jnp.concatenate([left, right], axis=0).astype(BF16)
        both = jnp.concatenate([tiles[s], tiles[s + 1]], axis=1)
        every = lax.dot_general(pair, both, (((1,), (1,)), ((), ())), preferred_element_type=F32)
        for v in range(2):
            chosen = (hour_line == these[u + v : u + v + 1, :]) & (s + v < live)
            part = jnp.where(chosen, every[v * hours : (v + 1) * hours], 0.0)
            partial[pl.ds(place[0, s + v], 1), :] = jnp.sum(part, axis=0, keepdims=True)


def first_forward_kernel(
    position, block, row, count, row_line, control, background, ensemble, footprint, hour,
    out, place_out, hour_rows, bg_buf, ens_buf, tile_buf,
    place, hour_buf, emis, partial, row_ids, ens_sem, bg_sem, tile_sem, hour_sem, place_sem,
):
    slots = tile_buf.shape[0]
    width = ens_buf.shape[2]
    senders = out.shape[0]
    share_tiles = hour_buf.shape[0] // senders
    live = count[0, 0]
    chunks = slots // TILE_CHUNK

    def ens_copy(c):
        return pltpu.make_async_copy(
            ensemble.at[:, pl.ds(c * width, width)], ens_buf.at[c], ens_sem.at[c]
        )

    def bg_copy(c):
        return pltpu.make_async_copy(
            background.at[:, pl.ds(c * width, width)], bg_buf.at[c], bg_sem.at[c]
        )

    def tile_copy(c):
        part = pl.ds(c * TILE_CHUNK, TILE_CHUNK)
        return pltpu.make_async_copy(footprint.at[part], tile_buf.at[part], tile_sem.at[c])

    for c in range(ENS_CHUNKS):
        ens_copy(c).start()
        bg_copy(c).start()
    hour_copy = pltpu.make_async_copy(hour, hour_buf, hour_sem)
    hour_copy.start()
    for c in range(chunks):
        @pl.when(c * TILE_CHUNK < live)
        def _():
            tile_copy(c).start()

    place_out[...] = slot_places(row_line[...], share_tiles, slots // senders)
    place_copy = pltpu.make_async_copy(place_out, place, place_sem)
    place_copy.start()
    partial[...] = jnp.zeros_like(partial)
    row_ids[...] = jnp.zeros_like(row_ids)

    scaled = control[...].astype(BF16)
    for c in range(ENS_CHUNKS):
        ens_copy(c).wait()
        bg_copy(c).wait()
        emissions(scaled, bg_buf, ens_buf, emis, c)
    place_copy.wait()
    hour_copy.wait()
    for c in range(chunks):
        @pl.when(c * TILE_CHUNK < live)
        def _():
            tile_copy(c).wait()

    def work(g):
        for u in range(UNROLL):
            s = g * UNROLL + u
            here = row[0, s]
            hour_rows[pl.ds(s, 1), :] = hour_buf[pl.ds(here, 1), :]
            number = (here & (share_tiles - 1)).astype(F32)
            row_ids[pl.ds(place[0, s], 1), :] = jnp.full((1, 128), number)
        forward_group(g, live, block, place, tile_buf, hour_rows, emis, partial)

    live_groups(live, work)
    data = partial[...].reshape(senders, slots // senders, 128)
    ids = row_ids[...].reshape(senders, slots // senders, 128)
    out[...] = jnp.concatenate([data, ids], axis=1).astype(BF16)


def next_forward_kernel(
    block, place, count, control, copies, hour_rows, bg_buf, ens_buf, tile_buf,
    out, gradient, emis, partial,
):
    live = count[0, 0]
    slots = tile_buf.shape[0]
    senders = out.shape[0]
    total = control[...] + jnp.sum(copies[...].astype(F32), axis=0)
    gradient[...] = total
    scaled = (control[...] - step_size * total).astype(BF16)
    partial[...] = jnp.zeros_like(partial)
    for c in range(ENS_CHUNKS):
        emissions(scaled, bg_buf, ens_buf, emis, c)
    live_groups(
        live, lambda g: forward_group(g, live, block, place, tile_buf, hour_rows, emis, partial)
    )
    data = partial[...].reshape(senders, slots // senders, 128)
    rounded = data.astype(BF16).astype(F32)
    out[...] = jnp.concatenate([rounded, data - rounded], axis=1).astype(BF16)


def owner_pick(received, tiles):
    ids = received[...].astype(F32)[:, 8:16, 0:tiles].reshape(received.shape[0] * 8, tiles)
    lane = lax.broadcasted_iota(I32, ids.shape, 1).astype(F32)
    return jnp.where(ids == lane, 1.0, 0.0).astype(BF16)


def picked_sum(pick, part):
    part = part.reshape(pick.shape[0], 128).astype(BF16)
    return lax.dot_general(pick, part, (((0,), (0,)), ((), ())), preferred_element_type=F32)


def first_departure_kernel(position, received, observed, inv_var, send):
    pick = owner_pick(received, observed.shape[0])
    own = picked_sum(pick, received[...].astype(F32)[:, 0:8, :])
    departure = (inv_var[...] * (own - observed[...])).astype(BF16)
    send[...] = jnp.dot(pick, departure, preferred_element_type=F32).astype(BF16)


def next_departure_kernel(position, named, received, observed, inv_var, modelled, send):
    pick = owner_pick(named, observed.shape[0])
    both = received[...].astype(F32)
    own = picked_sum(pick, both[:, 0:8, :]) + picked_sum(pick, both[:, 8:16, :])
    modelled[...] = own
    departure = (inv_var[...] * (own - observed[...])).astype(BF16)
    send[...] = jnp.dot(pick, departure, preferred_element_type=F32).astype(BF16)


def adjoint_kernel(
    block, place, count, departures, hour_rows, ens_buf, tile_buf, out, dep_buf, adjoint
):
    hours = out.shape[1]
    blocks = ens_buf.shape[2] // 128
    live = count[0, 0]
    hour_line = lax.broadcasted_iota(I32, (hours, 128), 0)
    dep_buf[...] = departures[...].astype(F32)
    adjoint[...] = jnp.zeros_like(adjoint)

    def work(g):
        base = pl.multiple_of(g * UNROLL, UNROLL)
        these = hour_rows[pl.ds(base, UNROLL), :]
        for u in range(0, UNROLL, 2):
            s = base + u
            weighted = []
            for v in range(2):
                chosen = (hour_line == these[u + v : u + v + 1, :]) & (s + v < live)
                weighted.append(jnp.where(chosen, dep_buf[pl.ds(place[0, s + v], 1), :], 0.0))
            pair = jnp.concatenate(weighted, axis=0).astype(BF16)
            both = jnp.concatenate([tile_buf[s], tile_buf[s + 1]], axis=1)
            every = jnp.dot(pair, both, preferred_element_type=F32)
            adjoint[block[0, s]] += every[0:hours, 0:128]
            adjoint[block[0, s + 1]] += every[hours : 2 * hours, 128:256]

    live_groups(live, work)
    total = jnp.zeros(out.shape[1:], F32)
    for c in range(ENS_CHUNKS):
        rounded = jnp.concatenate([adjoint[c * blocks + b] for b in range(blocks)], axis=1)
        total = total + lax.dot_general(
            rounded.astype(BF16), ens_buf[c], (((1,), (1,)), ((), ())), preferred_element_type=F32
        )
    total = total.astype(BF16)
    for j in range(out.shape[0]):
        out[j] = total


def exchange(value, axes):
    return lax.all_to_all(value, axes, 0, 0, tiled=True)


def per_device(
    control, background, ensemble, footprint, tile_block, tile_row, tile_count, hour, observed, inv_var,
):
    hours, members = control.shape
    cells_dev = background.shape[1]
    slots = footprint.shape[1]
    receptors = hour.shape[1]
    row_tiles = receptors // 128
    devices = lax.axis_size(CELLS)
    plane = lax.axis_size(PLANE)
    rest = lax.axis_size(REST)
    share_tiles = row_tiles // devices
    width = cells_dev // ENS_CHUNKS
    chunks = slots // TILE_CHUNK

    hour_tab = hour.reshape(row_tiles, 128)
    obs_tab = observed.reshape(row_tiles, 128)
    var_tab = inv_var.reshape(row_tiles, 128)
    position = lax.axis_index(CELLS).astype(I32).reshape(1)

    smem = pl.BlockSpec(memory_space=pltpu.SMEM)
    vmem = pl.BlockSpec(memory_space=pltpu.VMEM)
    hbm = pl.BlockSpec(memory_space=pl.ANY)
    limit = pltpu.CompilerParams(vmem_limit_bytes=24 * 1024 * 1024)
    emis = pltpu.VMEM((cells_dev // 128, hours, 128), F32)
    slot_lines = pltpu.VMEM((slots, 128), F32)

    first_forward = pl.pallas_call(
        first_forward_kernel,
        out_shape=(
            pltpu.VMEM((devices, 16, 128), BF16),
            pltpu.VMEM((1, slots), I32),
            pltpu.VMEM((slots, 128), I32),
            pltpu.VMEM((ENS_CHUNKS, hours, width), F32),
            pltpu.VMEM((ENS_CHUNKS, members, width), BF16),
            pltpu.VMEM((slots, 128, 128), BF16),
        ),
        in_specs=[smem, smem, smem, smem, vmem, vmem, hbm, hbm, hbm, hbm],
        out_specs=(vmem,) * 6,
        scratch_shapes=[
            pltpu.SMEM((1, slots), I32),
            pltpu.VMEM((row_tiles, 128), I32),
            emis,
            slot_lines,
            slot_lines,
            pltpu.SemaphoreType.DMA((ENS_CHUNKS,)),
            pltpu.SemaphoreType.DMA((ENS_CHUNKS,)),
            pltpu.SemaphoreType.DMA((chunks,)),
            pltpu.SemaphoreType.DMA,
            pltpu.SemaphoreType.DMA,
        ],
        compiler_params=limit,
        name="first_forward",
    )
    next_forward = pl.pallas_call(
        next_forward_kernel,
        out_shape=(
            pltpu.VMEM((devices, 16, 128), BF16),
            jax.ShapeDtypeStruct((hours, members), F32),
        ),
        in_specs=[smem, smem, smem] + [vmem] * 6,
        out_specs=(vmem, vmem),
        scratch_shapes=[emis, slot_lines],
        compiler_params=limit,
        name="next_forward",
    )

    share = pl.BlockSpec((share_tiles, 128), lambda i, p: (p[0], 0))
    sent = pltpu.VMEM((slots, 128), BF16)
    own = jax.ShapeDtypeStruct((share_tiles, 128), F32)

    def depart(kernel, arrays, out_shape, name):
        return pl.pallas_call(
            kernel,
            out_shape=out_shape,
            grid_spec=pltpu.PrefetchScalarGridSpec(
                num_scalar_prefetch=1,
                grid=(1,),
                in_specs=[vmem] * arrays + [share, share],
                out_specs=[vmem] * len(out_shape),
            ),
            compiler_params=pltpu.CompilerParams(vmem_limit_bytes=4 * 1024 * 1024),
            name=name,
        )

    adjoint = pl.pallas_call(
        adjoint_kernel,
        out_shape=pltpu.VMEM((rest, hours, members), BF16),
        in_specs=[smem, smem, smem] + [vmem] * 4,
        out_specs=vmem,
        scratch_shapes=[slot_lines, emis],
        compiler_params=limit,
        name="adjoint",
    )

    def summed(send, place, hour_rows, ens_buf, tile_buf):
        back = exchange(send.reshape(devices, slots // devices, 128), CELLS).reshape(slots, 128)
        copies = adjoint(tile_block, place, tile_count, back, hour_rows, ens_buf, tile_buf)
        partly = jnp.sum(exchange(copies, REST).astype(F32), axis=0)
        partly = lax.optimization_barrier(partly).astype(BF16)
        return exchange(jnp.broadcast_to(partly, (plane, hours, members)), PLANE)

    large = [
        pltpu.with_memory_space_constraint(array, pltpu.HBM)
        for array in (background, ensemble, footprint[0], hour_tab)
    ]
    partials, place, hour_rows, bg_buf, ens_buf, tile_buf = first_forward(
        position, tile_block, tile_row, tile_count, tile_row, control, *large
    )
    named = exchange(partials, CELLS)
    (send,) = depart(first_departure_kernel, 1, (sent,), "first_departure")(
        position, named, obs_tab, var_tab
    )
    copies = summed(send, place, hour_rows, ens_buf, tile_buf)
    partials, first_grad = next_forward(
        tile_block, place, tile_count, control, copies, hour_rows, bg_buf, ens_buf, tile_buf
    )
    received = exchange(partials, CELLS)
    final, send = depart(next_departure_kernel, 2, (own, sent), "next_departure")(
        position, named, received, obs_tab, var_tab
    )
    copies = summed(send, place, hour_rows, ens_buf, tile_buf)
    updated = control - step_size * first_grad
    second_grad = updated + jnp.sum(copies.astype(F32), axis=0)
    return jnp.stack([first_grad, second_grad]), final.reshape(1, receptors // devices)


def solution(mesh):
    torus = Mesh(
        mesh.devices.reshape(4, 4, 2, mesh.shape["rcpt"]), ("cells_0", "cells_1", "cells_2", "rcpt")
    )
    return jax.shard_map(
        per_device,
        mesh=torus,
        in_specs=(
            P(),
            P(None, CELLS),
            P(None, CELLS),
            P("rcpt", CELLS, None, None),
            P("rcpt", CELLS),
            P("rcpt", CELLS),
            P("rcpt", CELLS),
            P("rcpt", None),
            P("rcpt", None),
            P("rcpt", None),
        ),
        out_specs=(P(), P("rcpt", CELLS)),
        check_vma=False,
    )
```

time: 173 us -> 131 us (0.76); the launches traced: 171 us -> 131 us
  Pallas kernels: 54.1 us -> 19.4 us
  blocking collectives: 90.6 us -> 108 us
  starting transfers between devices: 10.4 us -> 0 us
  waiting for transfers between devices: 7.76 us -> 0 us
  other arithmetic: 6.38 us -> 0.7 us
    pallas_call x6, Pallas kernels: 54.1 us -> 19.4 us  [the longest x2 8.32 us: summed(): adjoint(tile_block, place, tile_count, back, hour_rows, ens_buf, tile_buf)]
    all_to_all x7 -> x8, blocking collectives: 90.6 us -> 108 us  [exchange(): return lax.all_to_all(value, axes, 0, 0, tiled=True)]
    all_to_all x1 -> x0, starting transfers between devices: 10.4 us -> none  [evaluate(): received = lax.all_to_all(partials, CELLS, 0, 0, tiled=True)]
    all_to_all x1 -> x0, waiting for transfers between devices: 7.76 us -> none  [evaluate(): received = lax.all_to_all(partials, CELLS, 0, 0, tiled=True)]
  transfers between devices with their start and end apart: 1 -> 0, of which waited for: 1 -> 0; matrix products, arithmetic and copies ran while one was open for 0% -> 0% of each run, Pallas kernels for 0% -> 0%
where the time goes in v2:
time: 131 us
  blocking collectives  108 us (82%)
  Pallas kernels  19.4 us (15%)
  local copies, waits for them, and re-layouts  2.13 us (2%)
  between operations  1.37 us (1%)
    all_to_all x8, blocking collectives, exchange(): return lax.all_to_all(value, axes, 0, 0, tiled=True)  108 us
    pallas_call x2, Pallas kernels, summed(): adjoint(tile_block, place, tile_count, back, hour_rows, ens_buf, tile_buf)  8.32 us
    pallas_call x1, Pallas kernels, per_device(): first_forward(position, tile_block, tile_row, tile_count, tile_row, contr...  6.74 us
    pallas_call x1, Pallas kernels, per_device(): next_forward(tile_block, place, tile_count, control, copies, hour_rows, b...  3.2 us

profile of v2, /device:TPU:0, one launch (start us, length us, event | category | flops | bytes accessed | tf_op | source)
XLA Modules:
  0.0 131.2 jit_solution(12863317768898128548)
XLA Ops:
  1.3 0.0 copy-start.2
  1.3 0.7 copy-done.2
  2.0 0.0 copy-start.4
  2.0 0.7 copy-done.4
  2.7 0.0 copy-start.6
  2.7 0.7 copy-done.6
  3.4 0.0 copy-start
  3.4 0.0 copy-start.1
  3.4 0.0 copy-start.5
  3.4 6.7 %first_forward.1 = (bf16[32,16,128]{2,1,0:T(8,128)(2,1)S(1)}, s32[1,256]{1,0:T(1,128)S(1)}, s32[256,128]{1,0:T(8,128)S(1)}, f32[8,24,2048]{2,1,0:T(8,128)S(1)}, ...) custom-call(s32[1]{0:T(128)} %bitcast.position, s32[1,256]{1,0:T(1,128)S(1)} %copy-done.4, ...), custom_call_target="tpu_custom_call" | custom-call | tf_op jit(solution)/shard_map/first_forward/pallas_call | solution.py:329
  10.1 20.7 %all_to_all.40.received.named = bf16[32,16,128]{2,1,0:T(8,128)(2,1)S(1)} all-to-all(bf16[32,16,128]{2,1,0:T(8,128)(2,1)S(1)} %get-tuple-element.13), channel_id=1, replica_groups=mesh['cells_0'=4,'cells_1'=4,'cells_2'=2,'rcpt'=4] {'cells_0','cells_1',..., dimensions={0} | all-to-all | bytes 262144 | tf_op jit(solution)/shard_map/all_to_all | solution.py:220
  30.9 0.0 copy-done
  30.9 0.0 copy-done.1
  30.9 0.3 first_departure.1
  31.2 11.0 %all_to_all.41 = bf16[32,8,128]{2,1,0:T(8,128)(2,1)S(1)} all-to-all(bf16[32,8,128]{2,1,0:T(8,128)(2,1)S(1)} %bitcast.19), channel_id=1, replica_groups=mesh['cells_0'=4,'cells_1'=4,'cells_2'=2,'rcpt'=4] {'cells_0','cells_1',..., dimensions={0} | all-to-all | bytes 131072 | tf_op jit(solution)/shard_map/all_to_all | solution.py:220
  42.2 0.0 copy-done.5
  42.2 0.0 copy-start.3
  42.2 4.2 %adjoint.2 = bf16[8,24,256]{2,1,0:T(8,128)(2,1)S(1)} custom-call(s32[1,256]{1,0:T(1,128)S(1)} %copy-done.5, s32[1,256]{1,0:T(1,128)S(1)} %get-tuple-element.12.place, s32[1,1]{1,0:T(1,128)S(6)} %copy.12.count, bf16[256,128]{1,0:T(8,128)(2,1)S(1)} %bitcast.18, s32[256,128]{1,0:T(8,128)S(1)} %get-tuple-element.14.hour_rows, ...), custom_call_target="tpu_custom_call" | custom-call | tf_op jit(solution)/shard_map/adjoint/pallas_call | solution.py:320
  46.4 11.4 %all_to_all.42 = bf16[8,24,256]{2,1,0:T(8,128)(2,1)S(1)} all-to-all(bf16[8,24,256]{2,1,0:T(8,128)(2,1)S(1)} %adjoint.2), channel_id=1, replica_groups=mesh['cells_0'=4,'cells_1'=4,'cells_2'=2,'rcpt'=4] {'cells_2','rcpt'}, dimensions={0} | all-to-all | bytes 196608 | tf_op jit(solution)/shard_map/all_to_all | solution.py:220
  57.8 13.9 %all_to_all.43.copies = bf16[16,24,256]{2,1,0:T(8,128)(2,1)S(1)} all-to-all(bf16[16,24,256]{2,1,0:T(8,128)(2,1)S(1)} %broadcast_in_dim.6), channel_id=1, replica_groups=mesh['cells_0'=4,'cells_1'=4,'cells_2'=2,'rcpt'=4] {'cells_0','cells_1'}, dimensions={0} | all-to-all | bytes 393216 | tf_op jit(solution)/shard_map/all_to_all | solution.py:220
  71.7 0.0 copy-done.3
  71.7 3.2 %next_forward.1 = (bf16[32,16,128]{2,1,0:T(8,128)(2,1)S(1)}, f32[24,256]{1,0:T(8,128)S(1)}) custom-call(s32[1,256]{1,0:T(1,128)S(1)} %copy-done.5, s32[1,256]{1,0:T(1,128)S(1)} %get-tuple-element.12.place, s32[1,1]{1,0:T(1,128)S(6)} %copy.12.count, f32[24,256]{1,0:T(8,128)S(1)} %copy-done.3, bf16[16,24,256]{2,1,0:T(8,128)(2,1)S(1)} %all_to_all.43.copies, ...), custom_call_target="tpu_custom_call" | custom-call | tf_op jit(solution)/shard_map/next_forward/pallas_call | solution.py:337
  74.9 16.1 %all_to_all.44.received = bf16[32,16,128]{2,1,0:T(8,128)(2,1)S(1)} all-to-all(bf16[32,16,128]{2,1,0:T(8,128)(2,1)S(1)} %get-tuple-element.19), channel_id=1, replica_groups=mesh['cells_0'=4,'cells_1'=4,'cells_2'=2,'rcpt'=4] {'cells_0','cells_1',..., dimensions={0} | all-to-all | bytes 262144 | tf_op jit(solution)/shard_map/all_to_all | solution.py:220
  91.0 0.8 next_departure.1
  91.9 10.9 %all_to_all.45 = bf16[32,8,128]{2,1,0:T(8,128)(2,1)S(1)} all-to-all(bf16[32,8,128]{2,1,0:T(8,128)(2,1)S(1)} %bitcast.21), channel_id=1, replica_groups=mesh['cells_0'=4,'cells_1'=4,'cells_2'=2,'rcpt'=4] {'cells_0','cells_1',..., dimensions={0} | all-to-all | bytes 131072 | tf_op jit(solution)/shard_map/all_to_all | solution.py:220
  102.8 4.2 %adjoint.3 = bf16[8,24,256]{2,1,0:T(8,128)(2,1)S(1)} custom-call(s32[1,256]{1,0:T(1,128)S(1)} %copy-done.5, s32[1,256]{1,0:T(1,128)S(1)} %get-tuple-element.12.place, s32[1,1]{1,0:T(1,128)S(6)} %copy.12.count, bf16[256,128]{1,0:T(8,128)(2,1)S(1)} %bitcast.17, s32[256,128]{1,0:T(8,128)S(1)} %get-tuple-element.14.hour_rows, ...), custom_call_target="tpu_custom_call" | custom-call | tf_op jit(solution)/shard_map/adjoint/pallas_call | solution.py:320
  107.0 8.7 %all_to_all.46 = bf16[8,24,256]{2,1,0:T(8,128)(2,1)S(1)} all-to-all(bf16[8,24,256]{2,1,0:T(8,128)(2,1)S(1)} %adjoint.3), channel_id=1, replica_groups=mesh['cells_0'=4,'cells_1'=4,'cells_2'=2,'rcpt'=4] {'cells_2','rcpt'}, dimensions={0} | all-to-all | bytes 196608 | tf_op jit(solution)/shard_map/all_to_all | solution.py:220
  115.7 14.8 %all_to_all.47 = bf16[16,24,256]{2,1,0:T(8,128)(2,1)S(1)} all-to-all(bf16[16,24,256]{2,1,0:T(8,128)(2,1)S(1)} %broadcast_in_dim.7), channel_id=1, replica_groups=mesh['cells_0'=4,'cells_1'=4,'cells_2'=2,'rcpt'=4] {'cells_0','cells_1'}, dimensions={0} | all-to-all | bytes 393216 | tf_op jit(solution)/shard_map/all_to_all | solution.py:220
  130.5 0.6 pad_maximum_fusion
  (6 shorter events, 0.1 us)
Async XLA Ops:
  1.3 0.7 copy-start.2
  2.0 0.7 copy-start.4
  2.7 0.7 copy-start.6
  3.4 27.5 %copy-start = (f32[1,262144]{1,0:T(1,128)S(1)}, f32[1,262144]{1,0:T(1,128)}, u32[]{:S(2)}) copy-start(f32[1,262144]{1,0:T(1,128)} %param.18) | copy-start | bytes 3145732
  3.4 27.5 %copy-start.1 = (f32[1,262144]{1,0:T(1,128)S(1)}, f32[1,262144]{1,0:T(1,128)}, u32[]{:S(2)}) copy-start(f32[1,262144]{1,0:T(1,128)} %param.19) | copy-start | bytes 3145732
  3.4 38.8 %copy-start.5 = (s32[1,256]{1,0:T(1,128)S(1)}, s32[1,256]{1,0:T(1,128)}, u32[]{:S(2)}) copy-start(s32[1,256]{1,0:T(1,128)} %block.7) | copy-start | bytes 3076
  42.2 29.6 %copy-start.3 = (f32[24,256]{1,0:T(8,128)S(1)}, f32[24,256]{1,0:T(8,128)}, u32[]{:S(2)}) copy-start(f32[24,256]{1,0:T(8,128)} %control.3) | copy-start | bytes 73732

commit v3 on v2

--- a/solution.py
+++ b/solution.py
@@ -13,8 +13,7 @@
 step_size = 0.5
 
 ENS_CHUNKS = 8
-TILE_CHUNK = 32
-UNROLL = 8
+UNROLL = 32
 F32 = jnp.float32
 BF16 = jnp.bfloat16
 I32 = jnp.int32
@@ -43,7 +42,12 @@
     lax.fori_loop(0, (live + UNROLL - 1) // UNROLL, lambda g, carry: (work(g), carry)[1], 0)
 
 
-def forward_group(g, live, block, place, tiles, hour_rows, emis, partial):
+def split_halves(value):
+    rounded = value.astype(BF16).astype(F32)
+    return [rounded, value - rounded]
+
+
+def forward_group(g, block, place, tiles, hour_rows, emis, partial):
     hours = emis.shape[1]
     hour_line = lax.broadcasted_iota(I32, (hours, 128), 0)
     none = jnp.zeros((hours, 128), F32)
@@ -57,22 +61,24 @@
         both = jnp.concatenate([tiles[s], tiles[s + 1]], axis=1)
         every = lax.dot_general(pair, both, (((1,), (1,)), ((), ())), preferred_element_type=F32)
         for v in range(2):
-            chosen = (hour_line == these[u + v : u + v + 1, :]) & (s + v < live)
+            chosen = hour_line == these[u + v : u + v + 1, :]
             part = jnp.where(chosen, every[v * hours : (v + 1) * hours], 0.0)
             partial[pl.ds(place[0, s + v], 1), :] = jnp.sum(part, axis=0, keepdims=True)
 
 
 def first_forward_kernel(
     position, block, row, count, row_line, control, background, ensemble, footprint, hour,
-    out, place_out, hour_rows, bg_buf, ens_buf, tile_buf,
-    place, hour_buf, emis, partial, row_ids, ens_sem, bg_sem, tile_sem, hour_sem, place_sem,
+    observed, inv_var,
+    out, place_out, hour_rows, bg_buf, ens_buf, tile_buf, own_observed, own_inv_var,
+    place, line_buf, control_buf, hour_buf, emis, partial, row_ids,
+    ens_sem, bg_sem, tile_sem, hour_sem, place_sem, small_sem,
 ):
     slots = tile_buf.shape[0]
     width = ens_buf.shape[2]
     senders = out.shape[0]
-    share_tiles = hour_buf.shape[0] // senders
+    share_tiles = own_observed.shape[0]
     live = count[0, 0]
-    chunks = slots // TILE_CHUNK
+    chunks = slots // UNROLL
 
     def ens_copy(c):
         return pltpu.make_async_copy(
@@ -85,50 +91,66 @@
         )
 
     def tile_copy(c):
-        part = pl.ds(c * TILE_CHUNK, TILE_CHUNK)
+        part = pl.ds(c * UNROLL, UNROLL)
         return pltpu.make_async_copy(footprint.at[part], tile_buf.at[part], tile_sem.at[c])
 
+    share = pl.ds(position[0] * share_tiles, share_tiles)
+    small = [
+        pltpu.make_async_copy(row_line, line_buf, small_sem.at[0]),
+        pltpu.make_async_copy(control, control_buf, small_sem.at[1]),
+        pltpu.make_async_copy(observed.at[share], own_observed, small_sem.at[2]),
+        pltpu.make_async_copy(inv_var.at[share], own_inv_var, small_sem.at[3]),
+    ]
+    small[0].start()
+    small[1].start()
     for c in range(ENS_CHUNKS):
         ens_copy(c).start()
         bg_copy(c).start()
     hour_copy = pltpu.make_async_copy(hour, hour_buf, hour_sem)
     hour_copy.start()
     for c in range(chunks):
-        @pl.when(c * TILE_CHUNK < live)
+        @pl.when(c * UNROLL < live)
         def _():
             tile_copy(c).start()
-
-    place_out[...] = slot_places(row_line[...], share_tiles, slots // senders)
+    small[2].start()
+    small[3].start()
+
+    small[0].wait()
+    place_out[...] = slot_places(line_buf[...], share_tiles, slots // senders)
     place_copy = pltpu.make_async_copy(place_out, place, place_sem)
     place_copy.start()
     partial[...] = jnp.zeros_like(partial)
     row_ids[...] = jnp.zeros_like(row_ids)
 
-    scaled = control[...].astype(BF16)
+    small[1].wait()
+    scaled = control_buf[...].astype(BF16)
     for c in range(ENS_CHUNKS):
         ens_copy(c).wait()
         bg_copy(c).wait()
         emissions(scaled, bg_buf, ens_buf, emis, c)
     place_copy.wait()
     hour_copy.wait()
-    for c in range(chunks):
-        @pl.when(c * TILE_CHUNK < live)
-        def _():
-            tile_copy(c).wait()
-
-    def work(g):
+
+    def name_group(g):
         for u in range(UNROLL):
             s = g * UNROLL + u
             here = row[0, s]
-            hour_rows[pl.ds(s, 1), :] = hour_buf[pl.ds(here, 1), :]
+            shown = hour_buf[pl.ds(here, 1), :]
+            hour_rows[pl.ds(s, 1), :] = jnp.where(s < live, shown, -1)
             number = (here & (share_tiles - 1)).astype(F32)
             row_ids[pl.ds(place[0, s], 1), :] = jnp.full((1, 128), number)
-        forward_group(g, live, block, place, tile_buf, hour_rows, emis, partial)
+
+    def work(g):
+        name_group(g)
+        tile_copy(g).wait()
+        forward_group(g, block, place, tile_buf, hour_rows, emis, partial)
 
     live_groups(live, work)
-    data = partial[...].reshape(senders, slots // senders, 128)
-    ids = row_ids[...].reshape(senders, slots // senders, 128)
-    out[...] = jnp.concatenate([data, ids], axis=1).astype(BF16)
+    small[2].wait()
+    small[3].wait()
+    parts = split_halves(partial[...]) + [row_ids[...]]
+    parts = [part.reshape(senders, slots // senders, 128) for part in parts]
+    out[...] = jnp.concatenate(parts, axis=1).astype(BF16)
 
 
 def next_forward_kernel(
@@ -144,39 +166,42 @@
     partial[...] = jnp.zeros_like(partial)
     for c in range(ENS_CHUNKS):
         emissions(scaled, bg_buf, ens_buf, emis, c)
-    live_groups(
-        live, lambda g: forward_group(g, live, block, place, tile_buf, hour_rows, emis, partial)
-    )
-    data = partial[...].reshape(senders, slots // senders, 128)
-    rounded = data.astype(BF16).astype(F32)
-    out[...] = jnp.concatenate([rounded, data - rounded], axis=1).astype(BF16)
+    live_groups(live, lambda g: forward_group(g, block, place, tile_buf, hour_rows, emis, partial))
+    parts = [part.reshape(senders, slots // senders, 128) for part in split_halves(partial[...])]
+    out[...] = jnp.concatenate(parts, axis=1).astype(BF16)
 
 
 def owner_pick(received, tiles):
-    ids = received[...].astype(F32)[:, 8:16, 0:tiles].reshape(received.shape[0] * 8, tiles)
+    ids = received[...].astype(F32)[:, 16:24, 0:tiles].reshape(received.shape[0] * 8, tiles)
     lane = lax.broadcasted_iota(I32, ids.shape, 1).astype(F32)
     return jnp.where(ids == lane, 1.0, 0.0).astype(BF16)
 
 
-def picked_sum(pick, part):
-    part = part.reshape(pick.shape[0], 128).astype(BF16)
-    return lax.dot_general(pick, part, (((0,), (0,)), ((), ())), preferred_element_type=F32)
-
-
-def first_departure_kernel(position, received, observed, inv_var, send):
-    pick = owner_pick(received, observed.shape[0])
-    own = picked_sum(pick, received[...].astype(F32)[:, 0:8, :])
+def own_sum(pick, received):
+    both = received[...].astype(F32)
+    own = None
+    for first in (0, 8):
+        part = both[:, first : first + 8, :].reshape(pick.shape[0], 128).astype(BF16)
+        part = lax.dot_general(pick, part, (((0,), (0,)), ((), ())), preferred_element_type=F32)
+        own = part if own is None else own + part
+    return own
+
+
+def send_departure(pick, own, observed, inv_var, send):
     departure = (inv_var[...] * (own - observed[...])).astype(BF16)
     send[...] = jnp.dot(pick, departure, preferred_element_type=F32).astype(BF16)
 
 
-def next_departure_kernel(position, named, received, observed, inv_var, modelled, send):
+def first_departure_kernel(received, observed, inv_var, send):
+    pick = owner_pick(received, observed.shape[0])
+    send_departure(pick, own_sum(pick, received), observed, inv_var, send)
+
+
+def next_departure_kernel(named, received, observed, inv_var, modelled, send):
     pick = owner_pick(named, observed.shape[0])
-    both = received[...].astype(F32)
-    own = picked_sum(pick, both[:, 0:8, :]) + picked_sum(pick, both[:, 8:16, :])
+    own = own_sum(pick, received)
     modelled[...] = own
-    departure = (inv_var[...] * (own - observed[...])).astype(BF16)
-    send[...] = jnp.dot(pick, departure, preferred_element_type=F32).astype(BF16)
+    send_departure(pick, own, observed, inv_var, send)
 
 
 def adjoint_kernel(
@@ -196,7 +221,7 @@
             s = base + u
             weighted = []
             for v in range(2):
-                chosen = (hour_line == these[u + v : u + v + 1, :]) & (s + v < live)
+                chosen = hour_line == these[u + v : u + v + 1, :]
                 weighted.append(jnp.where(chosen, dep_buf[pl.ds(place[0, s + v], 1), :], 0.0))
             pair = jnp.concatenate(weighted, axis=0).astype(BF16)
             both = jnp.concatenate([tile_buf[s], tile_buf[s + 1]], axis=1)
@@ -211,7 +236,12 @@
         total = total + lax.dot_general(
             rounded.astype(BF16), ens_buf[c], (((1,), (1,)), ((), ())), preferred_element_type=F32
         )
-    total = total.astype(BF16)
+    for j in range(out.shape[0]):
+        out[j] = total
+
+
+def sum_kernel(copies, out):
+    total = jnp.sum(copies[...], axis=0).astype(BF16)
     for j in range(out.shape[0]):
         out[j] = total
 
@@ -233,7 +263,6 @@
     rest = lax.axis_size(REST)
     share_tiles = row_tiles // devices
     width = cells_dev // ENS_CHUNKS
-    chunks = slots // TILE_CHUNK
 
     hour_tab = hour.reshape(row_tiles, 128)
     obs_tab = observed.reshape(row_tiles, 128)
@@ -250,26 +279,31 @@
     first_forward = pl.pallas_call(
         first_forward_kernel,
         out_shape=(
-            pltpu.VMEM((devices, 16, 128), BF16),
+            pltpu.VMEM((devices, 24, 128), BF16),
             pltpu.VMEM((1, slots), I32),
             pltpu.VMEM((slots, 128), I32),
             pltpu.VMEM((ENS_CHUNKS, hours, width), F32),
             pltpu.VMEM((ENS_CHUNKS, members, width), BF16),
             pltpu.VMEM((slots, 128, 128), BF16),
+            pltpu.VMEM((share_tiles, 128), F32),
+            pltpu.VMEM((share_tiles, 128), F32),
         ),
-        in_specs=[smem, smem, smem, smem, vmem, vmem, hbm, hbm, hbm, hbm],
-        out_specs=(vmem,) * 6,
+        in_specs=[smem] * 4 + [hbm] * 8,
+        out_specs=(vmem,) * 8,
         scratch_shapes=[
             pltpu.SMEM((1, slots), I32),
+            pltpu.VMEM((1, slots), I32),
+            pltpu.VMEM((hours, members), F32),
             pltpu.VMEM((row_tiles, 128), I32),
             emis,
             slot_lines,
             slot_lines,
             pltpu.SemaphoreType.DMA((ENS_CHUNKS,)),
             pltpu.SemaphoreType.DMA((ENS_CHUNKS,)),
-            pltpu.SemaphoreType.DMA((chunks,)),
+            pltpu.SemaphoreType.DMA((slots // UNROLL,)),
             pltpu.SemaphoreType.DMA,
             pltpu.SemaphoreType.DMA,
+            pltpu.SemaphoreType.DMA((4,)),
         ],
         compiler_params=limit,
         name="first_forward",
@@ -287,27 +321,22 @@
         name="next_forward",
     )
 
-    share = pl.BlockSpec((share_tiles, 128), lambda i, p: (p[0], 0))
     sent = pltpu.VMEM((slots, 128), BF16)
-    own = jax.ShapeDtypeStruct((share_tiles, 128), F32)
+    own = pltpu.VMEM((share_tiles, 128), F32)
 
     def depart(kernel, arrays, out_shape, name):
         return pl.pallas_call(
             kernel,
             out_shape=out_shape,
-            grid_spec=pltpu.PrefetchScalarGridSpec(
-                num_scalar_prefetch=1,
-                grid=(1,),
-                in_specs=[vmem] * arrays + [share, share],
-                out_specs=[vmem] * len(out_shape),
-            ),
+            in_specs=[vmem] * arrays,
+            out_specs=(vmem,) * len(out_shape),
             compiler_params=pltpu.CompilerParams(vmem_limit_bytes=4 * 1024 * 1024),
             name=name,
         )
 
     adjoint = pl.pallas_call(
         adjoint_kernel,
-        out_shape=pltpu.VMEM((rest, hours, members), BF16),
+        out_shape=pltpu.VMEM((rest, hours, members), F32),
         in_specs=[smem, smem, smem] + [vmem] * 4,
         out_specs=vmem,
         scratch_shapes=[slot_lines, emis],
@@ -315,31 +344,38 @@
         name="adjoint",
     )
 
+    add_copies = pl.pallas_call(
+        sum_kernel,
+        out_shape=pltpu.VMEM((plane, hours, members), BF16),
+        in_specs=[vmem],
+        out_specs=vmem,
+        compiler_params=pltpu.CompilerParams(vmem_limit_bytes=4 * 1024 * 1024),
+        name="add_copies",
+    )
+
     def summed(send, place, hour_rows, ens_buf, tile_buf):
         back = exchange(send.reshape(devices, slots // devices, 128), CELLS).reshape(slots, 128)
         copies = adjoint(tile_block, place, tile_count, back, hour_rows, ens_buf, tile_buf)
-        partly = jnp.sum(exchange(copies, REST).astype(F32), axis=0)
-        partly = lax.optimization_barrier(partly).astype(BF16)
-        return exchange(jnp.broadcast_to(partly, (plane, hours, members)), PLANE)
-
-    large = [
+        return exchange(add_copies(exchange(copies, REST)), PLANE)
+
+    pinned = [
         pltpu.with_memory_space_constraint(array, pltpu.HBM)
-        for array in (background, ensemble, footprint[0], hour_tab)
+        for array in (
+            tile_row, control, background, ensemble, footprint[0], hour_tab, obs_tab, var_tab
+        )
     ]
-    partials, place, hour_rows, bg_buf, ens_buf, tile_buf = first_forward(
-        position, tile_block, tile_row, tile_count, tile_row, control, *large
+    partials, place, hour_rows, bg_buf, ens_buf, tile_buf, own_obs, own_var = first_forward(
+        position, tile_block, tile_row, tile_count, *pinned
     )
     named = exchange(partials, CELLS)
-    (send,) = depart(first_departure_kernel, 1, (sent,), "first_departure")(
-        position, named, obs_tab, var_tab
-    )
+    (send,) = depart(first_departure_kernel, 3, (sent,), "first_departure")(named, own_obs, own_var)
     copies = summed(send, place, hour_rows, ens_buf, tile_buf)
     partials, first_grad = next_forward(
         tile_block, place, tile_count, control, copies, hour_rows, bg_buf, ens_buf, tile_buf
     )
     received = exchange(partials, CELLS)
-    final, send = depart(next_departure_kernel, 2, (own, sent), "next_departure")(
-        position, named, received, obs_tab, var_tab
+    final, send = depart(next_departure_kernel, 4, (own, sent), "next_departure")(
+        named, received, own_obs, own_var
     )
     copies = summed(send, place, hour_rows, ens_buf, tile_buf)
     updated = control - step_size * first_grad

time: 131 us -> 123 us (0.939)
  blocking collectives: 108 us -> 86.1 us
  waiting for transfers between devices: 0 us -> 7.72 us
  starting transfers between devices: 0 us -> 4.43 us
    all_to_all x8 -> x7, blocking collectives: 108 us -> 86.1 us  [exchange(): return lax.all_to_all(value, axes, 0, 0, tiled=True)]
    all_to_all x0 -> x1, waiting for transfers between devices: none -> 7.72 us  [exchange(): return lax.all_to_all(value, axes, 0, 0, tiled=True)]
    all_to_all x0 -> x1, starting transfers between devices: none -> 4.43 us  [exchange(): return lax.all_to_all(value, axes, 0, 0, tiled=True)]
    pallas_call x3 -> x5, Pallas kernels: 7.89 us -> 9.36 us  [the longest x1 7.93 us: per_device(): first_forward(position, tile_block, tile_row, tile_count, *pinned)]
  transfers between devices with their start and end apart: 0 -> 1, of which waited for: 0 -> 1; matrix products, arithmetic and copies ran while one was open for 0% -> 1% of each run, Pallas kernels for 0% -> 0%
where the time goes in v3:
time: 123 us; the launch traced here: 122 us
  blocking collectives  86.1 us (70%)
  Pallas kernels  20.3 us (17%)
  waiting for transfers between devices  7.72 us (6%)
  starting transfers between devices  4.43 us (4%)
  between operations  1.37 us (1%)
  local copies, waits for them, and re-layouts  1.3 us (1%)
    all_to_all x7, blocking collectives, exchange(): return lax.all_to_all(value, axes, 0, 0, tiled=True)  86.1 us
    pallas_call x1, Pallas kernels, per_device(): first_forward(position, tile_block, tile_row, tile_count, *pinned)  7.93 us
    pallas_call x2, Pallas kernels, summed(): adjoint(tile_block, place, tile_count, back, hour_rows, ens_buf, tile_buf)  7.8 us
    all_to_all x1, waiting for transfers between devices, exchange(): return lax.all_to_all(value, axes, 0, 0, tiled=True)  7.72 us
    all_to_all x1, starting transfers between devices, exchange(): return lax.all_to_all(value, axes, 0, 0, tiled=True)  4.43 us
    pallas_call x1, Pallas kernels, per_device(): next_forward(tile_block, place, tile_count, control, copies, hour_rows, b...  3.13 us
  transfers between devices with their start and end apart: 1, of which 1 were waited for; matrix products, arithmetic and copies ran while one was open for 1% of the time, Pallas kernels for 0%

profile of v3, /device:TPU:0, one launch (start us, length us, event | category | flops | bytes accessed | tf_op | source)
XLA Modules:
  0.0 121.9 jit_solution(13597681969406257976)
XLA Ops:
  1.3 0.0 copy-start.1
  1.3 0.7 copy-done.1
  2.0 0.0 copy-start.2
  2.0 7.9 %first_forward.1 = (bf16[32,24,128]{2,1,0:T(8,128)(2,1)S(1)}, s32[1,256]{1,0:T(1,128)S(1)}, s32[256,128]{1,0:T(8,128)S(1)}, f32[8,24,2048]{2,1,0:T(8,128)S(1)}, ...) custom-call(s32[1]{0:T(128)} %bitcast.position, ...), custom_call_target="tpu_custom_call" | custom-call | tf_op jit(solution)/shard_map/first_forward/pallas_call | solution.py:367
  9.9 19.8 %all_to_all.40.received.named = bf16[32,24,128]{2,1,0:T(8,128)(2,1)S(1)} all-to-all(bf16[32,24,128]{2,1,0:T(8,128)(2,1)S(1)} %get-tuple-element.15), channel_id=1, replica_groups=mesh['cells_0'=4,'cells_1'=4,'cells_2'=2,'rcpt'=4] {'cells_0','cells_1',..., dimensions={0} | all-to-all | bytes 393216 | tf_op jit(solution)/shard_map/all_to_all | solution.py:250
  29.7 0.4 first_departure.1
  30.0 11.2 %all_to_all.41 = bf16[32,8,128]{2,1,0:T(8,128)(2,1)S(1)} all-to-all(bf16[32,8,128]{2,1,0:T(8,128)(2,1)S(1)} %bitcast.16), channel_id=1, replica_groups=mesh['cells_0'=4,'cells_1'=4,'cells_2'=2,'rcpt'=4] {'cells_0','cells_1',..., dimensions={0} | all-to-all | bytes 131072 | tf_op jit(solution)/shard_map/all_to_all | solution.py:250
  41.2 0.0 copy-done.2
  41.2 0.0 copy-start
  41.2 3.9 %adjoint.2 = f32[8,24,256]{2,1,0:T(8,128)S(1)} custom-call(s32[1,256]{1,0:T(1,128)S(1)} %copy-done.2, s32[1,256]{1,0:T(1,128)S(1)} %get-tuple-element.14.place, s32[1,1]{1,0:T(1,128)S(6)} %copy.13.count, bf16[256,128]{1,0:T(8,128)(2,1)S(1)} %bitcast.15, s32[256,128]{1,0:T(8,128)S(1)} %get-tuple-element.18.hour_rows, ...), custom_call_target="tpu_custom_call" | custom-call | tf_op jit(solution)/shard_map/adjoint/pallas_call | solution.py:358
  45.1 9.4 %all_to_all.42.copies = f32[8,24,256]{2,1,0:T(8,128)S(1)} all-to-all(f32[8,24,256]{2,1,0:T(8,128)S(1)} %adjoint.2), channel_id=1, replica_groups=mesh['cells_0'=4,'cells_1'=4,'cells_2'=2,'rcpt'=4] {'cells_2','rcpt'}, dimensions={0} | all-to-all | bytes 393216 | tf_op jit(solution)/shard_map/all_to_all | solution.py:250
  54.5 12.7 %all_to_all.43.copies = bf16[16,24,256]{2,1,0:T(8,128)(2,1)S(1)} all-to-all(bf16[16,24,256]{2,1,0:T(8,128)(2,1)S(1)} %add_copies.2), channel_id=1, replica_groups=mesh['cells_0'=4,'cells_1'=4,'cells_2'=2,'rcpt'=4] {'cells_0','cells_1'}, dimensions={0} | all-to-all | bytes 393216 | tf_op jit(solution)/shard_map/all_to_all | solution.py:250
  67.2 0.0 copy-done
  67.2 3.1 %next_forward.1 = (bf16[32,16,128]{2,1,0:T(8,128)(2,1)S(1)}, f32[24,256]{1,0:T(8,128)S(1)}) custom-call(s32[1,256]{1,0:T(1,128)S(1)} %copy-done.2, s32[1,256]{1,0:T(1,128)S(1)} %get-tuple-element.14.place, s32[1,1]{1,0:T(1,128)S(6)} %copy.13.count, f32[24,256]{1,0:T(8,128)S(1)} %copy-done, bf16[16,24,256]{2,1,0:T(8,128)(2,1)S(1)} %all_to_all.43.copies, ...), custom_call_target="tpu_custom_call" | custom-call | tf_op jit(solution)/shard_map/next_forward/pallas_call | solution.py:373
  70.4 12.3 %all_to_all.44.received = bf16[32,16,128]{2,1,0:T(8,128)(2,1)S(1)} all-to-all(bf16[32,16,128]{2,1,0:T(8,128)(2,1)S(1)} %get-tuple-element.23), channel_id=1, replica_groups=mesh['cells_0'=4,'cells_1'=4,'cells_2'=2,'rcpt'=4] {'cells_0','cells_1',..., dimensions={0} | all-to-all | bytes 262144 | tf_op jit(solution)/shard_map/all_to_all | solution.py:250
  82.6 0.4 next_departure.1
  83.0 11.0 %all_to_all.45 = bf16[32,8,128]{2,1,0:T(8,128)(2,1)S(1)} all-to-all(bf16[32,8,128]{2,1,0:T(8,128)(2,1)S(1)} %bitcast.18), channel_id=1, replica_groups=mesh['cells_0'=4,'cells_1'=4,'cells_2'=2,'rcpt'=4] {'cells_0','cells_1',..., dimensions={0} | all-to-all | bytes 131072 | tf_op jit(solution)/shard_map/all_to_all | solution.py:250
  94.0 3.9 %adjoint.3 = f32[8,24,256]{2,1,0:T(8,128)S(1)} custom-call(s32[1,256]{1,0:T(1,128)S(1)} %copy-done.2, s32[1,256]{1,0:T(1,128)S(1)} %get-tuple-element.14.place, s32[1,1]{1,0:T(1,128)S(6)} %copy.13.count, bf16[256,128]{1,0:T(8,128)(2,1)S(1)} %bitcast.14, s32[256,128]{1,0:T(8,128)S(1)} %get-tuple-element.18.hour_rows, ...), custom_call_target="tpu_custom_call" | custom-call | tf_op jit(solution)/shard_map/adjoint/pallas_call | solution.py:358
  97.9 9.9 %all_to_all.46.copies = f32[8,24,256]{2,1,0:T(8,128)S(1)} all-to-all(f32[8,24,256]{2,1,0:T(8,128)S(1)} %adjoint.3), channel_id=1, replica_groups=mesh['cells_0'=4,'cells_1'=4,'cells_2'=2,'rcpt'=4] {'cells_2','rcpt'}, dimensions={0} | all-to-all | bytes 393216 | tf_op jit(solution)/shard_map/all_to_all | solution.py:250
  107.7 0.7 add_copies.3
  108.4 4.4 %all-to-all-start.7 = ((bf16[16,24,256]{2,1,0:T(8,128)(2,1)}), bf16[16,24,256]{2,1,0:T(8,128)(2,1)S(1)}, u32[]{:S(2)}, u32[]{:S(2)}) async-start(bf16[16,24,256]{2,1,0:T(8,128)(2,1)} %add_copies.3), calls=%async_computation.7 | async-start | bytes 393216 | tf_op jit(solution)/shard_map/all_to_all | solution.py:250
  112.9 0.6 copy.12
  113.5 7.7 %all-to-all-done.7 = bf16[16,24,256]{2,1,0:T(8,128)(2,1)S(1)} async-done(((bf16[16,24,256]{2,1,0:T(8,128)(2,1)}), bf16[16,24,256]{2,1,0:T(8,128)(2,1)S(1)}, u32[]{:S(2)}, u32[]{:S(2)}) %all-to-all-start.7) | async-done | bytes 196640 | tf_op jit(solution)/shard_map/all_to_all | solution.py:250
  121.3 0.6 pad_maximum_fusion
  (3 shorter events, 0.1 us)
Async XLA Ops:
  1.3 0.7 copy-start.1
  2.0 39.2 %copy-start.2 = (s32[1,256]{1,0:T(1,128)S(1)}, s32[1,256]{1,0:T(1,128)}, u32[]{:S(2)}) copy-start(s32[1,256]{1,0:T(1,128)} %block.7) | copy-start | bytes 3076
  41.2 26.1 %copy-start = (f32[24,256]{1,0:T(8,128)S(1)}, f32[24,256]{1,0:T(8,128)}, u32[]{:S(2)}) copy-start(f32[24,256]{1,0:T(8,128)} %control.3) | copy-start | bytes 73732
  108.4 12.8 %all-to-all-start.7 = ((bf16[16,24,256]{2,1,0:T(8,128)(2,1)}), bf16[16,24,256]{2,1,0:T(8,128)(2,1)S(1)}, u32[]{:S(2)}, u32[]{:S(2)}) async-start(bf16[16,24,256]{2,1,0:T(8,128)(2,1)} %add_copies.3), calls=%async_computation.7 | async-start | bytes 393216 | tf_op jit(solution)/shard_map/all_to_all | solution.py:250

commit v4 on v3

--- a/solution.py
+++ b/solution.py
@@ -14,6 +14,7 @@
 
 ENS_CHUNKS = 8
 UNROLL = 32
+NAMES = 8
 F32 = jnp.float32
 BF16 = jnp.bfloat16
 I32 = jnp.int32
@@ -67,17 +68,16 @@
 
 
 def first_forward_kernel(
-    position, block, row, count, row_line, control, background, ensemble, footprint, hour,
+    position, count, block_in, row_in, control, background, ensemble, footprint, hour,
     observed, inv_var,
     out, place_out, hour_rows, bg_buf, ens_buf, tile_buf, own_observed, own_inv_var,
-    place, line_buf, control_buf, hour_buf, emis, partial, row_ids,
+    place, block, row, line_buf, control_buf, hour_buf, emis, partial, row_ids,
     ens_sem, bg_sem, tile_sem, hour_sem, place_sem, small_sem,
 ):
     slots = tile_buf.shape[0]
     width = ens_buf.shape[2]
     senders = out.shape[0]
     share_tiles = own_observed.shape[0]
-    live = count[0, 0]
     chunks = slots // UNROLL
 
     def ens_copy(c):
@@ -95,25 +95,18 @@
         return pltpu.make_async_copy(footprint.at[part], tile_buf.at[part], tile_sem.at[c])
 
     share = pl.ds(position[0] * share_tiles, share_tiles)
-    small = [
-        pltpu.make_async_copy(row_line, line_buf, small_sem.at[0]),
-        pltpu.make_async_copy(control, control_buf, small_sem.at[1]),
-        pltpu.make_async_copy(observed.at[share], own_observed, small_sem.at[2]),
-        pltpu.make_async_copy(inv_var.at[share], own_inv_var, small_sem.at[3]),
+    pairs = [
+        (row_in, line_buf), (control, control_buf), (row_in, row),
+        (block_in, block), (observed.at[share], own_observed), (inv_var.at[share], own_inv_var),
     ]
-    small[0].start()
-    small[1].start()
+    small = [pltpu.make_async_copy(a, b, small_sem.at[i]) for i, (a, b) in enumerate(pairs)]
+    for copy in small[:4]:
+        copy.start()
+    hour_copy = pltpu.make_async_copy(hour, hour_buf, hour_sem)
+    hour_copy.start()
     for c in range(ENS_CHUNKS):
         ens_copy(c).start()
         bg_copy(c).start()
-    hour_copy = pltpu.make_async_copy(hour, hour_buf, hour_sem)
-    hour_copy.start()
-    for c in range(chunks):
-        @pl.when(c * UNROLL < live)
-        def _():
-            tile_copy(c).start()
-    small[2].start()
-    small[3].start()
 
     small[0].wait()
     place_out[...] = slot_places(line_buf[...], share_tiles, slots // senders)
@@ -121,33 +114,49 @@
     place_copy.start()
     partial[...] = jnp.zeros_like(partial)
     row_ids[...] = jnp.zeros_like(row_ids)
-
+    live = count[0, 0]
     small[1].wait()
     scaled = control_buf[...].astype(BF16)
-    for c in range(ENS_CHUNKS):
-        ens_copy(c).wait()
-        bg_copy(c).wait()
-        emissions(scaled, bg_buf, ens_buf, emis, c)
-    place_copy.wait()
-    hour_copy.wait()
-
-    def name_group(g):
-        for u in range(UNROLL):
-            s = g * UNROLL + u
+
+    def start_tiles(c):
+        @pl.when(c * UNROLL < live)
+        def _():
+            tile_copy(c).start()
+
+    def name_slots(g, carry):
+        for u in range(NAMES):
+            s = g * NAMES + u
             here = row[0, s]
             shown = hour_buf[pl.ds(here, 1), :]
             hour_rows[pl.ds(s, 1), :] = jnp.where(s < live, shown, -1)
             number = (here & (share_tiles - 1)).astype(F32)
             row_ids[pl.ds(place[0, s], 1), :] = jnp.full((1, 128), number)
+        return carry
+
+    for c in range(ENS_CHUNKS):
+        ens_copy(c).wait()
+        bg_copy(c).wait()
+        if c < chunks:
+            start_tiles(c)
+        emissions(scaled, bg_buf, ens_buf, emis, c)
+        if c == 1:
+            small[2].wait()
+            place_copy.wait()
+            hour_copy.wait()
+            lax.fori_loop(0, ((live + UNROLL - 1) // UNROLL) * (UNROLL // NAMES), name_slots, 0)
+    for c in range(ENS_CHUNKS, chunks):
+        start_tiles(c)
+    small[4].start()
+    small[5].start()
+    small[3].wait()
 
     def work(g):
-        name_group(g)
         tile_copy(g).wait()
         forward_group(g, block, place, tile_buf, hour_rows, emis, partial)
 
     live_groups(live, work)
-    small[2].wait()
-    small[3].wait()
+    small[4].wait()
+    small[5].wait()
     parts = split_halves(partial[...]) + [row_ids[...]]
     parts = [part.reshape(senders, slots // senders, 128) for part in parts]
     out[...] = jnp.concatenate(parts, axis=1).astype(BF16)
@@ -160,7 +169,7 @@
     live = count[0, 0]
     slots = tile_buf.shape[0]
     senders = out.shape[0]
-    total = control[...] + jnp.sum(copies[...].astype(F32), axis=0)
+    total = control[...] + jnp.sum(copies[...], axis=0)
     gradient[...] = total
     scaled = (control[...] - step_size * total).astype(BF16)
     partial[...] = jnp.zeros_like(partial)
@@ -236,12 +245,25 @@
         total = total + lax.dot_general(
             rounded.astype(BF16), ens_buf[c], (((1,), (1,)), ((), ())), preferred_element_type=F32
         )
+    total = total.astype(BF16)
     for j in range(out.shape[0]):
         out[j] = total
 
 
+def last_adjoint_kernel(
+    block, place, count, departures, hour_rows, ens_buf, tile_buf, own, out, final,
+    dep_buf, adjoint, sem,
+):
+    copy = pltpu.make_async_copy(own, final, sem)
+    copy.start()
+    adjoint_kernel(
+        block, place, count, departures, hour_rows, ens_buf, tile_buf, out, dep_buf, adjoint
+    )
+    copy.wait()
+
+
 def sum_kernel(copies, out):
-    total = jnp.sum(copies[...], axis=0).astype(BF16)
+    total = jnp.sum(copies[...].astype(F32), axis=0)
     for j in range(out.shape[0]):
         out[j] = total
 
@@ -288,9 +310,11 @@
             pltpu.VMEM((share_tiles, 128), F32),
             pltpu.VMEM((share_tiles, 128), F32),
         ),
-        in_specs=[smem] * 4 + [hbm] * 8,
+        in_specs=[smem, smem] + [hbm] * 9,
         out_specs=(vmem,) * 8,
         scratch_shapes=[
+            pltpu.SMEM((1, slots), I32),
+            pltpu.SMEM((1, slots), I32),
             pltpu.SMEM((1, slots), I32),
             pltpu.VMEM((1, slots), I32),
             pltpu.VMEM((hours, members), F32),
@@ -303,7 +327,7 @@
             pltpu.SemaphoreType.DMA((slots // UNROLL,)),
             pltpu.SemaphoreType.DMA,
             pltpu.SemaphoreType.DMA,
-            pltpu.SemaphoreType.DMA((4,)),
+            pltpu.SemaphoreType.DMA((6,)),
         ],
         compiler_params=limit,
         name="first_forward",
@@ -336,7 +360,7 @@
 
     adjoint = pl.pallas_call(
         adjoint_kernel,
-        out_shape=pltpu.VMEM((rest, hours, members), F32),
+        out_shape=pltpu.VMEM((rest, hours, members), BF16),
         in_specs=[smem, smem, smem] + [vmem] * 4,
         out_specs=vmem,
         scratch_shapes=[slot_lines, emis],
@@ -346,40 +370,59 @@
 
     add_copies = pl.pallas_call(
         sum_kernel,
-        out_shape=pltpu.VMEM((plane, hours, members), BF16),
+        out_shape=pltpu.VMEM((plane, hours, members), F32),
         in_specs=[vmem],
         out_specs=vmem,
         compiler_params=pltpu.CompilerParams(vmem_limit_bytes=4 * 1024 * 1024),
         name="add_copies",
     )
 
-    def summed(send, place, hour_rows, ens_buf, tile_buf):
-        back = exchange(send.reshape(devices, slots // devices, 128), CELLS).reshape(slots, 128)
-        copies = adjoint(tile_block, place, tile_count, back, hour_rows, ens_buf, tile_buf)
+    last_adjoint = pl.pallas_call(
+        last_adjoint_kernel,
+        out_shape=(
+            pltpu.VMEM((rest, hours, members), BF16),
+            jax.ShapeDtypeStruct((share_tiles, 128), F32),
+        ),
+        in_specs=[smem, smem, smem] + [vmem] * 5,
+        out_specs=(vmem, hbm),
+        scratch_shapes=[slot_lines, emis, pltpu.SemaphoreType.DMA],
+        compiler_params=limit,
+        name="last_adjoint",
+    )
+
+    def sent_back(send):
+        return exchange(send.reshape(devices, slots // devices, 128), CELLS).reshape(slots, 128)
+
+    def summed(copies):
         return exchange(add_copies(exchange(copies, REST)), PLANE)
 
     pinned = [
         pltpu.with_memory_space_constraint(array, pltpu.HBM)
         for array in (
-            tile_row, control, background, ensemble, footprint[0], hour_tab, obs_tab, var_tab
+            tile_block, tile_row, control, background, ensemble, footprint[0],
+            hour_tab, obs_tab, var_tab,
         )
     ]
     partials, place, hour_rows, bg_buf, ens_buf, tile_buf, own_obs, own_var = first_forward(
-        position, tile_block, tile_row, tile_count, *pinned
+        position, tile_count, *pinned
     )
     named = exchange(partials, CELLS)
     (send,) = depart(first_departure_kernel, 3, (sent,), "first_departure")(named, own_obs, own_var)
-    copies = summed(send, place, hour_rows, ens_buf, tile_buf)
+    kept = (hour_rows, ens_buf, tile_buf)
+    copies = summed(adjoint(tile_block, place, tile_count, sent_back(send), *kept))
     partials, first_grad = next_forward(
         tile_block, place, tile_count, control, copies, hour_rows, bg_buf, ens_buf, tile_buf
     )
     received = exchange(partials, CELLS)
-    final, send = depart(next_departure_kernel, 4, (own, sent), "next_departure")(
+    modelled, send = depart(next_departure_kernel, 4, (own, sent), "next_departure")(
         named, received, own_obs, own_var
     )
-    copies = summed(send, place, hour_rows, ens_buf, tile_buf)
+    copies, final = last_adjoint(
+        tile_block, place, tile_count, sent_back(send), *kept, modelled
+    )
+    copies = summed(copies)
     updated = control - step_size * first_grad
-    second_grad = updated + jnp.sum(copies.astype(F32), axis=0)
+    second_grad = updated + jnp.sum(copies, axis=0)
     return jnp.stack([first_grad, second_grad]), final.reshape(1, receptors // devices)
 
 

time: 123 us -> 120 us (0.976)
  blocking collectives: 86.1 us -> 97.7 us
  waiting for transfers between devices: 7.72 us -> 0 us
  starting transfers between devices: 4.43 us -> 0 us
  Pallas kernels: 20.3 us -> 18.8 us
  local copies, waits for them, and re-layouts: 1.3 us -> 0.01 us
    all_to_all x7 -> x8, blocking collectives: 86.1 us -> 97.7 us  [exchange(): return lax.all_to_all(value, axes, 0, 0, tiled=True)]
    all_to_all x1 -> x0, waiting for transfers between devices: 7.72 us -> none  [exchange(): return lax.all_to_all(value, axes, 0, 0, tiled=True)]
    all_to_all x1 -> x0, starting transfers between devices: 4.43 us -> none  [exchange(): return lax.all_to_all(value, axes, 0, 0, tiled=True)]
    unnamed x7 -> x4, local copies, waits for them, and re-layouts: 1.3 us -> 0.01 us
  transfers between devices with their start and end apart: 1 -> 0, of which waited for: 1 -> 0; matrix products, arithmetic and copies ran while one was open for 1% -> 0% of each run, Pallas kernels for 0% -> 0%
where the time goes in v4:
time: 120 us; the launch traced here: 118 us
  blocking collectives  97.7 us (81%)
  Pallas kernels  18.8 us (16%)
  between operations  1.36 us (1%)
    all_to_all x8, blocking collectives, exchange(): return lax.all_to_all(value, axes, 0, 0, tiled=True)  97.7 us
    pallas_call x1, Pallas kernels, per_device(): first_forward(position, tile_count, *pinned)  7.1 us
    pallas_call x1, Pallas kernels, per_device(): last_adjoint(tile_block, place, tile_count, sent_back(send), *kept, model...  3.91 us
    pallas_call x1, Pallas kernels, per_device(): adjoint(tile_block, place, tile_count, sent_back(send), *kept)  3.89 us
    pallas_call x1, Pallas kernels, per_device(): next_forward(tile_block, place, tile_count, control, copies, hour_rows, b...  3.1 us

profile of v4, /device:TPU:0, one launch (start us, length us, event | category | flops | bytes accessed | tf_op | source)
XLA Modules:
  0.0 118.5 jit_solution(15077278942030246462)
XLA Ops:
  1.3 0.0 copy-start.1
  1.3 7.1 %first_forward.1 = (bf16[32,24,128]{2,1,0:T(8,128)(2,1)S(1)}, s32[1,256]{1,0:T(1,128)S(1)}, s32[256,128]{1,0:T(8,128)S(1)}, f32[8,24,2048]{2,1,0:T(8,128)S(1)}, ...) custom-call(s32[1]{0:T(128)} %bitcast.position, ...), custom_call_target="tpu_custom_call" | custom-call | tf_op jit(solution)/shard_map/first_forward/pallas_call | solution.py:406
  8.4 17.4 %all_to_all.40.received.named = bf16[32,24,128]{2,1,0:T(8,128)(2,1)S(1)} all-to-all(bf16[32,24,128]{2,1,0:T(8,128)(2,1)S(1)} %get-tuple-element.17), channel_id=1, replica_groups=mesh['cells_0'=4,'cells_1'=4,'cells_2'=2,'rcpt'=4] {'cells_0','cells_1',..., dimensions={0} | all-to-all | bytes 393216 | tf_op jit(solution)/shard_map/all_to_all | solution.py:272
  25.8 0.4 first_departure.1
  26.2 11.2 %all_to_all.41 = bf16[32,8,128]{2,1,0:T(8,128)(2,1)S(1)} all-to-all(bf16[32,8,128]{2,1,0:T(8,128)(2,1)S(1)} %bitcast.15), channel_id=1, replica_groups=mesh['cells_0'=4,'cells_1'=4,'cells_2'=2,'rcpt'=4] {'cells_0','cells_1',..., dimensions={0} | all-to-all | bytes 131072 | tf_op jit(solution)/shard_map/all_to_all | solution.py:272
  37.4 0.0 copy-done.1
  37.4 0.0 copy-start
  37.4 3.9 %adjoint.1 = bf16[8,24,256]{2,1,0:T(8,128)(2,1)S(1)} custom-call(s32[1,256]{1,0:T(1,128)S(1)} %copy-done.1, s32[1,256]{1,0:T(1,128)S(1)} %get-tuple-element.16.place, s32[1,1]{1,0:T(1,128)S(6)} %copy.12.count, bf16[256,128]{1,0:T(8,128)(2,1)S(1)} %bitcast.14, s32[256,128]{1,0:T(8,128)S(1)} %get-tuple-element.20.hour_rows, ...), custom_call_target="tpu_custom_call" | custom-call | tf_op jit(solution)/shard_map/adjoint/pallas_call | solution.py:412
  41.3 10.0 %all_to_all.42.copies = bf16[8,24,256]{2,1,0:T(8,128)(2,1)S(1)} all-to-all(bf16[8,24,256]{2,1,0:T(8,128)(2,1)S(1)} %adjoint.1), channel_id=1, replica_groups=mesh['cells_0'=4,'cells_1'=4,'cells_2'=2,'rcpt'=4] {'cells_2','rcpt'}, dimensions={0} | all-to-all | bytes 196608 | tf_op jit(solution)/shard_map/all_to_all | solution.py:272
  51.3 14.1 %all_to_all.43.copies = f32[16,24,256]{2,1,0:T(8,128)S(1)} all-to-all(f32[16,24,256]{2,1,0:T(8,128)S(1)} %add_copies.2), channel_id=1, replica_groups=mesh['cells_0'=4,'cells_1'=4,'cells_2'=2,'rcpt'=4] {'cells_0','cells_1'}, dimensions={0} | all-to-all | bytes 786432 | tf_op jit(solution)/shard_map/all_to_all | solution.py:272
  65.4 0.0 copy-done
  65.4 3.1 %next_forward.1 = (bf16[32,16,128]{2,1,0:T(8,128)(2,1)S(1)}, f32[24,256]{1,0:T(8,128)S(1)}) custom-call(s32[1,256]{1,0:T(1,128)S(1)} %copy-done.1, s32[1,256]{1,0:T(1,128)S(1)} %get-tuple-element.16.place, s32[1,1]{1,0:T(1,128)S(6)} %copy.12.count, f32[24,256]{1,0:T(8,128)S(1)} %copy-done, f32[16,24,256]{2,1,0:T(8,128)S(1)} %all_to_all.43.copies, ...), custom_call_target="tpu_custom_call" | custom-call | tf_op jit(solution)/shard_map/next_forward/pallas_call | solution.py:413
  68.5 11.7 %all_to_all.44.received = bf16[32,16,128]{2,1,0:T(8,128)(2,1)S(1)} all-to-all(bf16[32,16,128]{2,1,0:T(8,128)(2,1)S(1)} %get-tuple-element.25), channel_id=1, replica_groups=mesh['cells_0'=4,'cells_1'=4,'cells_2'=2,'rcpt'=4] {'cells_0','cells_1',..., dimensions={0} | all-to-all | bytes 262144 | tf_op jit(solution)/shard_map/all_to_all | solution.py:272
  80.2 0.4 next_departure.1
  80.5 11.0 %all_to_all.45 = bf16[32,8,128]{2,1,0:T(8,128)(2,1)S(1)} all-to-all(bf16[32,8,128]{2,1,0:T(8,128)(2,1)S(1)} %bitcast.17), channel_id=1, replica_groups=mesh['cells_0'=4,'cells_1'=4,'cells_2'=2,'rcpt'=4] {'cells_0','cells_1',..., dimensions={0} | all-to-all | bytes 131072 | tf_op jit(solution)/shard_map/all_to_all | solution.py:272
  91.5 3.9 %last_adjoint.1 = (bf16[8,24,256]{2,1,0:T(8,128)(2,1)S(1)}, f32[64,128]{1,0:T(8,128)}) custom-call(s32[1,256]{1,0:T(1,128)S(1)} %copy-done.1, s32[1,256]{1,0:T(1,128)S(1)} %get-tuple-element.16.place, s32[1,1]{1,0:T(1,128)S(6)} %copy.12.count, bf16[256,128]{1,0:T(8,128)(2,1)S(1)} %bitcast.13, s32[256,128]{1,0:T(8,128)S(1)} %get-tuple-element.20.hour_rows, ...), custom_call_target="tpu_custom_call" | custom-call | tf_op jit(solution)/shard_map/last_adjoint/pallas_call | solution.py:420
  95.4 8.2 %all_to_all.46.copies = bf16[8,24,256]{2,1,0:T(8,128)(2,1)S(1)} all-to-all(bf16[8,24,256]{2,1,0:T(8,128)(2,1)S(1)} %get-tuple-element.28), channel_id=1, replica_groups=mesh['cells_0'=4,'cells_1'=4,'cells_2'=2,'rcpt'=4] {'cells_2','rcpt'}, dimensions={0} | all-to-all | bytes 196608 | tf_op jit(solution)/shard_map/all_to_all | solution.py:272
  103.7 14.1 %all_to_all.47 = f32[16,24,256]{2,1,0:T(8,128)S(1)} all-to-all(f32[16,24,256]{2,1,0:T(8,128)S(1)} %add_copies.3), channel_id=1, replica_groups=mesh['cells_0'=4,'cells_1'=4,'cells_2'=2,'rcpt'=4] {'cells_0','cells_1'}, dimensions={0} | all-to-all | bytes 786432 | tf_op jit(solution)/shard_map/all_to_all | solution.py:272
  117.9 0.6 pad_maximum_fusion
  (4 shorter events, 0.1 us)
Async XLA Ops:
  1.3 36.1 %copy-start.1 = (s32[1,256]{1,0:T(1,128)S(1)}, s32[1,256]{1,0:T(1,128)}, u32[]{:S(2)}) copy-start(s32[1,256]{1,0:T(1,128)} %block.5) | copy-start | bytes 3076
  37.4 28.1 %copy-start = (f32[24,256]{1,0:T(8,128)S(1)}, f32[24,256]{1,0:T(8,128)}, u32[]{:S(2)}) copy-start(f32[24,256]{1,0:T(8,128)} %control.3) | copy-start | bytes 73732

commit v5 on v4

--- a/solution.py
+++ b/solution.py
@@ -13,7 +13,8 @@
 step_size = 0.5
 
 ENS_CHUNKS = 8
-UNROLL = 32
+TILE_CHUNK = 32
+UNROLL = 64
 NAMES = 8
 F32 = jnp.float32
 BF16 = jnp.bfloat16
@@ -39,22 +40,17 @@
         emis[c * blocks + b] = values[:, b * 128 : (b + 1) * 128]
 
 
-def live_groups(live, work):
-    lax.fori_loop(0, (live + UNROLL - 1) // UNROLL, lambda g, carry: (work(g), carry)[1], 0)
-
-
-def split_halves(value):
-    rounded = value.astype(BF16).astype(F32)
-    return [rounded, value - rounded]
-
-
-def forward_group(g, block, place, tiles, hour_rows, emis, partial):
+def live_groups(live, unroll, work):
+    lax.fori_loop(0, (live + unroll - 1) // unroll, lambda g, carry: (work(g), carry)[1], 0)
+
+
+def forward_group(g, unroll, block, place, tiles, hour_rows, emis, partial):
     hours = emis.shape[1]
     hour_line = lax.broadcasted_iota(I32, (hours, 128), 0)
     none = jnp.zeros((hours, 128), F32)
-    base = pl.multiple_of(g * UNROLL, UNROLL)
-    these = hour_rows[pl.ds(base, UNROLL), :]
-    for u in range(0, UNROLL, 2):
+    base = pl.multiple_of(g * unroll, unroll)
+    these = hour_rows[pl.ds(base, unroll), :]
+    for u in range(0, unroll, 2):
         s = base + u
         left = jnp.concatenate([emis[block[0, s]], none], axis=1)
         right = jnp.concatenate([none, emis[block[0, s + 1]]], axis=1)
@@ -78,7 +74,7 @@
     width = ens_buf.shape[2]
     senders = out.shape[0]
     share_tiles = own_observed.shape[0]
-    chunks = slots // UNROLL
+    chunks = slots // TILE_CHUNK
 
     def ens_copy(c):
         return pltpu.make_async_copy(
@@ -91,7 +87,7 @@
         )
 
     def tile_copy(c):
-        part = pl.ds(c * UNROLL, UNROLL)
+        part = pl.ds(c * TILE_CHUNK, TILE_CHUNK)
         return pltpu.make_async_copy(footprint.at[part], tile_buf.at[part], tile_sem.at[c])
 
     share = pl.ds(position[0] * share_tiles, share_tiles)
@@ -115,11 +111,12 @@
     partial[...] = jnp.zeros_like(partial)
     row_ids[...] = jnp.zeros_like(row_ids)
     live = count[0, 0]
+    filled = ((live + UNROLL - 1) // UNROLL) * UNROLL
     small[1].wait()
     scaled = control_buf[...].astype(BF16)
 
     def start_tiles(c):
-        @pl.when(c * UNROLL < live)
+        @pl.when(c * TILE_CHUNK < filled)
         def _():
             tile_copy(c).start()
 
@@ -143,7 +140,7 @@
             small[2].wait()
             place_copy.wait()
             hour_copy.wait()
-            lax.fori_loop(0, ((live + UNROLL - 1) // UNROLL) * (UNROLL // NAMES), name_slots, 0)
+            lax.fori_loop(0, filled // NAMES, name_slots, 0)
     for c in range(ENS_CHUNKS, chunks):
         start_tiles(c)
     small[4].start()
@@ -152,13 +149,12 @@
 
     def work(g):
         tile_copy(g).wait()
-        forward_group(g, block, place, tile_buf, hour_rows, emis, partial)
-
-    live_groups(live, work)
+        forward_group(g, TILE_CHUNK, block, place, tile_buf, hour_rows, emis, partial)
+
+    live_groups(filled, TILE_CHUNK, work)
     small[4].wait()
     small[5].wait()
-    parts = split_halves(partial[...]) + [row_ids[...]]
-    parts = [part.reshape(senders, slots // senders, 128) for part in parts]
+    parts = [part[...].reshape(senders, slots // senders, 128) for part in (partial, row_ids)]
     out[...] = jnp.concatenate(parts, axis=1).astype(BF16)
 
 
@@ -167,33 +163,27 @@
     out, gradient, emis, partial,
 ):
     live = count[0, 0]
-    slots = tile_buf.shape[0]
-    senders = out.shape[0]
-    total = control[...] + jnp.sum(copies[...], axis=0)
+    total = control[...] + jnp.sum(copies[...].astype(F32), axis=0)
     gradient[...] = total
     scaled = (control[...] - step_size * total).astype(BF16)
     partial[...] = jnp.zeros_like(partial)
     for c in range(ENS_CHUNKS):
         emissions(scaled, bg_buf, ens_buf, emis, c)
-    live_groups(live, lambda g: forward_group(g, block, place, tile_buf, hour_rows, emis, partial))
-    parts = [part.reshape(senders, slots // senders, 128) for part in split_halves(partial[...])]
-    out[...] = jnp.concatenate(parts, axis=1).astype(BF16)
+    live_groups(
+        live, UNROLL,
+        lambda g: forward_group(g, UNROLL, block, place, tile_buf, hour_rows, emis, partial),
+    )
+    out[...] = partial[...].astype(BF16)
 
 
 def owner_pick(received, tiles):
-    ids = received[...].astype(F32)[:, 16:24, 0:tiles].reshape(received.shape[0] * 8, tiles)
+    ids = received[...].astype(F32)[:, 8:16, 0:tiles].reshape(received.shape[0] * 8, tiles)
     lane = lax.broadcasted_iota(I32, ids.shape, 1).astype(F32)
     return jnp.where(ids == lane, 1.0, 0.0).astype(BF16)
 
 
 def own_sum(pick, received):
-    both = received[...].astype(F32)
-    own = None
-    for first in (0, 8):
-        part = both[:, first : first + 8, :].reshape(pick.shape[0], 128).astype(BF16)
-        part = lax.dot_general(pick, part, (((0,), (0,)), ((), ())), preferred_element_type=F32)
-        own = part if own is None else own + part
-    return own
+    return lax.dot_general(pick, received, (((0,), (0,)), ((), ())), preferred_element_type=F32)
 
 
 def send_departure(pick, own, observed, inv_var, send):
@@ -203,12 +193,13 @@
 
 def first_departure_kernel(received, observed, inv_var, send):
     pick = owner_pick(received, observed.shape[0])
-    send_departure(pick, own_sum(pick, received), observed, inv_var, send)
+    data = received[...].astype(F32)[:, 0:8, :].reshape(pick.shape[0], 128).astype(BF16)
+    send_departure(pick, own_sum(pick, data), observed, inv_var, send)
 
 
 def next_departure_kernel(named, received, observed, inv_var, modelled, send):
     pick = owner_pick(named, observed.shape[0])
-    own = own_sum(pick, received)
+    own = own_sum(pick, received[...])
     modelled[...] = own
     send_departure(pick, own, observed, inv_var, send)
 
@@ -238,13 +229,14 @@
             adjoint[block[0, s]] += every[0:hours, 0:128]
             adjoint[block[0, s + 1]] += every[hours : 2 * hours, 128:256]
 
-    live_groups(live, work)
-    total = jnp.zeros(out.shape[1:], F32)
+    live_groups(live, UNROLL, work)
+    total = jnp.zeros((ens_buf.shape[1], hours), F32)
     for c in range(ENS_CHUNKS):
         rounded = jnp.concatenate([adjoint[c * blocks + b] for b in range(blocks)], axis=1)
         total = total + lax.dot_general(
-            rounded.astype(BF16), ens_buf[c], (((1,), (1,)), ((), ())), preferred_element_type=F32
+            ens_buf[c], rounded.astype(BF16), (((1,), (1,)), ((), ())), preferred_element_type=F32
         )
+    total = jnp.transpose(total)
     total = total.astype(BF16)
     for j in range(out.shape[0]):
         out[j] = total
@@ -263,7 +255,7 @@
 
 
 def sum_kernel(copies, out):
-    total = jnp.sum(copies[...].astype(F32), axis=0)
+    total = jnp.sum(copies[...].astype(F32), axis=0).astype(out.dtype)
     for j in range(out.shape[0]):
         out[j] = total
 
@@ -301,7 +293,7 @@
     first_forward = pl.pallas_call(
         first_forward_kernel,
         out_shape=(
-            pltpu.VMEM((devices, 24, 128), BF16),
+            pltpu.VMEM((devices, 16, 128), BF16),
             pltpu.VMEM((1, slots), I32),
             pltpu.VMEM((slots, 128), I32),
             pltpu.VMEM((ENS_CHUNKS, hours, width), F32),
@@ -324,7 +316,7 @@
             slot_lines,
             pltpu.SemaphoreType.DMA((ENS_CHUNKS,)),
             pltpu.SemaphoreType.DMA((ENS_CHUNKS,)),
-            pltpu.SemaphoreType.DMA((slots // UNROLL,)),
+            pltpu.SemaphoreType.DMA((slots // TILE_CHUNK,)),
             pltpu.SemaphoreType.DMA,
             pltpu.SemaphoreType.DMA,
             pltpu.SemaphoreType.DMA((6,)),
@@ -335,7 +327,7 @@
     next_forward = pl.pallas_call(
         next_forward_kernel,
         out_shape=(
-            pltpu.VMEM((devices, 16, 128), BF16),
+            pltpu.VMEM((slots, 128), BF16),
             jax.ShapeDtypeStruct((hours, members), F32),
         ),
         in_specs=[smem, smem, smem] + [vmem] * 6,
@@ -368,14 +360,15 @@
         name="adjoint",
     )
 
-    add_copies = pl.pallas_call(
-        sum_kernel,
-        out_shape=pltpu.VMEM((plane, hours, members), F32),
-        in_specs=[vmem],
-        out_specs=vmem,
-        compiler_params=pltpu.CompilerParams(vmem_limit_bytes=4 * 1024 * 1024),
-        name="add_copies",
-    )
+    def add_copies(copies, kind):
+        return pl.pallas_call(
+            sum_kernel,
+            out_shape=pltpu.VMEM((plane, hours, members), kind),
+            in_specs=[vmem],
+            out_specs=vmem,
+            compiler_params=pltpu.CompilerParams(vmem_limit_bytes=4 * 1024 * 1024),
+            name="add_copies",
+        )(copies)
 
     last_adjoint = pl.pallas_call(
         last_adjoint_kernel,
@@ -390,11 +383,11 @@
         name="last_adjoint",
     )
 
-    def sent_back(send):
-        return exchange(send.reshape(devices, slots // devices, 128), CELLS).reshape(slots, 128)
-
-    def summed(copies):
-        return exchange(add_copies(exchange(copies, REST)), PLANE)
+    def by_slots(rows):
+        return exchange(rows.reshape(devices, slots // devices, 128), CELLS).reshape(slots, 128)
+
+    def summed(copies, kind):
+        return exchange(add_copies(exchange(copies, REST), kind), PLANE)
 
     pinned = [
         pltpu.with_memory_space_constraint(array, pltpu.HBM)
@@ -409,20 +402,20 @@
     named = exchange(partials, CELLS)
     (send,) = depart(first_departure_kernel, 3, (sent,), "first_departure")(named, own_obs, own_var)
     kept = (hour_rows, ens_buf, tile_buf)
-    copies = summed(adjoint(tile_block, place, tile_count, sent_back(send), *kept))
+    copies = summed(adjoint(tile_block, place, tile_count, by_slots(send), *kept), F32)
     partials, first_grad = next_forward(
         tile_block, place, tile_count, control, copies, hour_rows, bg_buf, ens_buf, tile_buf
     )
-    received = exchange(partials, CELLS)
+    received = by_slots(partials)
     modelled, send = depart(next_departure_kernel, 4, (own, sent), "next_departure")(
         named, received, own_obs, own_var
     )
     copies, final = last_adjoint(
-        tile_block, place, tile_count, sent_back(send), *kept, modelled
-    )
-    copies = summed(copies)
+        tile_block, place, tile_count, by_slots(send), *kept, modelled
+    )
+    copies = summed(copies, BF16)
     updated = control - step_size * first_grad
-    second_grad = updated + jnp.sum(copies, axis=0)
+    second_grad = updated + jnp.sum(copies.astype(F32), axis=0)
     return jnp.stack([first_grad, second_grad]), final.reshape(1, receptors // devices)
 
 

time: 120 us -> 115 us (0.958)
  blocking collectives: 97.7 us -> 94.6 us
    all_to_all x8, blocking collectives: 97.7 us -> 94.6 us  [exchange(): return lax.all_to_all(value, axes, 0, 0, tiled=True)]
where the time goes in v5:
time: 115 us; the launch traced here: 114 us
  blocking collectives  94.6 us (82%)
  Pallas kernels  17.9 us (16%)
  between operations  1.35 us (1%)
    all_to_all x8, blocking collectives, exchange(): return lax.all_to_all(value, axes, 0, 0, tiled=True)  94.6 us
    pallas_call x1, Pallas kernels, per_device(): first_forward(position, tile_count, *pinned)  7.09 us
    pallas_call x1, Pallas kernels, per_device(): last_adjoint(tile_block, place, tile_count, by_slots(send), *kept, modelled)  3.55 us
    pallas_call x1, Pallas kernels, per_device(): adjoint(tile_block, place, tile_count, by_slots(send), *kept)  3.53 us
    pallas_call x1, Pallas kernels, per_device(): next_forward(tile_block, place, tile_count, control, copies, hour_rows, b...  2.97 us

profile of v5, /device:TPU:0, one launch (start us, length us, event | category | flops | bytes accessed | tf_op | source)
XLA Modules:
  0.0 114.5 jit_solution(15390634974724090263)
XLA Ops:
  1.3 0.0 copy-start.1
  1.3 7.1 %first_forward.1 = (bf16[32,16,128]{2,1,0:T(8,128)(2,1)S(1)}, s32[1,256]{1,0:T(1,128)S(1)}, s32[256,128]{1,0:T(8,128)S(1)}, f32[8,24,2048]{2,1,0:T(8,128)S(1)}, ...) custom-call(s32[1]{0:T(128)} %bitcast.position, ...), custom_call_target="tpu_custom_call" | custom-call | tf_op jit(solution)/shard_map/first_forward/pallas_call | solution.py:399
  8.4 17.3 %all_to_all.40.received.named = bf16[32,16,128]{2,1,0:T(8,128)(2,1)S(1)} all-to-all(bf16[32,16,128]{2,1,0:T(8,128)(2,1)S(1)} %get-tuple-element.17), channel_id=1, replica_groups=mesh['cells_0'=4,'cells_1'=4,'cells_2'=2,'rcpt'=4] {'cells_0','cells_1',..., dimensions={0} | all-to-all | bytes 262144 | tf_op jit(solution)/shard_map/all_to_all | solution.py:264
  25.7 0.3 first_departure.1
  26.0 11.0 %all_to_all.41 = bf16[32,8,128]{2,1,0:T(8,128)(2,1)S(1)} all-to-all(bf16[32,8,128]{2,1,0:T(8,128)(2,1)S(1)} %bitcast.18), channel_id=1, replica_groups=mesh['cells_0'=4,'cells_1'=4,'cells_2'=2,'rcpt'=4] {'cells_0','cells_1',..., dimensions={0} | all-to-all | bytes 131072 | tf_op jit(solution)/shard_map/all_to_all | solution.py:264
  37.0 0.0 copy-done.1
  37.0 0.0 copy-start
  37.0 3.5 %adjoint.1 = bf16[8,24,256]{2,1,0:T(8,128)(2,1)S(1)} custom-call(s32[1,256]{1,0:T(1,128)S(1)} %copy-done.1, s32[1,256]{1,0:T(1,128)S(1)} %get-tuple-element.16.place, s32[1,1]{1,0:T(1,128)S(6)} %copy.12.count, bf16[256,128]{1,0:T(8,128)(2,1)S(1)} %bitcast.16, s32[256,128]{1,0:T(8,128)S(1)} %get-tuple-element.20.hour_rows, ...), custom_call_target="tpu_custom_call" | custom-call | tf_op jit(solution)/shard_map/adjoint/pallas_call | solution.py:405
  40.5 9.7 %all_to_all.42.copies = bf16[8,24,256]{2,1,0:T(8,128)(2,1)S(1)} all-to-all(bf16[8,24,256]{2,1,0:T(8,128)(2,1)S(1)} %adjoint.1), channel_id=1, replica_groups=mesh['cells_0'=4,'cells_1'=4,'cells_2'=2,'rcpt'=4] {'cells_2','rcpt'}, dimensions={0} | all-to-all | bytes 196608 | tf_op jit(solution)/shard_map/all_to_all | solution.py:264
  50.3 13.8 %all_to_all.43.copies = f32[16,24,256]{2,1,0:T(8,128)S(1)} all-to-all(f32[16,24,256]{2,1,0:T(8,128)S(1)} %add_copies.2), channel_id=1, replica_groups=mesh['cells_0'=4,'cells_1'=4,'cells_2'=2,'rcpt'=4] {'cells_0','cells_1'}, dimensions={0} | all-to-all | bytes 786432 | tf_op jit(solution)/shard_map/all_to_all | solution.py:264
  64.1 0.0 copy-done
  64.1 3.0 %next_forward.1 = (bf16[256,128]{1,0:T(8,128)(2,1)S(1)}, f32[24,256]{1,0:T(8,128)S(1)}) custom-call(s32[1,256]{1,0:T(1,128)S(1)} %copy-done.1, s32[1,256]{1,0:T(1,128)S(1)} %get-tuple-element.16.place, s32[1,1]{1,0:T(1,128)S(6)} %copy.12.count, f32[24,256]{1,0:T(8,128)S(1)} %copy-done, f32[16,24,256]{2,1,0:T(8,128)S(1)} %all_to_all.43.copies, ...), custom_call_target="tpu_custom_call" | custom-call | tf_op jit(solution)/shard_map/next_forward/pallas_call | solution.py:406
  67.0 11.3 %all_to_all.44 = bf16[32,8,128]{2,1,0:T(8,128)(2,1)S(1)} all-to-all(bf16[32,8,128]{2,1,0:T(8,128)(2,1)S(1)} %bitcast.21), channel_id=1, replica_groups=mesh['cells_0'=4,'cells_1'=4,'cells_2'=2,'rcpt'=4] {'cells_0','cells_1',..., dimensions={0} | all-to-all | bytes 131072 | tf_op jit(solution)/shard_map/all_to_all | solution.py:264
  78.3 0.3 next_departure.1
  78.6 10.9 %all_to_all.45 = bf16[32,8,128]{2,1,0:T(8,128)(2,1)S(1)} all-to-all(bf16[32,8,128]{2,1,0:T(8,128)(2,1)S(1)} %bitcast.20), channel_id=1, replica_groups=mesh['cells_0'=4,'cells_1'=4,'cells_2'=2,'rcpt'=4] {'cells_0','cells_1',..., dimensions={0} | all-to-all | bytes 131072 | tf_op jit(solution)/shard_map/all_to_all | solution.py:264
  89.5 3.5 %last_adjoint.1 = (bf16[8,24,256]{2,1,0:T(8,128)(2,1)S(1)}, f32[64,128]{1,0:T(8,128)}) custom-call(s32[1,256]{1,0:T(1,128)S(1)} %copy-done.1, s32[1,256]{1,0:T(1,128)S(1)} %get-tuple-element.16.place, s32[1,1]{1,0:T(1,128)S(6)} %copy.12.count, bf16[256,128]{1,0:T(8,128)(2,1)S(1)} %bitcast.15, s32[256,128]{1,0:T(8,128)S(1)} %get-tuple-element.20.hour_rows, ...), custom_call_target="tpu_custom_call" | custom-call | tf_op jit(solution)/shard_map/last_adjoint/pallas_call | solution.py:413
  93.1 8.9 %all_to_all.46.copies = bf16[8,24,256]{2,1,0:T(8,128)(2,1)S(1)} all-to-all(bf16[8,24,256]{2,1,0:T(8,128)(2,1)S(1)} %get-tuple-element.28), channel_id=1, replica_groups=mesh['cells_0'=4,'cells_1'=4,'cells_2'=2,'rcpt'=4] {'cells_2','rcpt'}, dimensions={0} | all-to-all | bytes 196608 | tf_op jit(solution)/shard_map/all_to_all | solution.py:264
  102.0 11.7 %all_to_all.47 = bf16[16,24,256]{2,1,0:T(8,128)(2,1)S(1)} all-to-all(bf16[16,24,256]{2,1,0:T(8,128)(2,1)S(1)} %add_copies.3), channel_id=1, replica_groups=mesh['cells_0'=4,'cells_1'=4,'cells_2'=2,'rcpt'=4] {'cells_0','cells_1'}, dimensions={0} | all-to-all | bytes 393216 | tf_op jit(solution)/shard_map/all_to_all | solution.py:264
  113.8 0.6 pad_maximum_fusion
  (4 shorter events, 0.1 us)
Async XLA Ops:
  1.3 35.7 %copy-start.1 = (s32[1,256]{1,0:T(1,128)S(1)}, s32[1,256]{1,0:T(1,128)}, u32[]{:S(2)}) copy-start(s32[1,256]{1,0:T(1,128)} %block.5) | copy-start | bytes 3076
  37.0 27.1 %copy-start = (f32[24,256]{1,0:T(8,128)S(1)}, f32[24,256]{1,0:T(8,128)}, u32[]{:S(2)}) copy-start(f32[24,256]{1,0:T(8,128)} %control.3) | copy-start | bytes 73732

commit v6 on v5

--- a/solution.py
+++ b/solution.py
@@ -13,6 +13,8 @@
 step_size = 0.5
 
 ENS_CHUNKS = 8
+HOURS_AFTER = 2
+TILES_AT_ONCE = 2
 TILE_CHUNK = 32
 UNROLL = 64
 NAMES = 8
@@ -35,7 +37,6 @@
 def emissions(scaled, background, ensemble, emis, c):
     blocks = ensemble.shape[2] // 128
     values = background[c] + jnp.dot(scaled, ensemble[c], preferred_element_type=F32)
-    values = values.astype(BF16).astype(F32)
     for b in range(blocks):
         emis[c * blocks + b] = values[:, b * 128 : (b + 1) * 128]
 
@@ -64,7 +65,7 @@
 
 
 def first_forward_kernel(
-    position, count, block_in, row_in, control, background, ensemble, footprint, hour,
+    count, block_in, row_in, control, background, ensemble, footprint, hour,
     observed, inv_var,
     out, place_out, hour_rows, bg_buf, ens_buf, tile_buf, own_observed, own_inv_var,
     place, block, row, line_buf, control_buf, hour_buf, emis, partial, row_ids,
@@ -90,7 +91,7 @@
         part = pl.ds(c * TILE_CHUNK, TILE_CHUNK)
         return pltpu.make_async_copy(footprint.at[part], tile_buf.at[part], tile_sem.at[c])
 
-    share = pl.ds(position[0] * share_tiles, share_tiles)
+    share = pl.ds(lax.axis_index(CELLS) * share_tiles, share_tiles)
     pairs = [
         (row_in, line_buf), (control, control_buf), (row_in, row),
         (block_in, block), (observed.at[share], own_observed), (inv_var.at[share], own_inv_var),
@@ -99,18 +100,20 @@
     for copy in small[:4]:
         copy.start()
     hour_copy = pltpu.make_async_copy(hour, hour_buf, hour_sem)
-    hour_copy.start()
     for c in range(ENS_CHUNKS):
         ens_copy(c).start()
         bg_copy(c).start()
+        if c == HOURS_AFTER:
+            hour_copy.start()
 
     small[0].wait()
-    place_out[...] = slot_places(line_buf[...], share_tiles, slots // senders)
+    live = count[0, 0]
+    places = slot_places(line_buf[...], share_tiles, slots // senders)
+    place_out[...] = jnp.concatenate([places, jnp.full((1, 128), live)], axis=1)
     place_copy = pltpu.make_async_copy(place_out, place, place_sem)
     place_copy.start()
     partial[...] = jnp.zeros_like(partial)
     row_ids[...] = jnp.zeros_like(row_ids)
-    live = count[0, 0]
     filled = ((live + UNROLL - 1) // UNROLL) * UNROLL
     small[1].wait()
     scaled = control_buf[...].astype(BF16)
@@ -133,25 +136,25 @@
     for c in range(ENS_CHUNKS):
         ens_copy(c).wait()
         bg_copy(c).wait()
-        if c < chunks:
-            start_tiles(c)
+        for t in range(chunks):
+            if ENS_CHUNKS - 1 - (chunks - 1 - t) // TILES_AT_ONCE == c:
+                start_tiles(t)
         emissions(scaled, bg_buf, ens_buf, emis, c)
-        if c == 1:
+        if c == HOURS_AFTER + 2:
             small[2].wait()
             place_copy.wait()
             hour_copy.wait()
             lax.fori_loop(0, filled // NAMES, name_slots, 0)
-    for c in range(ENS_CHUNKS, chunks):
-        start_tiles(c)
     small[4].start()
     small[5].start()
     small[3].wait()
 
     def work(g):
-        tile_copy(g).wait()
-        forward_group(g, TILE_CHUNK, block, place, tile_buf, hour_rows, emis, partial)
-
-    live_groups(filled, TILE_CHUNK, work)
+        for part in range(UNROLL // TILE_CHUNK):
+            tile_copy(g * (UNROLL // TILE_CHUNK) + part).wait()
+        forward_group(g, UNROLL, block, place, tile_buf, hour_rows, emis, partial)
+
+    live_groups(live, UNROLL, work)
     small[4].wait()
     small[5].wait()
     parts = [part[...].reshape(senders, slots // senders, 128) for part in (partial, row_ids)]
@@ -159,10 +162,10 @@
 
 
 def next_forward_kernel(
-    block, place, count, control, copies, hour_rows, bg_buf, ens_buf, tile_buf,
+    block, place, control, copies, hour_rows, bg_buf, ens_buf, tile_buf,
     out, gradient, emis, partial,
 ):
-    live = count[0, 0]
+    live = place[0, tile_buf.shape[0]]
     total = control[...] + jnp.sum(copies[...].astype(F32), axis=0)
     gradient[...] = total
     scaled = (control[...] - step_size * total).astype(BF16)
@@ -205,11 +208,11 @@
 
 
 def adjoint_kernel(
-    block, place, count, departures, hour_rows, ens_buf, tile_buf, out, dep_buf, adjoint
+    block, place, departures, hour_rows, ens_buf, tile_buf, out, dep_buf, adjoint
 ):
     hours = out.shape[1]
     blocks = ens_buf.shape[2] // 128
-    live = count[0, 0]
+    live = place[0, tile_buf.shape[0]]
     hour_line = lax.broadcasted_iota(I32, (hours, 128), 0)
     dep_buf[...] = departures[...].astype(F32)
     adjoint[...] = jnp.zeros_like(adjoint)
@@ -243,13 +246,13 @@
 
 
 def last_adjoint_kernel(
-    block, place, count, departures, hour_rows, ens_buf, tile_buf, own, out, final,
+    block, place, departures, hour_rows, ens_buf, tile_buf, own, out, final,
     dep_buf, adjoint, sem,
 ):
     copy = pltpu.make_async_copy(own, final, sem)
     copy.start()
     adjoint_kernel(
-        block, place, count, departures, hour_rows, ens_buf, tile_buf, out, dep_buf, adjoint
+        block, place, departures, hour_rows, ens_buf, tile_buf, out, dep_buf, adjoint
     )
     copy.wait()
 
@@ -281,7 +284,6 @@
     hour_tab = hour.reshape(row_tiles, 128)
     obs_tab = observed.reshape(row_tiles, 128)
     var_tab = inv_var.reshape(row_tiles, 128)
-    position = lax.axis_index(CELLS).astype(I32).reshape(1)
 
     smem = pl.BlockSpec(memory_space=pltpu.SMEM)
     vmem = pl.BlockSpec(memory_space=pltpu.VMEM)
@@ -294,7 +296,7 @@
         first_forward_kernel,
         out_shape=(
             pltpu.VMEM((devices, 16, 128), BF16),
-            pltpu.VMEM((1, slots), I32),
+            pltpu.VMEM((1, slots + 128), I32),
             pltpu.VMEM((slots, 128), I32),
             pltpu.VMEM((ENS_CHUNKS, hours, width), F32),
             pltpu.VMEM((ENS_CHUNKS, members, width), BF16),
@@ -302,10 +304,10 @@
             pltpu.VMEM((share_tiles, 128), F32),
             pltpu.VMEM((share_tiles, 128), F32),
         ),
-        in_specs=[smem, smem] + [hbm] * 9,
+        in_specs=[smem] + [hbm] * 9,
         out_specs=(vmem,) * 8,
         scratch_shapes=[
-            pltpu.SMEM((1, slots), I32),
+            pltpu.SMEM((1, slots + 128), I32),
             pltpu.SMEM((1, slots), I32),
             pltpu.SMEM((1, slots), I32),
             pltpu.VMEM((1, slots), I32),
@@ -330,7 +332,7 @@
             pltpu.VMEM((slots, 128), BF16),
             jax.ShapeDtypeStruct((hours, members), F32),
         ),
-        in_specs=[smem, smem, smem] + [vmem] * 6,
+        in_specs=[smem, smem] + [vmem] * 6,
         out_specs=(vmem, vmem),
         scratch_shapes=[emis, slot_lines],
         compiler_params=limit,
@@ -352,18 +354,18 @@
 
     adjoint = pl.pallas_call(
         adjoint_kernel,
-        out_shape=pltpu.VMEM((rest, hours, members), BF16),
-        in_specs=[smem, smem, smem] + [vmem] * 4,
+        out_shape=pltpu.VMEM((plane, hours, members), BF16),
+        in_specs=[smem, smem] + [vmem] * 4,
         out_specs=vmem,
         scratch_shapes=[slot_lines, emis],
         compiler_params=limit,
         name="adjoint",
     )
 
-    def add_copies(copies, kind):
+    def add_copies(copies, count, kind):
         return pl.pallas_call(
             sum_kernel,
-            out_shape=pltpu.VMEM((plane, hours, members), kind),
+            out_shape=pltpu.VMEM((count, hours, members), kind),
             in_specs=[vmem],
             out_specs=vmem,
             compiler_params=pltpu.CompilerParams(vmem_limit_bytes=4 * 1024 * 1024),
@@ -376,7 +378,7 @@
             pltpu.VMEM((rest, hours, members), BF16),
             jax.ShapeDtypeStruct((share_tiles, 128), F32),
         ),
-        in_specs=[smem, smem, smem] + [vmem] * 5,
+        in_specs=[smem, smem] + [vmem] * 5,
         out_specs=(vmem, hbm),
         scratch_shapes=[slot_lines, emis, pltpu.SemaphoreType.DMA],
         compiler_params=limit,
@@ -385,9 +387,6 @@
 
     def by_slots(rows):
         return exchange(rows.reshape(devices, slots // devices, 128), CELLS).reshape(slots, 128)
-
-    def summed(copies, kind):
-        return exchange(add_copies(exchange(copies, REST), kind), PLANE)
 
     pinned = [
         pltpu.with_memory_space_constraint(array, pltpu.HBM)
@@ -397,23 +396,24 @@
         )
     ]
     partials, place, hour_rows, bg_buf, ens_buf, tile_buf, own_obs, own_var = first_forward(
-        position, tile_count, *pinned
+        tile_count, *pinned
     )
     named = exchange(partials, CELLS)
     (send,) = depart(first_departure_kernel, 3, (sent,), "first_departure")(named, own_obs, own_var)
     kept = (hour_rows, ens_buf, tile_buf)
-    copies = summed(adjoint(tile_block, place, tile_count, by_slots(send), *kept), F32)
+    copies = adjoint(tile_block, place, by_slots(send), *kept)
+    copies = exchange(add_copies(exchange(copies, PLANE), rest, F32), REST)
     partials, first_grad = next_forward(
-        tile_block, place, tile_count, control, copies, hour_rows, bg_buf, ens_buf, tile_buf
+        tile_block, place, control, copies, hour_rows, bg_buf, ens_buf, tile_buf
     )
     received = by_slots(partials)
     modelled, send = depart(next_departure_kernel, 4, (own, sent), "next_departure")(
         named, received, own_obs, own_var
     )
     copies, final = last_adjoint(
-        tile_block, place, tile_count, by_slots(send), *kept, modelled
-    )
-    copies = summed(copies, BF16)
+        tile_block, place, by_slots(send), *kept, modelled
+    )
+    copies = exchange(add_copies(exchange(copies, REST), plane, BF16), PLANE)
     updated = control - step_size * first_grad
     second_grad = updated + jnp.sum(copies.astype(F32), axis=0)
     return jnp.stack([first_grad, second_grad]), final.reshape(1, receptors // devices)

time: 115 us -> 115 us (level)
  blocking collectives: 94.6 us -> 92.1 us
  Pallas kernels: 17.9 us -> 20.3 us
    pallas_call x6, Pallas kernels: 17.2 us -> 19.7 us  [the longest x1 7.58 us: per_device(): first_forward(tile_count, *pinned)]
    all_to_all x8, blocking collectives: 94.6 us -> 92.1 us  [exchange(): return lax.all_to_all(value, axes, 0, 0, tiled=True)]
where the time goes in v6:
time: 115 us; the launch traced here: 114 us
  blocking collectives  92.1 us (80%)
  Pallas kernels  20.3 us (18%)
  between operations  1.34 us (1%)
    all_to_all x8, blocking collectives, exchange(): return lax.all_to_all(value, axes, 0, 0, tiled=True)  92.1 us
    pallas_call x1, Pallas kernels, per_device(): first_forward(tile_count, *pinned)  7.58 us
    pallas_call x1, Pallas kernels, per_device(): last_adjoint(tile_block, place, by_slots(send), *kept, modelled)  4.07 us
    pallas_call x1, Pallas kernels, per_device(): copies = adjoint(tile_block, place, by_slots(send), *kept)  4.07 us
    pallas_call x1, Pallas kernels, per_device(): next_forward(tile_block, place, control, copies, hour_rows, bg_buf, ens_b...  3.9 us

profile of v6, /device:TPU:0, one launch (start us, length us, event | category | flops | bytes accessed | tf_op | source)
XLA Modules:
  0.0 114.5 jit_solution(9002869785752767713)
XLA Ops:
  1.3 0.0 copy-start.1
  1.3 7.6 %first_forward.1 = (bf16[32,16,128]{2,1,0:T(8,128)(2,1)S(1)}, s32[1,384]{1,0:T(1,128)S(1)}, s32[256,128]{1,0:T(8,128)S(1)}, f32[8,24,2048]{2,1,0:T(8,128)S(1)}, ...) custom-call(s32[1,1]{1,0:T(1,128)S(6)} %copy.12.count, ...), custom_call_target="tpu_custom_call" | custom-call | tf_op jit(solution)/shard_map/first_forward/pallas_call | solution.py:398
  8.9 15.8 %all_to_all.40.received.named = bf16[32,16,128]{2,1,0:T(8,128)(2,1)S(1)} all-to-all(bf16[32,16,128]{2,1,0:T(8,128)(2,1)S(1)} %get-tuple-element.17), channel_id=1, replica_groups=mesh['cells_0'=4,'cells_1'=4,'cells_2'=2,'rcpt'=4] {'cells_0','cells_1',..., dimensions={0} | all-to-all | bytes 262144 | tf_op jit(solution)/shard_map/all_to_all | solution.py:267
  24.7 0.3 first_departure.1
  25.1 11.0 %all_to_all.41 = bf16[32,8,128]{2,1,0:T(8,128)(2,1)S(1)} all-to-all(bf16[32,8,128]{2,1,0:T(8,128)(2,1)S(1)} %bitcast.17), channel_id=1, replica_groups=mesh['cells_0'=4,'cells_1'=4,'cells_2'=2,'rcpt'=4] {'cells_0','cells_1',..., dimensions={0} | all-to-all | bytes 131072 | tf_op jit(solution)/shard_map/all_to_all | solution.py:267
  36.0 0.0 copy-done.1
  36.0 0.0 copy-start
  36.0 4.1 %adjoint.1 = bf16[16,24,256]{2,1,0:T(8,128)(2,1)S(1)} custom-call(s32[1,256]{1,0:T(1,128)S(1)} %copy-done.1, s32[1,384]{1,0:T(1,128)S(1)} %get-tuple-element.16.place, bf16[256,128]{1,0:T(8,128)(2,1)S(1)} %bitcast.15, s32[256,128]{1,0:T(8,128)S(1)} %get-tuple-element.20.hour_rows, bf16[8,256,2048]{2,1,0:T(8,128)(2,1)S(1)} %get-tuple-element.21.ens_buf, ...), custom_call_target="tpu_custom_call" | custom-call | tf_op jit(solution)/shard_map/adjoint/pallas_call | solution.py:404
  40.1 11.7 %all_to_all.42.copies = bf16[16,24,256]{2,1,0:T(8,128)(2,1)S(1)} all-to-all(bf16[16,24,256]{2,1,0:T(8,128)(2,1)S(1)} %adjoint.1), channel_id=1, replica_groups=mesh['cells_0'=4,'cells_1'=4,'cells_2'=2,'rcpt'=4] {'cells_0','cells_1'}, dimensions={0} | all-to-all | bytes 393216 | tf_op jit(solution)/shard_map/all_to_all | solution.py:267
  51.8 11.1 %all_to_all.43.copies = f32[8,24,256]{2,1,0:T(8,128)S(1)} all-to-all(f32[8,24,256]{2,1,0:T(8,128)S(1)} %add_copies.2), channel_id=1, replica_groups=mesh['cells_0'=4,'cells_1'=4,'cells_2'=2,'rcpt'=4] {'cells_2','rcpt'}, dimensions={0} | all-to-all | bytes 393216 | tf_op jit(solution)/shard_map/all_to_all | solution.py:267
  62.9 0.0 copy-done
  62.9 3.9 %next_forward.1 = (bf16[256,128]{1,0:T(8,128)(2,1)S(1)}, f32[24,256]{1,0:T(8,128)S(1)}) custom-call(s32[1,256]{1,0:T(1,128)S(1)} %copy-done.1, s32[1,384]{1,0:T(1,128)S(1)} %get-tuple-element.16.place, f32[24,256]{1,0:T(8,128)S(1)} %copy-done, f32[8,24,256]{2,1,0:T(8,128)S(1)} %all_to_all.43.copies, s32[256,128]{1,0:T(8,128)S(1)} %get-tuple-element.20.hour_rows, ...), custom_call_target="tpu_custom_call" | custom-call | tf_op jit(solution)/shard_map/next_forward/pallas_call | solution.py:406
  66.8 11.5 %all_to_all.44 = bf16[32,8,128]{2,1,0:T(8,128)(2,1)S(1)} all-to-all(bf16[32,8,128]{2,1,0:T(8,128)(2,1)S(1)} %bitcast.20), channel_id=1, replica_groups=mesh['cells_0'=4,'cells_1'=4,'cells_2'=2,'rcpt'=4] {'cells_0','cells_1',..., dimensions={0} | all-to-all | bytes 131072 | tf_op jit(solution)/shard_map/all_to_all | solution.py:267
  78.3 0.3 next_departure.1
  78.7 10.9 %all_to_all.45 = bf16[32,8,128]{2,1,0:T(8,128)(2,1)S(1)} all-to-all(bf16[32,8,128]{2,1,0:T(8,128)(2,1)S(1)} %bitcast.19), channel_id=1, replica_groups=mesh['cells_0'=4,'cells_1'=4,'cells_2'=2,'rcpt'=4] {'cells_0','cells_1',..., dimensions={0} | all-to-all | bytes 131072 | tf_op jit(solution)/shard_map/all_to_all | solution.py:267
  89.5 4.1 %last_adjoint.1 = (bf16[8,24,256]{2,1,0:T(8,128)(2,1)S(1)}, f32[64,128]{1,0:T(8,128)}) custom-call(s32[1,256]{1,0:T(1,128)S(1)} %copy-done.1, s32[1,384]{1,0:T(1,128)S(1)} %get-tuple-element.16.place, bf16[256,128]{1,0:T(8,128)(2,1)S(1)} %bitcast.14, s32[256,128]{1,0:T(8,128)S(1)} %get-tuple-element.20.hour_rows, ...), custom_call_target="tpu_custom_call" | custom-call | tf_op jit(solution)/shard_map/last_adjoint/pallas_call | solution.py:413
  93.6 7.8 %all_to_all.46.copies = bf16[8,24,256]{2,1,0:T(8,128)(2,1)S(1)} all-to-all(bf16[8,24,256]{2,1,0:T(8,128)(2,1)S(1)} %get-tuple-element.28), channel_id=1, replica_groups=mesh['cells_0'=4,'cells_1'=4,'cells_2'=2,'rcpt'=4] {'cells_2','rcpt'}, dimensions={0} | all-to-all | bytes 196608 | tf_op jit(solution)/shard_map/all_to_all | solution.py:267
  101.5 12.3 %all_to_all.47 = bf16[16,24,256]{2,1,0:T(8,128)(2,1)S(1)} all-to-all(bf16[16,24,256]{2,1,0:T(8,128)(2,1)S(1)} %add_copies.3), channel_id=1, replica_groups=mesh['cells_0'=4,'cells_1'=4,'cells_2'=2,'rcpt'=4] {'cells_0','cells_1'}, dimensions={0} | all-to-all | bytes 393216 | tf_op jit(solution)/shard_map/all_to_all | solution.py:267
  113.9 0.6 pad_maximum_fusion
  (4 shorter events, 0.1 us)
Async XLA Ops:
  1.3 34.7 %copy-start.1 = (s32[1,256]{1,0:T(1,128)S(1)}, s32[1,256]{1,0:T(1,128)}, u32[]{:S(2)}) copy-start(s32[1,256]{1,0:T(1,128)} %block.5) | copy-start | bytes 3076
  36.0 26.9 %copy-start = (f32[24,256]{1,0:T(8,128)S(1)}, f32[24,256]{1,0:T(8,128)}, u32[]{:S(2)}) copy-start(f32[24,256]{1,0:T(8,128)} %control.3) | copy-start | bytes 73732

commit v7 on v6

--- a/solution.py
+++ b/solution.py
@@ -67,8 +67,8 @@
 def first_forward_kernel(
     count, block_in, row_in, control, background, ensemble, footprint, hour,
     observed, inv_var,
-    out, place_out, hour_rows, bg_buf, ens_buf, tile_buf, own_observed, own_inv_var,
-    place, block, row, line_buf, control_buf, hour_buf, emis, partial, row_ids,
+    out, place, block, hour_rows, bg_buf, ens_buf, tile_buf, own_observed, own_inv_var,
+    place_buf, row, line_buf, control_buf, hour_buf, emis, partial, row_ids,
     ens_sem, bg_sem, tile_sem, hour_sem, place_sem, small_sem,
 ):
     slots = tile_buf.shape[0]
@@ -109,8 +109,8 @@
     small[0].wait()
     live = count[0, 0]
     places = slot_places(line_buf[...], share_tiles, slots // senders)
-    place_out[...] = jnp.concatenate([places, jnp.full((1, 128), live)], axis=1)
-    place_copy = pltpu.make_async_copy(place_out, place, place_sem)
+    place_buf[...] = jnp.concatenate([places, jnp.full((1, 128), live)], axis=1)
+    place_copy = pltpu.make_async_copy(place_buf, place, place_sem)
     place_copy.start()
     partial[...] = jnp.zeros_like(partial)
     row_ids[...] = jnp.zeros_like(row_ids)
@@ -296,7 +296,8 @@
         first_forward_kernel,
         out_shape=(
             pltpu.VMEM((devices, 16, 128), BF16),
-            pltpu.VMEM((1, slots + 128), I32),
+            pltpu.SMEM((1, slots + 128), I32),
+            pltpu.SMEM((1, slots), I32),
             pltpu.VMEM((slots, 128), I32),
             pltpu.VMEM((ENS_CHUNKS, hours, width), F32),
             pltpu.VMEM((ENS_CHUNKS, members, width), BF16),
@@ -305,10 +306,9 @@
             pltpu.VMEM((share_tiles, 128), F32),
         ),
         in_specs=[smem] + [hbm] * 9,
-        out_specs=(vmem,) * 8,
+        out_specs=(vmem, smem, smem) + (vmem,) * 6,
         scratch_shapes=[
-            pltpu.SMEM((1, slots + 128), I32),
-            pltpu.SMEM((1, slots), I32),
+            pltpu.VMEM((1, slots + 128), I32),
             pltpu.SMEM((1, slots), I32),
             pltpu.VMEM((1, slots), I32),
             pltpu.VMEM((hours, members), F32),
@@ -395,23 +395,23 @@
             hour_tab, obs_tab, var_tab,
         )
     ]
-    partials, place, hour_rows, bg_buf, ens_buf, tile_buf, own_obs, own_var = first_forward(
+    partials, place, block, hour_rows, bg_buf, ens_buf, tile_buf, own_obs, own_var = first_forward(
         tile_count, *pinned
     )
     named = exchange(partials, CELLS)
     (send,) = depart(first_departure_kernel, 3, (sent,), "first_departure")(named, own_obs, own_var)
     kept = (hour_rows, ens_buf, tile_buf)
-    copies = adjoint(tile_block, place, by_slots(send), *kept)
+    copies = adjoint(block, place, by_slots(send), *kept)
     copies = exchange(add_copies(exchange(copies, PLANE), rest, F32), REST)
     partials, first_grad = next_forward(
-        tile_block, place, control, copies, hour_rows, bg_buf, ens_buf, tile_buf
+        block, place, control, copies, hour_rows, bg_buf, ens_buf, tile_buf
     )
     received = by_slots(partials)
     modelled, send = depart(next_departure_kernel, 4, (own, sent), "next_departure")(
         named, received, own_obs, own_var
     )
     copies, final = last_adjoint(
-        tile_block, place, by_slots(send), *kept, modelled
+        block, place, by_slots(send), *kept, modelled
     )
     copies = exchange(add_copies(exchange(copies, REST), plane, BF16), PLANE)
     updated = control - step_size * first_grad

time: 115 us -> 114 us (level); the launches traced: 114 us -> 112 us
  Pallas kernels: 20.3 us -> 18.6 us
    pallas_call x3, Pallas kernels: 12 us -> 10.3 us  [the longest x1 3.51 us: per_device(): copies, final = last_adjoint(block, place, by_slots(send), *kept, modelled)]
where the time goes in v7:
time: 114 us; the launch traced here: 112 us
  blocking collectives  91.6 us (80%)
  Pallas kernels  18.6 us (16%)
  between operations  1.34 us (1%)
    all_to_all x8, blocking collectives, exchange(): return lax.all_to_all(value, axes, 0, 0, tiled=True)  91.6 us
    pallas_call x1, Pallas kernels, per_device(): first_forward(tile_count, *pinned)  7.58 us
    pallas_call x1, Pallas kernels, per_device(): copies, final = last_adjoint(block, place, by_slots(send), *kept, modelled)  3.51 us
    pallas_call x1, Pallas kernels, per_device(): copies = adjoint(block, place, by_slots(send), *kept)  3.51 us
    pallas_call x1, Pallas kernels, per_device(): next_forward(block, place, control, copies, hour_rows, bg_buf, ens_buf, t...  3.29 us

profile of v7, /device:TPU:0, one launch (start us, length us, event | category | flops | bytes accessed | tf_op | source)
XLA Modules:
  0.0 112.3 jit_solution(8926820383772370334)
XLA Ops:
  1.3 7.6 %first_forward.1 = (bf16[32,16,128]{2,1,0:T(8,128)(2,1)S(1)}, s32[1,384]{1,0:T(1,128)S(4)}, s32[1,256]{1,0:T(1,128)S(4)}, s32[256,128]{1,0:T(8,128)S(1)}, f32[8,...) custom-call(s32[1,1]{1,0:T(1,128)S(6)} %copy.12.count, ...), custom_call_target="tpu_custom_call" | custom-call | tf_op jit(solution)/shard_map/first_forward/pallas_call | solution.py:398
  8.9 15.9 %all_to_all.40.received.named = bf16[32,16,128]{2,1,0:T(8,128)(2,1)S(1)} all-to-all(bf16[32,16,128]{2,1,0:T(8,128)(2,1)S(1)} %get-tuple-element.19), channel_id=1, replica_groups=mesh['cells_0'=4,'cells_1'=4,'cells_2'=2,'rcpt'=4] {'cells_0','cells_1',..., dimensions={0} | all-to-all | bytes 262144 | tf_op jit(solution)/shard_map/all_to_all | solution.py:267
  24.7 0.3 first_departure.1
  25.1 11.0 %all_to_all.41 = bf16[32,8,128]{2,1,0:T(8,128)(2,1)S(1)} all-to-all(bf16[32,8,128]{2,1,0:T(8,128)(2,1)S(1)} %bitcast.17), channel_id=1, replica_groups=mesh['cells_0'=4,'cells_1'=4,'cells_2'=2,'rcpt'=4] {'cells_0','cells_1',..., dimensions={0} | all-to-all | bytes 131072 | tf_op jit(solution)/shard_map/all_to_all | solution.py:267
  36.0 0.0 copy-start
  36.0 3.5 %adjoint.1 = bf16[16,24,256]{2,1,0:T(8,128)(2,1)S(1)} custom-call(s32[1,256]{1,0:T(1,128)S(4)} %get-tuple-element.17.block, s32[1,384]{1,0:T(1,128)S(4)} %get-tuple-element.18.place, bf16[256,128]{1,0:T(8,128)(2,1)S(1)} %bitcast.15, s32[256,128]{1,0:T(8,128)S(1)} %get-tuple-element.22.hour_rows, bf16[8,256,2048]{2,1,0:T(8,128)(2,1)S(1)} %get-tuple-element.23.ens_buf, ...), custom_call_target="tpu_custom_call" | custom-call | tf_op jit(solution)/shard_map/adjoint/pallas_call | solution.py:404
  39.5 11.8 %all_to_all.42.copies = bf16[16,24,256]{2,1,0:T(8,128)(2,1)S(1)} all-to-all(bf16[16,24,256]{2,1,0:T(8,128)(2,1)S(1)} %adjoint.1), channel_id=1, replica_groups=mesh['cells_0'=4,'cells_1'=4,'cells_2'=2,'rcpt'=4] {'cells_0','cells_1'}, dimensions={0} | all-to-all | bytes 393216 | tf_op jit(solution)/shard_map/all_to_all | solution.py:267
  51.4 10.8 %all_to_all.43.copies = f32[8,24,256]{2,1,0:T(8,128)S(1)} all-to-all(f32[8,24,256]{2,1,0:T(8,128)S(1)} %add_copies.2), channel_id=1, replica_groups=mesh['cells_0'=4,'cells_1'=4,'cells_2'=2,'rcpt'=4] {'cells_2','rcpt'}, dimensions={0} | all-to-all | bytes 393216 | tf_op jit(solution)/shard_map/all_to_all | solution.py:267
  62.2 0.0 copy-done
  62.2 3.3 %next_forward.1 = (bf16[256,128]{1,0:T(8,128)(2,1)S(1)}, f32[24,256]{1,0:T(8,128)S(1)}) custom-call(s32[1,256]{1,0:T(1,128)S(4)} %get-tuple-element.17.block, s32[1,384]{1,0:T(1,128)S(4)} %get-tuple-element.18.place, f32[24,256]{1,0:T(8,128)S(1)} %copy-done, f32[8,24,256]{2,1,0:T(8,128)S(1)} %all_to_all.43.copies, ...), custom_call_target="tpu_custom_call" | custom-call | tf_op jit(solution)/shard_map/next_forward/pallas_call | solution.py:406
  65.5 11.3 %all_to_all.44 = bf16[32,8,128]{2,1,0:T(8,128)(2,1)S(1)} all-to-all(bf16[32,8,128]{2,1,0:T(8,128)(2,1)S(1)} %bitcast.20), channel_id=1, replica_groups=mesh['cells_0'=4,'cells_1'=4,'cells_2'=2,'rcpt'=4] {'cells_0','cells_1',..., dimensions={0} | all-to-all | bytes 131072 | tf_op jit(solution)/shard_map/all_to_all | solution.py:267
  76.8 0.3 next_departure.1
  77.1 10.9 %all_to_all.45 = bf16[32,8,128]{2,1,0:T(8,128)(2,1)S(1)} all-to-all(bf16[32,8,128]{2,1,0:T(8,128)(2,1)S(1)} %bitcast.19), channel_id=1, replica_groups=mesh['cells_0'=4,'cells_1'=4,'cells_2'=2,'rcpt'=4] {'cells_0','cells_1',..., dimensions={0} | all-to-all | bytes 131072 | tf_op jit(solution)/shard_map/all_to_all | solution.py:267
  88.0 3.5 %last_adjoint.1 = (bf16[8,24,256]{2,1,0:T(8,128)(2,1)S(1)}, f32[64,128]{1,0:T(8,128)}) custom-call(s32[1,256]{1,0:T(1,128)S(4)} %get-tuple-element.17.block, s32[1,384]{1,0:T(1,128)S(4)} %get-tuple-element.18.place, bf16[256,128]{1,0:T(8,128)(2,1)S(1)} %bitcast.14, s32[256,128]{1,0:T(8,128)S(1)} %get-tuple-element.22.hour_rows, ...), custom_call_target="tpu_custom_call" | custom-call | tf_op jit(solution)/shard_map/last_adjoint/pallas_call | solution.py:413
  91.5 8.1 %all_to_all.46.copies = bf16[8,24,256]{2,1,0:T(8,128)(2,1)S(1)} all-to-all(bf16[8,24,256]{2,1,0:T(8,128)(2,1)S(1)} %get-tuple-element.30), channel_id=1, replica_groups=mesh['cells_0'=4,'cells_1'=4,'cells_2'=2,'rcpt'=4] {'cells_2','rcpt'}, dimensions={0} | all-to-all | bytes 196608 | tf_op jit(solution)/shard_map/all_to_all | solution.py:267
  99.6 12.0 %all_to_all.47 = bf16[16,24,256]{2,1,0:T(8,128)(2,1)S(1)} all-to-all(bf16[16,24,256]{2,1,0:T(8,128)(2,1)S(1)} %add_copies.3), channel_id=1, replica_groups=mesh['cells_0'=4,'cells_1'=4,'cells_2'=2,'rcpt'=4] {'cells_0','cells_1'}, dimensions={0} | all-to-all | bytes 393216 | tf_op jit(solution)/shard_map/all_to_all | solution.py:267
  111.6 0.6 pad_maximum_fusion
  (4 shorter events, 0.1 us)
Async XLA Ops:
  36.0 26.2 %copy-start = (f32[24,256]{1,0:T(8,128)S(1)}, f32[24,256]{1,0:T(8,128)}, u32[]{:S(2)}) copy-start(f32[24,256]{1,0:T(8,128)} %control.3) | copy-start | bytes 73732

commit v8 on v7

--- a/solution.py
+++ b/solution.py
@@ -16,7 +16,8 @@
 HOURS_AFTER = 2
 TILES_AT_ONCE = 2
 TILE_CHUNK = 32
-UNROLL = 64
+FIRST_UNROLL = 64
+UNROLL = 128
 NAMES = 8
 F32 = jnp.float32
 BF16 = jnp.bfloat16
@@ -150,11 +151,17 @@
     small[3].wait()
 
     def work(g):
-        for part in range(UNROLL // TILE_CHUNK):
-            tile_copy(g * (UNROLL // TILE_CHUNK) + part).wait()
-        forward_group(g, UNROLL, block, place, tile_buf, hour_rows, emis, partial)
-
-    live_groups(live, UNROLL, work)
+        for part in range(FIRST_UNROLL // TILE_CHUNK):
+            tile_copy(g * (FIRST_UNROLL // TILE_CHUNK) + part).wait()
+        forward_group(g, FIRST_UNROLL, block, place, tile_buf, hour_rows, emis, partial)
+
+    live_groups(live, FIRST_UNROLL, work)
+    taken = ((live + FIRST_UNROLL - 1) // FIRST_UNROLL) * FIRST_UNROLL
+    for c in range(chunks):
+        @pl.when((c * TILE_CHUNK >= taken) & (c * TILE_CHUNK < filled))
+        def _():
+            tile_copy(c).wait()
+
     small[4].wait()
     small[5].wait()
     parts = [part[...].reshape(senders, slots // senders, 128) for part in (partial, row_ids)]

time: 114 us -> 112 us (0.982); the launches traced: 112 us -> 113 us
  blocking collectives: 91.6 us -> 93.5 us
  Pallas kernels: 18.6 us -> 17.3 us
    all_to_all x8, blocking collectives: 91.6 us -> 93.5 us  [exchange(): return lax.all_to_all(value, axes, 0, 0, tiled=True)]
where the time goes in v8:
time: 112 us; the launch traced here: 113 us
  blocking collectives  93.5 us (83%)
  Pallas kernels  17.3 us (15%)
  between operations  1.34 us (1%)
    all_to_all x8, blocking collectives, exchange(): return lax.all_to_all(value, axes, 0, 0, tiled=True)  93.5 us
    pallas_call x1, Pallas kernels, per_device(): first_forward(tile_count, *pinned)  6.71 us
    pallas_call x1, Pallas kernels, per_device(): copies, final = last_adjoint(block, place, by_slots(send), *kept, modelled)  3.37 us
    pallas_call x1, Pallas kernels, per_device(): copies = adjoint(block, place, by_slots(send), *kept)  3.35 us
    pallas_call x1, Pallas kernels, per_device(): next_forward(block, place, control, copies, hour_rows, bg_buf, ens_buf, t...  3.17 us

profile of v8, /device:TPU:0, one launch (start us, length us, event | category | flops | bytes accessed | tf_op | source)
XLA Modules:
  0.0 112.9 jit_solution(1940636738079247810)
XLA Ops:
  1.3 6.7 %first_forward.1 = (bf16[32,16,128]{2,1,0:T(8,128)(2,1)S(1)}, s32[1,384]{1,0:T(1,128)S(4)}, s32[1,256]{1,0:T(1,128)S(4)}, s32[256,128]{1,0:T(8,128)S(1)}, f32[8,...) custom-call(s32[1,1]{1,0:T(1,128)S(6)} %copy.12.count, ...), custom_call_target="tpu_custom_call" | custom-call | tf_op jit(solution)/shard_map/first_forward/pallas_call | solution.py:405
  8.0 18.5 %all_to_all.40.received.named = bf16[32,16,128]{2,1,0:T(8,128)(2,1)S(1)} all-to-all(bf16[32,16,128]{2,1,0:T(8,128)(2,1)S(1)} %get-tuple-element.19), channel_id=1, replica_groups=mesh['cells_0'=4,'cells_1'=4,'cells_2'=2,'rcpt'=4] {'cells_0','cells_1',..., dimensions={0} | all-to-all | bytes 262144 | tf_op jit(solution)/shard_map/all_to_all | solution.py:274
  26.5 0.3 first_departure.1
  26.8 11.0 %all_to_all.41 = bf16[32,8,128]{2,1,0:T(8,128)(2,1)S(1)} all-to-all(bf16[32,8,128]{2,1,0:T(8,128)(2,1)S(1)} %bitcast.17), channel_id=1, replica_groups=mesh['cells_0'=4,'cells_1'=4,'cells_2'=2,'rcpt'=4] {'cells_0','cells_1',..., dimensions={0} | all-to-all | bytes 131072 | tf_op jit(solution)/shard_map/all_to_all | solution.py:274
  37.8 0.0 copy-start
  37.8 3.4 %adjoint.1 = bf16[16,24,256]{2,1,0:T(8,128)(2,1)S(1)} custom-call(s32[1,256]{1,0:T(1,128)S(4)} %get-tuple-element.17.block, s32[1,384]{1,0:T(1,128)S(4)} %get-tuple-element.18.place, bf16[256,128]{1,0:T(8,128)(2,1)S(1)} %bitcast.15, s32[256,128]{1,0:T(8,128)S(1)} %get-tuple-element.22.hour_rows, bf16[8,256,2048]{2,1,0:T(8,128)(2,1)S(1)} %get-tuple-element.23.ens_buf, ...), custom_call_target="tpu_custom_call" | custom-call | tf_op jit(solution)/shard_map/adjoint/pallas_call | solution.py:411
  41.1 12.4 %all_to_all.42.copies = bf16[16,24,256]{2,1,0:T(8,128)(2,1)S(1)} all-to-all(bf16[16,24,256]{2,1,0:T(8,128)(2,1)S(1)} %adjoint.1), channel_id=1, replica_groups=mesh['cells_0'=4,'cells_1'=4,'cells_2'=2,'rcpt'=4] {'cells_0','cells_1'}, dimensions={0} | all-to-all | bytes 393216 | tf_op jit(solution)/shard_map/all_to_all | solution.py:274
  53.5 8.6 %all_to_all.43.copies = f32[8,24,256]{2,1,0:T(8,128)S(1)} all-to-all(f32[8,24,256]{2,1,0:T(8,128)S(1)} %add_copies.2), channel_id=1, replica_groups=mesh['cells_0'=4,'cells_1'=4,'cells_2'=2,'rcpt'=4] {'cells_2','rcpt'}, dimensions={0} | all-to-all | bytes 393216 | tf_op jit(solution)/shard_map/all_to_all | solution.py:274
  62.1 0.0 copy-done
  62.1 3.2 %next_forward.1 = (bf16[256,128]{1,0:T(8,128)(2,1)S(1)}, f32[24,256]{1,0:T(8,128)S(1)}) custom-call(s32[1,256]{1,0:T(1,128)S(4)} %get-tuple-element.17.block, s32[1,384]{1,0:T(1,128)S(4)} %get-tuple-element.18.place, f32[24,256]{1,0:T(8,128)S(1)} %copy-done, f32[8,24,256]{2,1,0:T(8,128)S(1)} %all_to_all.43.copies, ...), custom_call_target="tpu_custom_call" | custom-call | tf_op jit(solution)/shard_map/next_forward/pallas_call | solution.py:413
  65.3 12.1 %all_to_all.44 = bf16[32,8,128]{2,1,0:T(8,128)(2,1)S(1)} all-to-all(bf16[32,8,128]{2,1,0:T(8,128)(2,1)S(1)} %bitcast.20), channel_id=1, replica_groups=mesh['cells_0'=4,'cells_1'=4,'cells_2'=2,'rcpt'=4] {'cells_0','cells_1',..., dimensions={0} | all-to-all | bytes 131072 | tf_op jit(solution)/shard_map/all_to_all | solution.py:274
  77.4 0.3 next_departure.1
  77.8 10.9 %all_to_all.45 = bf16[32,8,128]{2,1,0:T(8,128)(2,1)S(1)} all-to-all(bf16[32,8,128]{2,1,0:T(8,128)(2,1)S(1)} %bitcast.19), channel_id=1, replica_groups=mesh['cells_0'=4,'cells_1'=4,'cells_2'=2,'rcpt'=4] {'cells_0','cells_1',..., dimensions={0} | all-to-all | bytes 131072 | tf_op jit(solution)/shard_map/all_to_all | solution.py:274
  88.6 3.4 %last_adjoint.1 = (bf16[8,24,256]{2,1,0:T(8,128)(2,1)S(1)}, f32[64,128]{1,0:T(8,128)}) custom-call(s32[1,256]{1,0:T(1,128)S(4)} %get-tuple-element.17.block, s32[1,384]{1,0:T(1,128)S(4)} %get-tuple-element.18.place, bf16[256,128]{1,0:T(8,128)(2,1)S(1)} %bitcast.14, s32[256,128]{1,0:T(8,128)S(1)} %get-tuple-element.22.hour_rows, ...), custom_call_target="tpu_custom_call" | custom-call | tf_op jit(solution)/shard_map/last_adjoint/pallas_call | solution.py:420
  92.0 7.8 %all_to_all.46.copies = bf16[8,24,256]{2,1,0:T(8,128)(2,1)S(1)} all-to-all(bf16[8,24,256]{2,1,0:T(8,128)(2,1)S(1)} %get-tuple-element.30), channel_id=1, replica_groups=mesh['cells_0'=4,'cells_1'=4,'cells_2'=2,'rcpt'=4] {'cells_2','rcpt'}, dimensions={0} | all-to-all | bytes 196608 | tf_op jit(solution)/shard_map/all_to_all | solution.py:274
  99.8 12.4 %all_to_all.47 = bf16[16,24,256]{2,1,0:T(8,128)(2,1)S(1)} all-to-all(bf16[16,24,256]{2,1,0:T(8,128)(2,1)S(1)} %add_copies.3), channel_id=1, replica_groups=mesh['cells_0'=4,'cells_1'=4,'cells_2'=2,'rcpt'=4] {'cells_0','cells_1'}, dimensions={0} | all-to-all | bytes 393216 | tf_op jit(solution)/shard_map/all_to_all | solution.py:274
  112.2 0.6 pad_maximum_fusion
  (4 shorter events, 0.1 us)
Async XLA Ops:
  37.8 24.4 %copy-start = (f32[24,256]{1,0:T(8,128)S(1)}, f32[24,256]{1,0:T(8,128)}, u32[]{:S(2)}) copy-start(f32[24,256]{1,0:T(8,128)} %control.3) | copy-start | bytes 73732

commit v9 on v8

--- a/solution.py
+++ b/solution.py
@@ -115,7 +115,8 @@
     place_copy.start()
     partial[...] = jnp.zeros_like(partial)
     row_ids[...] = jnp.zeros_like(row_ids)
-    filled = ((live + UNROLL - 1) // UNROLL) * UNROLL
+    filled = ((live + FIRST_UNROLL - 1) // FIRST_UNROLL) * FIRST_UNROLL
+    named = ((live + UNROLL - 1) // UNROLL) * UNROLL
     small[1].wait()
     scaled = control_buf[...].astype(BF16)
 
@@ -145,7 +146,7 @@
             small[2].wait()
             place_copy.wait()
             hour_copy.wait()
-            lax.fori_loop(0, filled // NAMES, name_slots, 0)
+            lax.fori_loop(0, named // NAMES, name_slots, 0)
     small[4].start()
     small[5].start()
     small[3].wait()
@@ -156,12 +157,6 @@
         forward_group(g, FIRST_UNROLL, block, place, tile_buf, hour_rows, emis, partial)
 
     live_groups(live, FIRST_UNROLL, work)
-    taken = ((live + FIRST_UNROLL - 1) // FIRST_UNROLL) * FIRST_UNROLL
-    for c in range(chunks):
-        @pl.when((c * TILE_CHUNK >= taken) & (c * TILE_CHUNK < filled))
-        def _():
-            tile_copy(c).wait()
-
     small[4].wait()
     small[5].wait()
     parts = [part[...].reshape(senders, slots // senders, 128) for part in (partial, row_ids)]
@@ -234,7 +229,9 @@
                 chosen = hour_line == these[u + v : u + v + 1, :]
                 weighted.append(jnp.where(chosen, dep_buf[pl.ds(place[0, s + v], 1), :], 0.0))
             pair = jnp.concatenate(weighted, axis=0).astype(BF16)
-            both = jnp.concatenate([tile_buf[s], tile_buf[s + 1]], axis=1)
+            loaded = jnp.minimum(s, live - 1)
+            beside = jnp.minimum(s + 1, live - 1)
+            both = jnp.concatenate([tile_buf[loaded], tile_buf[beside]], axis=1)
             every = jnp.dot(pair, both, preferred_element_type=F32)
             adjoint[block[0, s]] += every[0:hours, 0:128]
             adjoint[block[0, s + 1]] += every[hours : 2 * hours, 128:256]

time: 112 us -> 113 us (level)
  no operation moved by 1% of the time
where the time goes in v9:
time: 113 us
  blocking collectives  93.1 us (82%)
  Pallas kernels  18.2 us (16%)
  between operations  1.34 us (1%)
    all_to_all x8, blocking collectives, exchange(): return lax.all_to_all(value, axes, 0, 0, tiled=True)  93.1 us
    pallas_call x1, Pallas kernels, per_device(): first_forward(tile_count, *pinned)  7.58 us
    pallas_call x1, Pallas kernels, per_device(): copies, final = last_adjoint(block, place, by_slots(send), *kept, modelled)  3.37 us
    pallas_call x1, Pallas kernels, per_device(): copies = adjoint(block, place, by_slots(send), *kept)  3.35 us
    pallas_call x1, Pallas kernels, per_device(): next_forward(block, place, control, copies, hour_rows, bg_buf, ens_buf, t...  3.18 us

profile of v9, /device:TPU:0, one launch (start us, length us, event | category | flops | bytes accessed | tf_op | source)
XLA Modules:
  0.0 113.3 jit_solution(12298718750620015264)
XLA Ops:
  1.3 7.6 %first_forward.1 = (bf16[32,16,128]{2,1,0:T(8,128)(2,1)S(1)}, s32[1,384]{1,0:T(1,128)S(4)}, s32[1,256]{1,0:T(1,128)S(4)}, s32[256,128]{1,0:T(8,128)S(1)}, f32[8,...) custom-call(s32[1,1]{1,0:T(1,128)S(6)} %copy.12.count, ...), custom_call_target="tpu_custom_call" | custom-call | tf_op jit(solution)/shard_map/first_forward/pallas_call | solution.py:402
  8.9 15.8 %all_to_all.40.received.named = bf16[32,16,128]{2,1,0:T(8,128)(2,1)S(1)} all-to-all(bf16[32,16,128]{2,1,0:T(8,128)(2,1)S(1)} %get-tuple-element.19), channel_id=1, replica_groups=mesh['cells_0'=4,'cells_1'=4,'cells_2'=2,'rcpt'=4] {'cells_0','cells_1',..., dimensions={0} | all-to-all | bytes 262144 | tf_op jit(solution)/shard_map/all_to_all | solution.py:271
  24.7 0.3 first_departure.1
  25.1 11.0 %all_to_all.41 = bf16[32,8,128]{2,1,0:T(8,128)(2,1)S(1)} all-to-all(bf16[32,8,128]{2,1,0:T(8,128)(2,1)S(1)} %bitcast.17), channel_id=1, replica_groups=mesh['cells_0'=4,'cells_1'=4,'cells_2'=2,'rcpt'=4] {'cells_0','cells_1',..., dimensions={0} | all-to-all | bytes 131072 | tf_op jit(solution)/shard_map/all_to_all | solution.py:271
  36.0 0.0 copy-start
  36.0 3.4 %adjoint.1 = bf16[16,24,256]{2,1,0:T(8,128)(2,1)S(1)} custom-call(s32[1,256]{1,0:T(1,128)S(4)} %get-tuple-element.17.block, s32[1,384]{1,0:T(1,128)S(4)} %get-tuple-element.18.place, bf16[256,128]{1,0:T(8,128)(2,1)S(1)} %bitcast.15, s32[256,128]{1,0:T(8,128)S(1)} %get-tuple-element.22.hour_rows, bf16[8,256,2048]{2,1,0:T(8,128)(2,1)S(1)} %get-tuple-element.23.ens_buf, ...), custom_call_target="tpu_custom_call" | custom-call | tf_op jit(solution)/shard_map/adjoint/pallas_call | solution.py:408
  39.4 11.5 %all_to_all.42.copies = bf16[16,24,256]{2,1,0:T(8,128)(2,1)S(1)} all-to-all(bf16[16,24,256]{2,1,0:T(8,128)(2,1)S(1)} %adjoint.1), channel_id=1, replica_groups=mesh['cells_0'=4,'cells_1'=4,'cells_2'=2,'rcpt'=4] {'cells_0','cells_1'}, dimensions={0} | all-to-all | bytes 393216 | tf_op jit(solution)/shard_map/all_to_all | solution.py:271
  50.9 12.4 %all_to_all.43.copies = f32[8,24,256]{2,1,0:T(8,128)S(1)} all-to-all(f32[8,24,256]{2,1,0:T(8,128)S(1)} %add_copies.2), channel_id=1, replica_groups=mesh['cells_0'=4,'cells_1'=4,'cells_2'=2,'rcpt'=4] {'cells_2','rcpt'}, dimensions={0} | all-to-all | bytes 393216 | tf_op jit(solution)/shard_map/all_to_all | solution.py:271
  63.3 0.0 copy-done
  63.3 3.2 %next_forward.1 = (bf16[256,128]{1,0:T(8,128)(2,1)S(1)}, f32[24,256]{1,0:T(8,128)S(1)}) custom-call(s32[1,256]{1,0:T(1,128)S(4)} %get-tuple-element.17.block, s32[1,384]{1,0:T(1,128)S(4)} %get-tuple-element.18.place, f32[24,256]{1,0:T(8,128)S(1)} %copy-done, f32[8,24,256]{2,1,0:T(8,128)S(1)} %all_to_all.43.copies, ...), custom_call_target="tpu_custom_call" | custom-call | tf_op jit(solution)/shard_map/next_forward/pallas_call | solution.py:410
  66.5 11.4 %all_to_all.44 = bf16[32,8,128]{2,1,0:T(8,128)(2,1)S(1)} all-to-all(bf16[32,8,128]{2,1,0:T(8,128)(2,1)S(1)} %bitcast.20), channel_id=1, replica_groups=mesh['cells_0'=4,'cells_1'=4,'cells_2'=2,'rcpt'=4] {'cells_0','cells_1',..., dimensions={0} | all-to-all | bytes 131072 | tf_op jit(solution)/shard_map/all_to_all | solution.py:271
  77.9 0.3 next_departure.1
  78.2 10.9 %all_to_all.45 = bf16[32,8,128]{2,1,0:T(8,128)(2,1)S(1)} all-to-all(bf16[32,8,128]{2,1,0:T(8,128)(2,1)S(1)} %bitcast.19), channel_id=1, replica_groups=mesh['cells_0'=4,'cells_1'=4,'cells_2'=2,'rcpt'=4] {'cells_0','cells_1',..., dimensions={0} | all-to-all | bytes 131072 | tf_op jit(solution)/shard_map/all_to_all | solution.py:271
  89.1 3.4 %last_adjoint.1 = (bf16[8,24,256]{2,1,0:T(8,128)(2,1)S(1)}, f32[64,128]{1,0:T(8,128)}) custom-call(s32[1,256]{1,0:T(1,128)S(4)} %get-tuple-element.17.block, s32[1,384]{1,0:T(1,128)S(4)} %get-tuple-element.18.place, bf16[256,128]{1,0:T(8,128)(2,1)S(1)} %bitcast.14, s32[256,128]{1,0:T(8,128)S(1)} %get-tuple-element.22.hour_rows, ...), custom_call_target="tpu_custom_call" | custom-call | tf_op jit(solution)/shard_map/last_adjoint/pallas_call | solution.py:417
  92.5 8.3 %all_to_all.46.copies = bf16[8,24,256]{2,1,0:T(8,128)(2,1)S(1)} all-to-all(bf16[8,24,256]{2,1,0:T(8,128)(2,1)S(1)} %get-tuple-element.30), channel_id=1, replica_groups=mesh['cells_0'=4,'cells_1'=4,'cells_2'=2,'rcpt'=4] {'cells_2','rcpt'}, dimensions={0} | all-to-all | bytes 196608 | tf_op jit(solution)/shard_map/all_to_all | solution.py:271
  100.8 11.8 %all_to_all.47 = bf16[16,24,256]{2,1,0:T(8,128)(2,1)S(1)} all-to-all(bf16[16,24,256]{2,1,0:T(8,128)(2,1)S(1)} %add_copies.3), channel_id=1, replica_groups=mesh['cells_0'=4,'cells_1'=4,'cells_2'=2,'rcpt'=4] {'cells_0','cells_1'}, dimensions={0} | all-to-all | bytes 393216 | tf_op jit(solution)/shard_map/all_to_all | solution.py:271
  112.7 0.6 pad_maximum_fusion
  (4 shorter events, 0.1 us)
Async XLA Ops:
  36.0 27.3 %copy-start = (f32[24,256]{1,0:T(8,128)S(1)}, f32[24,256]{1,0:T(8,128)}, u32[]{:S(2)}) copy-start(f32[24,256]{1,0:T(8,128)} %control.3) | copy-start | bytes 73732

commit v10 on v9

--- a/solution.py
+++ b/solution.py
@@ -12,9 +12,9 @@
 
 step_size = 0.5
 
-ENS_CHUNKS = 8
-HOURS_AFTER = 2
-TILES_AT_ONCE = 2
+ENS_CHUNKS = 16
+HOURS_AFTER = 5
+TILES_AT_ONCE = 1
 TILE_CHUNK = 32
 FIRST_UNROLL = 64
 UNROLL = 128

time: 113 us -> 115 us (1.018)
  Pallas kernels: 18.2 us -> 25.3 us
  blocking collectives: 93.1 us -> 87.1 us
    all_to_all x8, blocking collectives: 93.1 us -> 87.1 us  [exchange(): return lax.all_to_all(value, axes, 0, 0, tiled=True)]
    pallas_call x1, Pallas kernels: 7.58 us -> 11.3 us  [per_device(): first_forward(tile_count, *pinned)]
    pallas_call x1, Pallas kernels: 3.18 us -> 4.78 us  [per_device(): next_forward(block, place, control, copies, hour_rows, bg_buf, ens_buf, t...]
where the time goes in v10:
time: 115 us; the launch traced here: 114 us
  blocking collectives  87.1 us (76%)
  Pallas kernels  25.3 us (22%)
  between operations  1.34 us (1%)
    all_to_all x8, blocking collectives, exchange(): return lax.all_to_all(value, axes, 0, 0, tiled=True)  87.1 us
    pallas_call x1, Pallas kernels, per_device(): first_forward(tile_count, *pinned)  11.3 us
    pallas_call x1, Pallas kernels, per_device(): next_forward(block, place, control, copies, hour_rows, bg_buf, ens_buf, t...  4.78 us
    pallas_call x1, Pallas kernels, per_device(): copies, final = last_adjoint(block, place, by_slots(send), *kept, modelled)  4.26 us
    pallas_call x1, Pallas kernels, per_device(): copies = adjoint(block, place, by_slots(send), *kept)  4.25 us

profile of v10, /device:TPU:0, one launch (start us, length us, event | category | flops | bytes accessed | tf_op | source)
XLA Modules:
  0.0 114.4 jit_solution(15580003128351317648)
XLA Ops:
  1.3 11.3 %first_forward.1 = (bf16[32,16,128]{2,1,0:T(8,128)(2,1)S(1)}, s32[1,384]{1,0:T(1,128)S(4)}, s32[1,256]{1,0:T(1,128)S(4)}, s32[256,128]{1,0:T(8,128)S(1)}, f32[16...) custom-call(s32[1,1]{1,0:T(1,128)S(6)} %copy.12.count, ...), custom_call_target="tpu_custom_call" | custom-call | tf_op jit(solution)/shard_map/first_forward/pallas_call | solution.py:402
  12.6 13.5 %all_to_all.40.received.named = bf16[32,16,128]{2,1,0:T(8,128)(2,1)S(1)} all-to-all(bf16[32,16,128]{2,1,0:T(8,128)(2,1)S(1)} %get-tuple-element.19), channel_id=1, replica_groups=mesh['cells_0'=4,'cells_1'=4,'cells_2'=2,'rcpt'=4] {'cells_0','cells_1',..., dimensions={0} | all-to-all | bytes 262144 | tf_op jit(solution)/shard_map/all_to_all | solution.py:271
  26.1 0.3 first_departure.1
  26.4 11.0 %all_to_all.41 = bf16[32,8,128]{2,1,0:T(8,128)(2,1)S(1)} all-to-all(bf16[32,8,128]{2,1,0:T(8,128)(2,1)S(1)} %bitcast.17), channel_id=1, replica_groups=mesh['cells_0'=4,'cells_1'=4,'cells_2'=2,'rcpt'=4] {'cells_0','cells_1',..., dimensions={0} | all-to-all | bytes 131072 | tf_op jit(solution)/shard_map/all_to_all | solution.py:271
  37.4 0.0 copy-start
  37.4 4.2 %adjoint.1 = bf16[16,24,256]{2,1,0:T(8,128)(2,1)S(1)} custom-call(s32[1,256]{1,0:T(1,128)S(4)} %get-tuple-element.17.block, s32[1,384]{1,0:T(1,128)S(4)} %get-tuple-element.18.place, bf16[256,128]{1,0:T(8,128)(2,1)S(1)} %bitcast.15, s32[256,128]{1,0:T(8,128)S(1)} %get-tuple-element.22.hour_rows, bf16[16,256,1024]{2,1,0:T(8,128)(2,1)S(1)} %get-tuple-element.23.ens_buf, ...), custom_call_target="tpu_custom_call" | custom-call | tf_op jit(solution)/shard_map/adjoint/pallas_call | solution.py:408
  41.6 10.9 %all_to_all.42.copies = bf16[16,24,256]{2,1,0:T(8,128)(2,1)S(1)} all-to-all(bf16[16,24,256]{2,1,0:T(8,128)(2,1)S(1)} %adjoint.1), channel_id=1, replica_groups=mesh['cells_0'=4,'cells_1'=4,'cells_2'=2,'rcpt'=4] {'cells_0','cells_1'}, dimensions={0} | all-to-all | bytes 393216 | tf_op jit(solution)/shard_map/all_to_all | solution.py:271
  52.6 11.5 %all_to_all.43.copies = f32[8,24,256]{2,1,0:T(8,128)S(1)} all-to-all(f32[8,24,256]{2,1,0:T(8,128)S(1)} %add_copies.2), channel_id=1, replica_groups=mesh['cells_0'=4,'cells_1'=4,'cells_2'=2,'rcpt'=4] {'cells_2','rcpt'}, dimensions={0} | all-to-all | bytes 393216 | tf_op jit(solution)/shard_map/all_to_all | solution.py:271
  64.1 0.0 copy-done
  64.1 4.8 %next_forward.1 = (bf16[256,128]{1,0:T(8,128)(2,1)S(1)}, f32[24,256]{1,0:T(8,128)S(1)}) custom-call(s32[1,256]{1,0:T(1,128)S(4)} %get-tuple-element.17.block, s32[1,384]{1,0:T(1,128)S(4)} %get-tuple-element.18.place, f32[24,256]{1,0:T(8,128)S(1)} %copy-done, f32[8,24,256]{2,1,0:T(8,128)S(1)} %all_to_all.43.copies, ...), custom_call_target="tpu_custom_call" | custom-call | tf_op jit(solution)/shard_map/next_forward/pallas_call | solution.py:410
  68.9 10.4 %all_to_all.44 = bf16[32,8,128]{2,1,0:T(8,128)(2,1)S(1)} all-to-all(bf16[32,8,128]{2,1,0:T(8,128)(2,1)S(1)} %bitcast.20), channel_id=1, replica_groups=mesh['cells_0'=4,'cells_1'=4,'cells_2'=2,'rcpt'=4] {'cells_0','cells_1',..., dimensions={0} | all-to-all | bytes 131072 | tf_op jit(solution)/shard_map/all_to_all | solution.py:271
  79.3 0.3 next_departure.1
  79.6 10.9 %all_to_all.45 = bf16[32,8,128]{2,1,0:T(8,128)(2,1)S(1)} all-to-all(bf16[32,8,128]{2,1,0:T(8,128)(2,1)S(1)} %bitcast.19), channel_id=1, replica_groups=mesh['cells_0'=4,'cells_1'=4,'cells_2'=2,'rcpt'=4] {'cells_0','cells_1',..., dimensions={0} | all-to-all | bytes 131072 | tf_op jit(solution)/shard_map/all_to_all | solution.py:271
  90.5 4.3 %last_adjoint.1 = (bf16[8,24,256]{2,1,0:T(8,128)(2,1)S(1)}, f32[64,128]{1,0:T(8,128)}) custom-call(s32[1,256]{1,0:T(1,128)S(4)} %get-tuple-element.17.block, s32[1,384]{1,0:T(1,128)S(4)} %get-tuple-element.18.place, bf16[256,128]{1,0:T(8,128)(2,1)S(1)} %bitcast.14, s32[256,128]{1,0:T(8,128)S(1)} %get-tuple-element.22.hour_rows, ...), custom_call_target="tpu_custom_call" | custom-call | tf_op jit(solution)/shard_map/last_adjoint/pallas_call | solution.py:417
  94.8 7.8 %all_to_all.46.copies = bf16[8,24,256]{2,1,0:T(8,128)(2,1)S(1)} all-to-all(bf16[8,24,256]{2,1,0:T(8,128)(2,1)S(1)} %get-tuple-element.30), channel_id=1, replica_groups=mesh['cells_0'=4,'cells_1'=4,'cells_2'=2,'rcpt'=4] {'cells_2','rcpt'}, dimensions={0} | all-to-all | bytes 196608 | tf_op jit(solution)/shard_map/all_to_all | solution.py:271
  102.6 11.1 %all_to_all.47 = bf16[16,24,256]{2,1,0:T(8,128)(2,1)S(1)} all-to-all(bf16[16,24,256]{2,1,0:T(8,128)(2,1)S(1)} %add_copies.3), channel_id=1, replica_groups=mesh['cells_0'=4,'cells_1'=4,'cells_2'=2,'rcpt'=4] {'cells_0','cells_1'}, dimensions={0} | all-to-all | bytes 393216 | tf_op jit(solution)/shard_map/all_to_all | solution.py:271
  113.8 0.6 pad_maximum_fusion
  (4 shorter events, 0.1 us)
Async XLA Ops:
  37.4 26.7 %copy-start = (f32[24,256]{1,0:T(8,128)S(1)}, f32[24,256]{1,0:T(8,128)}, u32[]{:S(2)}) copy-start(f32[24,256]{1,0:T(8,128)} %control.3) | copy-start | bytes 73732
